TPU v7x, 128 devices: a whole 4x4x4 slice. The times are simulated.
128 devices in a mesh: outer: 8 (over x, core), inner: 16 (over z, y).
Axes of the slice: x: 4, y: 4, z: 4, core: 2. Of those that a mesh axis runs over, the one named last changes fastest.
Arguments:
- tokens: bfloat16 [2048, 3584], P(('outer', 'inner')), may hold values from -6 to 6
- experts: int32 [2048, 8], P(('outer', 'inner')), may hold values from 0 to 127, as said below
- gate_score: int32 [2048, 8], P(('outer', 'inner')), may hold values from 1 to 16
- expert_gate: bfloat16 [128, 3584, 1024], P(('outer', 'inner')), may hold values from -0.09375 to 0.09375
- expert_up: bfloat16 [128, 3584, 1024], P(('outer', 'inner')), may hold values from -0.09375 to 0.09375
- expert_down: bfloat16 [128, 1024, 3584], P(('outer', 'inner')), may hold values from -0.1875 to 0.1875
- shared_gate: bfloat16 [3584, 2048], P(None, 'inner'), may hold values from -0.09375 to 0.09375
- shared_up: bfloat16 [3584, 2048], P(None, 'inner'), may hold values from -0.09375 to 0.09375
- shared_down: bfloat16 [2048, 3584], P('inner'), may hold values from -0.125 to 0.125
Outputs:
- moe_out: bfloat16 [2048, 3584], P(('outer', 'inner'))
Inputs may be any that keep to these rules, and one draw needn't show every extreme that they name: Each token names 8 different experts, exactly two in each of 4 different groups, where expert e lies in group e // 16. One group, drawn from the seed, is named by every token. The 16 tokens of one device name one expert at most 2 times, and name each expert of that group exactly 2 times.
All inputs are finite; a program needn't handle non-finite values.
Results may differ from a plain program's by a relative error of at most 0.012.
Values may be sent and summed in bfloat16 or wider, within the bound.
A program may use at most 128 MiB of HBM per device.

v0:
```python
import jax
import jax.numpy as jnp
from jax import lax
from jax.sharding import PartitionSpec as P

TOPK = 8
TOP_GROUPS = 4


def gated_mlp(inputs, gate_matrix, up_matrix, down_matrix):
    gate_part = jnp.dot(inputs, gate_matrix, preferred_element_type=jnp.float32)
    up_part = jnp.dot(inputs, up_matrix, preferred_element_type=jnp.float32)
    hidden = (jax.nn.silu(gate_part) * up_part).astype(jnp.bfloat16)
    return jnp.dot(hidden, down_matrix, preferred_element_type=jnp.float32).astype(jnp.bfloat16)


def gate_weights(gate_score):
    values = gate_score.astype(jnp.float32)
    return 2.5 * values / jnp.sum(values, axis=-1, keepdims=True)


def group_rank(group_ids):
    slot_width = group_ids.shape[-1]
    same_group = group_ids[..., :, None] == group_ids[..., None, :]
    earlier = jnp.arange(slot_width)[None, :] < jnp.arange(slot_width)[:, None]
    return jnp.sum(jnp.logical_and(same_group, earlier), axis=-1)


def combine_pairs(pair_rows, pair_weights):
    values = pair_rows.astype(jnp.float32)
    mixed = (
        pair_weights[..., 0, None] * values[..., 0, :]
        + pair_weights[..., 1, None] * values[..., 1, :]
    )
    return mixed.astype(jnp.bfloat16)


def rank_slots(matches):
    named_mask = jnp.any(matches, axis=-2).astype(jnp.int32)
    earlier = jnp.cumsum(named_mask, axis=-2) - named_mask
    slot_ranks = jnp.sum(jnp.where(matches, earlier[..., None, :], 0), axis=-1)
    return (named_mask, earlier, slot_ranks)


def pair_tables(group_ids, slot_rank, slot_index, weights, group_count):
    wanted = jnp.arange(group_count, dtype=jnp.int32)
    in_group = group_ids[..., None, None, :] == wanted[:, None, None]
    in_place = slot_rank[..., None, None, :] == jnp.arange(2, dtype=jnp.int32)[None, :, None]
    picked = jnp.logical_and(in_group, in_place)
    chosen = jnp.sum(jnp.where(picked, slot_index[..., None, None, :], 0), axis=-1)
    present = jnp.any(picked, axis=-1)
    pair_weights = jnp.sum(jnp.where(picked, weights[..., None, None, :], 0.0), axis=-1)
    return (chosen, present, pair_weights)


def per_device(
    tokens,
    experts,
    gate_score,
    expert_gate,
    expert_up,
    expert_down,
    shared_gate,
    shared_up,
    shared_down,
):
    row_count = tokens.shape[0]
    model_width = tokens.shape[1]
    inner_count = lax.axis_size("inner")
    outer_count = lax.axis_size("outer")
    capacity = TOPK // TOP_GROUPS * row_count // inner_count
    gate_matrix = expert_gate[0]
    up_matrix = expert_up[0]
    down_matrix = expert_down[0]
    segment = lax.all_gather(tokens, "inner", axis=0, tiled=True)
    gate_part = jnp.dot(segment, shared_gate, preferred_element_type=jnp.float32)
    up_part = jnp.dot(segment, shared_up, preferred_element_type=jnp.float32)
    shared_hidden = (jax.nn.silu(gate_part) * up_part).astype(jnp.bfloat16)
    shared = lax.psum_scatter(
        jnp.dot(shared_hidden, shared_down, preferred_element_type=jnp.float32).astype(
            jnp.bfloat16
        ),
        "inner",
        scatter_dimension=0,
        tiled=True,
    ).astype(jnp.float32)
    weights = gate_weights(gate_score)
    group_ids = experts // inner_count
    slot_rank = group_rank(group_ids)
    total_count = inner_count * outer_count
    matches = experts[:, :, None] == jnp.arange(total_count, dtype=jnp.int32)[None, None, :]
    named_mask, earlier, slot_ranks = rank_slots(matches)
    slot_ids = jnp.arange(capacity, dtype=jnp.int32)[None, :, None]
    selector = jnp.logical_and(
        named_mask.T[:, None, :] == 1, earlier.T[:, None, :] == slot_ids
    ).astype(jnp.bfloat16)
    outbound = jnp.einsum(
        "ecr,rd->ecd", selector, tokens, preferred_element_type=jnp.float32
    ).astype(jnp.bfloat16)
    received = lax.all_to_all(outbound, ("outer", "inner"), split_axis=0, concat_axis=0, tiled=True)
    answer = gated_mlp(received.reshape(-1, model_width), gate_matrix, up_matrix, down_matrix)
    returned = lax.all_to_all(
        answer.reshape(received.shape), ("outer", "inner"), split_axis=0, concat_axis=0, tiled=True
    )
    flat_rows = returned.reshape(-1, model_width)
    slot_index = experts * capacity + slot_ranks
    chosen, present, pair_weights = pair_tables(
        group_ids, slot_rank, slot_index, weights, outer_count
    )
    pair_rows = jnp.where(present[..., None], flat_rows[chosen], jnp.zeros((), jnp.bfloat16))
    partial_value = combine_pairs(pair_rows, pair_weights)
    routed = jnp.sum(partial_value.astype(jnp.float32), axis=1)
    return (shared + routed).astype(jnp.bfloat16)


def solution(mesh):
    return jax.shard_map(
        per_device,
        mesh=mesh,
        in_specs=(
            P(("outer", "inner"), None),
            P(("outer", "inner"), None),
            P(("outer", "inner"), None),
            P(("outer", "inner"), None, None),
            P(("outer", "inner"), None, None),
            P(("outer", "inner"), None, None),
            P(None, "inner"),
            P(None, "inner"),
            P("inner", None),
        ),
        out_specs=P(("outer", "inner"), None),
        check_vma=False,
    )
```

profile of v0, /device:TPU:1, one launch (start us, length us, event | category | flops | bytes accessed | tf_op | source)
XLA Modules:
  0.0 171.9 jit_solution(15658388694802100174)
XLA Ops:
  6.5 0.0 copy-start
  6.5 0.8 copy.47
  7.4 0.1 fusion.31
  7.5 1.6 convolution_convert_fusion.1
  9.1 3.1 %copy.48 = bf16[128,2,3584]{2,1,0:T(2,128)(2,1)} copy(bf16[128,2,3584]{2,0,1:T(8,128)(2,1)S(1)} %convolution_convert_fusion.1) | data formatting | bytes 3670016 | tf_op jit(solution)/shard_map/convert_element_type | solution.py:99
  12.2 0.0 copy-start.3
  12.2 11.5 %all-to-all-start = ((bf16[128,2,3584]{2,1,0:T(2,128)(2,1)}), bf16[128,2,3584]{2,1,0:T(2,128)(2,1)S(1)}, u32[]{:S(2)}, u32[]{:S(2)}) async-start(bf16[128,2,3584]{2,1,0:T(2,128)(2,1)} %copy.48), calls=%async_computation.1 | async-start | bytes 3670016 | tf_op jit(solution)/shard_map/all_to_all | solution.py:100
  23.7 0.0 all-gather.2.cloned.1.call-start
  23.8 0.7 all-gather.2.cloned.1.call-update
  24.5 0.4 select_reduce_fusion
  24.9 0.1 copy.49
  25.0 0.0 copy-done.3
  25.0 0.1 convert_reduce_fusion.1
  25.1 25.3 %all-to-all-done = bf16[128,2,3584]{2,1,0:T(2,128)(2,1)S(1)} async-done(((bf16[128,2,3584]{2,1,0:T(2,128)(2,1)}), bf16[128,2,3584]{2,1,0:T(2,128)(2,1)S(1)}, u32[]{:S(2)}, u32[]{:S(2)}) %all-to-all-start) | async-done | bytes 1835040 | tf_op jit(solution)/shard_map/all_to_all | solution.py:100
  50.4 1.6 reshape.66
  52.0 0.0 copy-start.2
  52.0 6.8 %fusion.4 = f32[256,1024]{1,0:T(8,128)} fusion(bf16[256,3584]{1,0:T(8,128)(2,1)} %reshape.66, bf16[1,3584,1024]{2,1,0:T(8,128)(2,1)} %param.12), kind=kOutput, calls=%fused_computation.5 | convolution fusion | flops 1879048192 | bytes 10223616 | tf_op jit(solution)/shard_map/dot_general | solution.py:11
  58.9 0.0 copy-done.2
  58.9 10.9 %fusion.6 = bf16[256,3584]{1,0:T(8,128)(2,1)} fusion(bf16[1,1024,3584]{2,1,0:T(8,128)(2,1)} %param.14, bf16[256,3584]{1,0:T(8,128)(2,1)S(1)} %copy-done.2, bf16[1,3584,1024]{2,1,0:T(8,128)(2,1)} %param.13, f32[256,1024]{1,0:T(8,128)} %fusion.4), kind=kOutput, calls=%fused_computation.7 | convolution fusion | flops 3760586752 | bytes 19398656 | tf_op jit(solution)/shard_map/dot_general | solution.py:14
  69.8 4.7 %reshape.67 = bf16[128,2,3584]{2,1,0:T(2,128)(2,1)} reshape(bf16[256,3584]{1,0:T(8,128)(2,1)} %fusion.6) | data formatting | bytes 3670016 | tf_op jit(solution)/shard_map/reshape | solution.py:103
  74.6 5.9 %all-to-all-start.1 = ((bf16[128,2,3584]{2,1,0:T(2,128)(2,1)}), bf16[128,2,3584]{2,1,0:T(2,128)(2,1)}, u32[]{:S(2)}, u32[]{:S(2)}) async-start(bf16[128,2,3584]{2,1,0:T(2,128)(2,1)} %reshape.67), calls=%async_computation.2 | async-start | bytes 3670016 | tf_op jit(solution)/shard_map/all_to_all | solution.py:102
  80.5 0.2 reduce-scatter.2.cloned.1.call-start
  80.7 0.0 all-gather.2.cloned.1.call-done
  80.8 0.0 copy-start.1
  80.8 2.5 %fusion.43 = f32[256,128]{1,0:T(8,128)S(1)} fusion(bf16[256,3584]{1,0:T(8,128)(2,1)} %all-gather.2.cloned.1.call-done, bf16[3584,128]{1,0:T(8,128)(2,1)} %param.15), kind=kOutput, calls=%fused_computation.65 | convolution fusion | flops 234881024 | bytes 2883584 | tf_op jit(solution)/shard_map/dot_general | solution.py:76
  83.3 0.0 copy-done
  83.3 0.0 copy-done.1
  83.3 3.6 %convolution_convert_fusion = bf16[256,3584]{1,0:T(8,128)(2,1)} fusion(bf16[128,3584]{1,0:T(8,128)(2,1)S(1)} %copy-done, bf16[256,3584]{1,0:T(8,128)(2,1)S(1)} %copy-done.1, bf16[3584,128]{1,0:T(8,128)(2,1)} %param.16, f32[256,128]{1,0:T(8,128)S(1)} %fusion.43), kind=kOutput, calls=%fused_computation.8 | convolution fusion | flops 470876160 | bytes 5636096 | tf_op jit(solution)/shard_map/dot_general | solution.py:80
  86.9 0.0 copy-start.4
  86.9 0.0 reduce-scatter.2.cloned.1.call-update
  87.0 0.1 copy.50
  87.1 0.1 reshape.71
  87.3 0.1 copy.46
  87.5 0.1 copy-done.4
  87.7 0.1 copy.45
  87.8 0.1 copy.52
  87.8 19.2 %all-to-all-done.1 = bf16[128,2,3584]{2,1,0:T(2,128)(2,1)} async-done(((bf16[128,2,3584]{2,1,0:T(2,128)(2,1)}), bf16[128,2,3584]{2,1,0:T(2,128)(2,1)}, u32[]{:S(2)}, u32[]{:S(2)}) %all-to-all-start.1) | async-done | bytes 1835040 | tf_op jit(solution)/shard_map/all_to_all | solution.py:102
  107.0 4.1 %reshape.68 = bf16[256,3584]{1,0:T(8,128)(2,1)S(1)} reshape(bf16[128,2,3584]{2,1,0:T(2,128)(2,1)} %all-to-all-done.1) | data formatting | bytes 3670016 | tf_op jit(solution)/shard_map/reshape | solution.py:105
  111.1 2.9 %gather_fusion = bf16[256,3584]{1,0:T(8,128)(2,1)} fusion(bf16[256,3584]{1,0:T(8,128)(2,1)S(1)} %reshape.68, s32[1024]{0:T(1024)S(1)} %pad_clamp_fusion), kind=kCustom, calls=%fused_computation | custom fusion | bytes 3671040 | tf_op jit(solution)/shard_map/gather | solution.py:110
  114.1 3.9 %reshape.70 = bf16[16,8,2,3584]{3,2,1,0:T(2,128)(2,1)S(1)} reshape(bf16[256,3584]{1,0:T(8,128)(2,1)} %gather_fusion) | data formatting | bytes 3670016 | tf_op jit(solution)/shard_map/gather | solution.py:110
  117.9 1.5 fusion.9
  119.5 3.9 %fusion.41 = (f32[16,8,1,3584]{3,2,1,0:T(1,128)S(1)}, f32[16,8,1,3584]{3,2,1,0:T(1,128)S(1)}) fusion(f32[16,8,2,3584]{3,2,1,0:T(2,128)S(1)} %fusion.9), kind=kLoop, calls=%fused_computation.63 | loop fusion | bytes 7340032 | tf_op jit(solution)/shard_map/slice | solution.py:32
  123.4 0.8 convert_reduce_fusion
  124.2 39.3 %reduce-scatter.2.cloned.1.call-done = bf16[16,3584]{1,0:T(8,128)(2,1)} async-done(((bf16[256,3584]{1,0:T(8,128)(2,1)}), bf16[16,3584]{1,0:T(8,128)(2,1)}) %reduce-scatter.2.cloned.1.call-update) | async-done | bytes 114704 | tf_op jit(solution)/shard_map/reduce_scatter | solution.py:79
  163.5 1.6 add_convert_fusion
  (15 shorter events, 0.2 us)
Async XLA Ops:
  6.5 76.7 %copy-start = (bf16[128,3584]{1,0:T(8,128)(2,1)S(1)}, bf16[128,3584]{1,0:T(8,128)(2,1)}, u32[]{:S(2)}) copy-start(bf16[128,3584]{1,0:T(8,128)(2,1)} %param.17) | copy-start | bytes 2752516
  12.2 12.7 %copy-start.3 = (s32[16,8]{0,1:T(8,128)S(1)}, s32[16,8]{0,1:T(8,128)}, u32[]{:S(2)}) copy-start(s32[16,8]{0,1:T(8,128)} %param.10) | copy-start | bytes 1540
  12.2 38.2 %all-to-all-start = ((bf16[128,2,3584]{2,1,0:T(2,128)(2,1)}), bf16[128,2,3584]{2,1,0:T(2,128)(2,1)S(1)}, u32[]{:S(2)}, u32[]{:S(2)}) async-start(bf16[128,2,3584]{2,1,0:T(2,128)(2,1)} %copy.48), calls=%async_computation.1 | async-start | bytes 3670016 | tf_op jit(solution)/shard_map/all_to_all | solution.py:100
  23.7 57.0 %all-gather.2.cloned.1.call-start = ((), (), s32[]{:S(2)}) async-start(), calls=%async_computation.3 | async-start | bytes 1949696 | tf_op jit(solution)/shard_map/all_gather | solution.py:75
  52.0 6.8 %copy-start.2 = (bf16[256,3584]{1,0:T(8,128)(2,1)S(1)}, bf16[256,3584]{1,0:T(8,128)(2,1)}, u32[]{:S(2)}) copy-start(bf16[256,3584]{1,0:T(8,128)(2,1)} %reshape.66) | copy-start | bytes 5505028
  74.6 32.5 %all-to-all-start.1 = ((bf16[128,2,3584]{2,1,0:T(2,128)(2,1)}), bf16[128,2,3584]{2,1,0:T(2,128)(2,1)}, u32[]{:S(2)}, u32[]{:S(2)}) async-start(bf16[128,2,3584]{2,1,0:T(2,128)(2,1)} %reshape.67), calls=%async_computation.2 | async-start | bytes 3670016 | tf_op jit(solution)/shard_map/all_to_all | solution.py:102
  80.5 83.0 %reduce-scatter.2.cloned.1.call-start = ((), (), s32[]{:S(2)}) async-start(), calls=%async_computation.4 | async-start | bytes 1949696 | tf_op jit(solution)/shard_map/reduce_scatter | solution.py:79
  80.8 2.5 %copy-start.1 = (bf16[256,3584]{1,0:T(8,128)(2,1)S(1)}, bf16[256,3584]{1,0:T(8,128)(2,1)}, u32[]{:S(2)}) copy-start(bf16[256,3584]{1,0:T(8,128)(2,1)} %all-gather.2.cloned.1.call-done) | copy-start | bytes 5505028
  86.9 0.7 copy-start.4
Sparse Core Ops, SparseCore 0:
  26.7 49.5 all-gather.1
  87.1 76.3 reduce-scatter.1
where the time goes:
time: 173 us; the launch traced here: 172 us
  waiting for transfers between devices  84.5 us (49%)
  local copies, waits for them, and re-layouts  25.9 us (15%)
  matrix products  25.4 us (15%)
  starting transfers between devices  17.7 us (10%)
  between operations  13.6 us (8%)
  other arithmetic  4.73 us (3%)
    reduce_scatter x1, waiting for transfers between devices, per_device(): lax.psum_scatter(jnp.dot(shared_hidden, shared_down, preferred_element_ty...  39.3 us
    all_to_all x1, waiting for transfers between devices, per_device(): lax.all_to_all(outbound, ('outer', 'inner'), split_axis=0, concat_axis=0,...  25.3 us
    all_to_all x1, waiting for transfers between devices, per_device(): lax.all_to_all(answer.reshape(received.shape), ('outer', 'inner'), split_...  19.2 us
    all_to_all x1, starting transfers between devices, per_device(): lax.all_to_all(outbound, ('outer', 'inner'), split_axis=0, concat_axis=0,...  11.5 us
    dot_general x1, matrix products, gated_mlp(): jnp.dot(hidden, down_matrix, preferred_element_type=jnp.float32)  10.9 us
    gather x2, local copies, waits for them, and re-layouts, per_device(): flat_rows[chosen]  6.83 us
    dot_general x1, matrix products, gated_mlp(): gate_part = jnp.dot(inputs, gate_matrix, preferred_element_type=jnp.float32)  6.82 us
    all_to_all x1, starting transfers between devices, per_device(): lax.all_to_all(answer.reshape(received.shape), ('outer', 'inner'), split_...  5.94 us
  transfers between devices with their start and end apart: 4, of which 3 were waited for; matrix products, arithmetic and copies ran while one was open for 28% of the time, Pallas kernels for 0%

commit v1 on v0

--- a/solution.py
+++ b/solution.py
@@ -72,18 +72,24 @@
     gate_matrix = expert_gate[0]
     up_matrix = expert_up[0]
     down_matrix = expert_down[0]
-    segment = lax.all_gather(tokens, "inner", axis=0, tiled=True)
+    tiled_tokens = jnp.broadcast_to(tokens[None], (inner_count,) + tokens.shape)
+    segment = lax.all_to_all(
+        tiled_tokens, "inner", split_axis=0, concat_axis=0, tiled=True
+    ).reshape(inner_count * row_count, model_width)
     gate_part = jnp.dot(segment, shared_gate, preferred_element_type=jnp.float32)
     up_part = jnp.dot(segment, shared_up, preferred_element_type=jnp.float32)
     shared_hidden = (jax.nn.silu(gate_part) * up_part).astype(jnp.bfloat16)
-    shared = lax.psum_scatter(
-        jnp.dot(shared_hidden, shared_down, preferred_element_type=jnp.float32).astype(
-            jnp.bfloat16
-        ),
+    shared_partial = jnp.dot(
+        shared_hidden, shared_down, preferred_element_type=jnp.float32
+    ).astype(jnp.bfloat16)
+    shared_parts = lax.all_to_all(
+        shared_partial.reshape(inner_count, row_count, model_width),
         "inner",
-        scatter_dimension=0,
+        split_axis=0,
+        concat_axis=0,
         tiled=True,
-    ).astype(jnp.float32)
+    )
+    shared = jnp.sum(shared_parts.astype(jnp.float32), axis=0)
     weights = gate_weights(gate_score)
     group_ids = experts // inner_count
     slot_rank = group_rank(group_ids)

time: 173 us -> 158 us (0.913)
  waiting for transfers between devices: 84.5 us -> 68.4 us
  between operations: 13.6 us -> 0.2 us
  starting transfers between devices: 17.7 us -> 29.5 us
  local copies, waits for them, and re-layouts: 25.9 us -> 30.8 us
    reduce_scatter x1 -> x0, waiting for transfers between devices: 39.3 us -> none  [per_device(): lax.psum_scatter(jnp.dot(shared_hidden, shared_down, preferred_element_ty...]
    all_to_all x0 -> x2, waiting for transfers between devices: none -> 22.7 us  [the longest x1 22.7 us: per_device(): lax.all_to_all(tiled_tokens, 'inner', split_axis=0, concat_axis=0, tiled=...]
    all_to_all x0 -> x2, starting transfers between devices: none -> 12.6 us  [the longest x1 8.73 us: per_device(): lax.all_to_all(tiled_tokens, 'inner', split_axis=0, concat_axis=0, tiled=...]
    all_to_all x1, waiting for transfers between devices: 19.2 us -> 25.3 us  [per_device(): lax.all_to_all(answer.reshape(received.shape), ('outer', 'inner'), split_...]
    all_to_all x1, waiting for transfers between devices: 25.3 us -> 20.3 us  [per_device(): lax.all_to_all(outbound, ('outer', 'inner'), split_axis=0, concat_axis=0,...]
    all_to_all x1, starting transfers between devices: 11.5 us -> 7.56 us  [per_device(): lax.all_to_all(outbound, ('outer', 'inner'), split_axis=0, concat_axis=0,...]
    all_to_all x1, starting transfers between devices: 5.94 us -> 9.35 us  [per_device(): lax.all_to_all(answer.reshape(received.shape), ('outer', 'inner'), split_...]
    reshape x1, local copies, waits for them, and re-layouts: 1.62 us -> 4.93 us  [per_device(): received.reshape(-1, model_width)]
  transfers between devices with their start and end apart: 4 -> 4, of which waited for: 3 -> 3; matrix products, arithmetic and copies ran while one was open for 28% -> 25% of each run, Pallas kernels for 0% -> 0%
where the time goes in v1:
time: 158 us; the launch traced here: 157 us
  waiting for transfers between devices  68.4 us (43%)
  local copies, waits for them, and re-layouts  30.8 us (19%)
  starting transfers between devices  29.5 us (19%)
  matrix products  24.1 us (15%)
  other arithmetic  4.14 us (3%)
    all_to_all x1, waiting for transfers between devices, per_device(): lax.all_to_all(answer.reshape(received.shape), ('outer', 'inner'), split_...  25.3 us
    all_to_all x1, waiting for transfers between devices, per_device(): lax.all_to_all(tiled_tokens, 'inner', split_axis=0, concat_axis=0, tiled=...  22.7 us
    all_to_all x1, waiting for transfers between devices, per_device(): lax.all_to_all(outbound, ('outer', 'inner'), split_axis=0, concat_axis=0,...  20.3 us
    dot_general x1, matrix products, gated_mlp(): jnp.dot(hidden, down_matrix, preferred_element_type=jnp.float32)  11.2 us
    all_to_all x1, starting transfers between devices, per_device(): lax.all_to_all(answer.reshape(received.shape), ('outer', 'inner'), split_...  9.35 us
    all_to_all x1, starting transfers between devices, per_device(): lax.all_to_all(tiled_tokens, 'inner', split_axis=0, concat_axis=0, tiled=...  8.73 us
    all_to_all x1, starting transfers between devices, per_device(): lax.all_to_all(outbound, ('outer', 'inner'), split_axis=0, concat_axis=0,...  7.56 us
    gather x2, local copies, waits for them, and re-layouts, per_device(): flat_rows[chosen]  6.85 us
  transfers between devices with their start and end apart: 4, of which 3 were waited for; matrix products, arithmetic and copies ran while one was open for 25% of the time, Pallas kernels for 0%

profile of v1, /device:TPU:1, one launch (start us, length us, event | category | flops | bytes accessed | tf_op | source)
XLA Modules:
  0.0 157.0 jit_solution(17153737181531135530)
XLA Ops:
  0.0 0.0 copy-start
  0.0 2.4 %broadcast_in_dim.46 = bf16[16,16,3584]{2,1,0:T(8,128)(2,1)} broadcast(bf16[16,3584]{1,0:T(8,128)(2,1)} %param.9), dimensions={1,2} | broadcast | bytes 1949696 | tf_op jit(solution)/shard_map/broadcast_in_dim | solution.py:75
  2.4 0.0 copy-start.2
  2.4 0.0 copy-start.1
  2.4 8.7 %all-to-all-start = ((bf16[16,16,3584]{2,1,0:T(8,128)(2,1)}), bf16[16,16,3584]{2,1,0:T(8,128)(2,1)S(1)}, u32[]{:S(2)}, u32[]{:S(2)}) async-start(bf16[16,16,3584]{2,1,0:T(8,128)(2,1)} %broadcast_in_dim.46), calls=%async_computation | async-start | bytes 3670016 | tf_op jit(solution)/shard_map/all_to_all | solution.py:76
  11.2 0.0 copy-done.2
  11.2 0.1 copy.47
  11.2 0.1 fusion.31
  11.4 0.0 copy-done.1
  11.4 0.7 convolution_convert_fusion.1
  12.1 3.1 %copy.48 = bf16[128,2,3584]{2,1,0:T(2,128)(2,1)} copy(bf16[128,2,3584]{2,0,1:T(8,128)(2,1)S(1)} %convolution_convert_fusion.1) | data formatting | bytes 3670016 | tf_op jit(solution)/shard_map/convert_element_type | solution.py:105
  15.2 22.7 %all-to-all-done = bf16[16,16,3584]{2,1,0:T(8,128)(2,1)S(1)} async-done(((bf16[16,16,3584]{2,1,0:T(8,128)(2,1)}), bf16[16,16,3584]{2,1,0:T(8,128)(2,1)S(1)}, u32[]{:S(2)}, u32[]{:S(2)}) %all-to-all-start) | async-done | bytes 1835040 | tf_op jit(solution)/shard_map/all_to_all | solution.py:76
  37.9 7.6 %all-to-all-start.2 = ((bf16[128,2,3584]{2,1,0:T(2,128)(2,1)}), bf16[128,2,3584]{2,1,0:T(2,128)(2,1)}, u32[]{:S(2)}, u32[]{:S(2)}) async-start(bf16[128,2,3584]{2,1,0:T(2,128)(2,1)} %copy.48), calls=%async_computation.2 | async-start | bytes 3670016 | tf_op jit(solution)/shard_map/all_to_all | solution.py:106
  45.5 0.4 select_reduce_fusion
  45.9 0.1 copy.49
  46.0 0.1 convert_reduce_fusion.2
  46.1 1.8 %fusion.43 = f32[256,128]{1,0:T(8,128)S(1)} fusion(bf16[256,3584]{1,0:T(8,128)(2,1)S(1)} %bitcast.56, bf16[3584,128]{1,0:T(8,128)(2,1)} %param.15), kind=kOutput, calls=%fused_computation.66 | convolution fusion | flops 234881024 | bytes 2883584 | tf_op jit(solution)/shard_map/dot_general | solution.py:79
  47.9 0.0 copy-done
  47.9 3.6 %convolution_convert_fusion = bf16[256,3584]{1,0:T(8,128)(2,1)} fusion(bf16[128,3584]{1,0:T(8,128)(2,1)S(1)} %copy-done, bf16[256,3584]{1,0:T(8,128)(2,1)S(1)} %bitcast.57, bf16[3584,128]{1,0:T(8,128)(2,1)} %param.16, f32[256,128]{1,0:T(8,128)S(1)} %fusion.43), kind=kOutput, calls=%fused_computation.8 | convolution fusion | flops 470876160 | bytes 5636096 | tf_op jit(solution)/shard_map/dot_general | solution.py:82
  51.5 20.3 %all-to-all-done.2 = bf16[128,2,3584]{2,1,0:T(2,128)(2,1)} async-done(((bf16[128,2,3584]{2,1,0:T(2,128)(2,1)}), bf16[128,2,3584]{2,1,0:T(2,128)(2,1)}, u32[]{:S(2)}, u32[]{:S(2)}) %all-to-all-start.2) | async-done | bytes 1835040 | tf_op jit(solution)/shard_map/all_to_all | solution.py:106
  71.8 3.9 %all-to-all-start.1 = ((bf16[16,16,3584]{2,1,0:T(8,128)(2,1)}), bf16[16,16,3584]{2,1,0:T(8,128)(2,1)S(1)}, u32[]{:S(2)}, u32[]{:S(2)}) async-start(bf16[16,16,3584]{2,1,0:T(8,128)(2,1)} %bitcast.58), calls=%async_computation.1 | async-start | bytes 3670016 | tf_op jit(solution)/shard_map/all_to_all | solution.py:85
  75.8 4.9 %reshape.75 = bf16[256,3584]{1,0:T(8,128)(2,1)} reshape(bf16[128,2,3584]{2,1,0:T(2,128)(2,1)} %all-to-all-done.2) | data formatting | bytes 3670016 | tf_op jit(solution)/shard_map/reshape | solution.py:107
  80.7 6.7 %fusion.4 = f32[256,1024]{1,0:T(8,128)} fusion(bf16[256,3584]{1,0:T(8,128)(2,1)} %reshape.75, bf16[1,3584,1024]{2,1,0:T(8,128)(2,1)} %param.12), kind=kOutput, calls=%fused_computation.5 | convolution fusion | flops 1879048192 | bytes 10223616 | tf_op jit(solution)/shard_map/dot_general | solution.py:11
  87.4 11.2 %fusion.6 = bf16[256,3584]{1,0:T(8,128)(2,1)} fusion(bf16[1,1024,3584]{2,1,0:T(8,128)(2,1)} %param.14, bf16[256,3584]{1,0:T(8,128)(2,1)} %reshape.75, bf16[1,3584,1024]{2,1,0:T(8,128)(2,1)} %param.13, f32[256,1024]{1,0:T(8,128)} %fusion.4), kind=kOutput, calls=%fused_computation.7 | convolution fusion | flops 3760586752 | bytes 19398656 | tf_op jit(solution)/shard_map/dot_general | solution.py:14
  98.6 4.8 %reshape.76 = bf16[128,2,3584]{2,1,0:T(2,128)(2,1)} reshape(bf16[256,3584]{1,0:T(8,128)(2,1)} %fusion.6) | data formatting | bytes 3670016 | tf_op jit(solution)/shard_map/reshape | solution.py:109
  103.4 0.0 copy-start.3
  103.4 0.0 all-to-all-done.1
  103.4 9.4 %all-to-all-start.3 = ((bf16[128,2,3584]{2,1,0:T(2,128)(2,1)}), bf16[128,2,3584]{2,1,0:T(2,128)(2,1)}, u32[]{:S(2)}, u32[]{:S(2)}) async-start(bf16[128,2,3584]{2,1,0:T(2,128)(2,1)} %reshape.76), calls=%async_computation.3 | async-start | bytes 3670016 | tf_op jit(solution)/shard_map/all_to_all | solution.py:108
  112.8 0.1 copy.50
  113.0 0.1 reshape.80
  113.2 0.1 copy.46
  113.3 0.0 copy-done.3
  113.4 0.1 copy.45
  113.5 0.1 copy.52
  113.6 0.2 convert_reduce_fusion
  113.8 25.3 %all-to-all-done.3 = bf16[128,2,3584]{2,1,0:T(2,128)(2,1)} async-done(((bf16[128,2,3584]{2,1,0:T(2,128)(2,1)}), bf16[128,2,3584]{2,1,0:T(2,128)(2,1)}, u32[]{:S(2)}, u32[]{:S(2)}) %all-to-all-start.3) | async-done | bytes 1835040 | tf_op jit(solution)/shard_map/all_to_all | solution.py:108
  139.1 4.1 %reshape.77 = bf16[256,3584]{1,0:T(8,128)(2,1)S(1)} reshape(bf16[128,2,3584]{2,1,0:T(2,128)(2,1)} %all-to-all-done.3) | data formatting | bytes 3670016 | tf_op jit(solution)/shard_map/reshape | solution.py:111
  143.2 3.0 %gather_fusion = bf16[256,3584]{1,0:T(8,128)(2,1)} fusion(bf16[256,3584]{1,0:T(8,128)(2,1)S(1)} %reshape.77, s32[1024]{0:T(1024)S(1)} %pad_clamp_fusion), kind=kCustom, calls=%fused_computation | custom fusion | bytes 3671040 | tf_op jit(solution)/shard_map/gather | solution.py:116
  146.2 3.9 %reshape.79 = bf16[16,8,2,3584]{3,2,1,0:T(2,128)(2,1)S(1)} reshape(bf16[256,3584]{1,0:T(8,128)(2,1)} %gather_fusion) | data formatting | bytes 3670016 | tf_op jit(solution)/shard_map/gather | solution.py:116
  150.1 1.5 fusion.9
  151.6 3.9 %fusion.41 = (f32[16,8,1,3584]{3,2,1,0:T(1,128)S(1)}, f32[16,8,1,3584]{3,2,1,0:T(1,128)S(1)}) fusion(f32[16,8,2,3584]{3,2,1,0:T(2,128)S(1)} %fusion.9), kind=kLoop, calls=%fused_computation.64 | loop fusion | bytes 7340032 | tf_op jit(solution)/shard_map/slice | solution.py:32
  155.5 0.8 convert_reduce_fusion.1
  156.4 0.7 add_convert_fusion
  (15 shorter events, 0.2 us)
Async XLA Ops:
  0.0 47.9 %copy-start = (bf16[128,3584]{1,0:T(8,128)(2,1)S(1)}, bf16[128,3584]{1,0:T(8,128)(2,1)}, u32[]{:S(2)}) copy-start(bf16[128,3584]{1,0:T(8,128)(2,1)} %param.17) | copy-start | bytes 2752516
  2.4 8.7 %copy-start.2 = (s32[16,8]{0,1:T(8,128)S(1)}, s32[16,8]{0,1:T(8,128)}, u32[]{:S(2)}) copy-start(s32[16,8]{0,1:T(8,128)} %param.10) | copy-start | bytes 1540
  2.4 9.0 %copy-start.1 = (bf16[16,3584]{1,0:T(8,128)(2,1)S(1)}, bf16[16,3584]{1,0:T(8,128)(2,1)}, u32[]{:S(2)}) copy-start(bf16[16,3584]{1,0:T(8,128)(2,1)} %param.9) | copy-start | bytes 344068
  2.4 35.5 %all-to-all-start = ((bf16[16,16,3584]{2,1,0:T(8,128)(2,1)}), bf16[16,16,3584]{2,1,0:T(8,128)(2,1)S(1)}, u32[]{:S(2)}, u32[]{:S(2)}) async-start(bf16[16,16,3584]{2,1,0:T(8,128)(2,1)} %broadcast_in_dim.46), calls=%async_computation | async-start | bytes 3670016 | tf_op jit(solution)/shard_map/all_to_all | solution.py:76
  37.9 34.0 %all-to-all-start.2 = ((bf16[128,2,3584]{2,1,0:T(2,128)(2,1)}), bf16[128,2,3584]{2,1,0:T(2,128)(2,1)}, u32[]{:S(2)}, u32[]{:S(2)}) async-start(bf16[128,2,3584]{2,1,0:T(2,128)(2,1)} %copy.48), calls=%async_computation.2 | async-start | bytes 3670016 | tf_op jit(solution)/shard_map/all_to_all | solution.py:106
  71.8 31.6 %all-to-all-start.1 = ((bf16[16,16,3584]{2,1,0:T(8,128)(2,1)}), bf16[16,16,3584]{2,1,0:T(8,128)(2,1)S(1)}, u32[]{:S(2)}, u32[]{:S(2)}) async-start(bf16[16,16,3584]{2,1,0:T(8,128)(2,1)} %bitcast.58), calls=%async_computation.1 | async-start | bytes 3670016 | tf_op jit(solution)/shard_map/all_to_all | solution.py:85
  103.4 9.9 %copy-start.3 = (s32[16,8]{0,1:T(8,128)S(1)}, s32[16,8]{0,1:T(8,128)}, u32[]{:S(2)}) copy-start(s32[16,8]{0,1:T(8,128)} %param.11) | copy-start | bytes 1540
  103.4 35.7 %all-to-all-start.3 = ((bf16[128,2,3584]{2,1,0:T(2,128)(2,1)}), bf16[128,2,3584]{2,1,0:T(2,128)(2,1)}, u32[]{:S(2)}, u32[]{:S(2)}) async-start(bf16[128,2,3584]{2,1,0:T(2,128)(2,1)} %reshape.76), calls=%async_computation.3 | async-start | bytes 3670016 | tf_op jit(solution)/shard_map/all_to_all | solution.py:108

commit v2 on v0

--- a/solution.py
+++ b/solution.py
@@ -1,10 +1,137 @@
+import functools
+
 import jax
 import jax.numpy as jnp
 from jax import lax
+from jax.experimental import pallas as pl
+from jax.experimental.pallas import tpu as pltpu
 from jax.sharding import PartitionSpec as P
 
 TOPK = 8
 TOP_GROUPS = 4
+MESH_ID = pl.DeviceIdType.MESH
+ALL_AXES = ("outer", "inner")
+
+
+def flat_index(axes, sizes):
+    index = 0
+    for axis, size in zip(axes, sizes):
+        index = index * size + lax.axis_index(axis)
+    return index
+
+
+def mesh_coords(flat, axes, sizes):
+    coords = []
+    for size in reversed(sizes):
+        coords.append(flat % size)
+        flat = flat // size
+    return dict(zip(axes, reversed(coords)))
+
+
+def exchange_kernel(plans, sizes, *refs):
+    count = len(plans)
+    sends = refs[:count]
+    recvs = refs[count:2 * count]
+    send_sems = refs[2 * count:3 * count]
+    recv_sems = refs[3 * count:4 * count]
+    local_sems = refs[4 * count]
+    axis_size = dict(zip(ALL_AXES, sizes))
+    world = sizes[0] * sizes[1]
+    world_me = flat_index(ALL_AXES, sizes)
+
+    barrier = pltpu.get_barrier_semaphore()
+
+    @pl.loop(1, world)
+    def _(step):
+        peer = lax.rem(world_me + step, world)
+        pl.semaphore_signal(
+            barrier, inc=1, device_id=mesh_coords(peer, ALL_AXES, sizes),
+            device_id_type=MESH_ID,
+        )
+
+    pl.semaphore_wait(barrier, world - 1)
+
+    def block(ref, index, rows, same):
+        if same:
+            return ref
+        return ref.at[pl.ds(index * rows, rows)]
+
+    locals_ = []
+    for k, (axes, rows, same) in enumerate(plans):
+        axis_sizes = tuple(axis_size[a] for a in axes)
+        me = flat_index(axes, axis_sizes)
+        local = pltpu.make_async_copy(
+            block(sends[k], me, rows, same), recvs[k].at[pl.ds(me * rows, rows)],
+            local_sems.at[k],
+        )
+        local.start()
+        locals_.append(local)
+
+    for k, (axes, rows, same) in enumerate(plans):
+        axis_sizes = tuple(axis_size[a] for a in axes)
+        n = 1
+        for size in axis_sizes:
+            n *= size
+        me = flat_index(axes, axis_sizes)
+
+        @pl.loop(1, n)
+        def _(step):
+            peer = lax.rem(me + step, n)
+            pltpu.make_async_remote_copy(
+                src_ref=block(sends[k], peer, rows, same),
+                dst_ref=recvs[k].at[pl.ds(me * rows, rows)],
+                send_sem=send_sems[k].at[peer],
+                recv_sem=recv_sems[k].at[me],
+                device_id=mesh_coords(peer, axes, axis_sizes),
+                device_id_type=MESH_ID,
+            ).start()
+
+    for k, (axes, rows, same) in enumerate(plans):
+        axis_sizes = tuple(axis_size[a] for a in axes)
+        n = 1
+        for size in axis_sizes:
+            n *= size
+        me = flat_index(axes, axis_sizes)
+
+        @pl.loop(1, n)
+        def _(step):
+            peer = lax.rem(me + step, n)
+            pltpu.make_async_remote_copy(
+                src_ref=block(sends[k], peer, rows, same),
+                dst_ref=recvs[k].at[pl.ds(peer * rows, rows)],
+                send_sem=send_sems[k].at[peer],
+                recv_sem=recv_sems[k].at[peer],
+                device_id=mesh_coords(peer, axes, axis_sizes),
+                device_id_type=MESH_ID,
+            ).wait()
+
+    for local in locals_:
+        local.wait()
+
+
+def exchange(sends, plans, collective_id):
+    sizes = (lax.axis_size("outer"), lax.axis_size("inner"))
+    axis_size = dict(zip(ALL_AXES, sizes))
+    out_shapes = []
+    sem_shapes = []
+    for send, (axes, rows, same) in zip(sends, plans):
+        n = 1
+        for a in axes:
+            n *= axis_size[a]
+        out_shapes.append(jax.ShapeDtypeStruct((n * rows,) + send.shape[1:], send.dtype))
+        sem_shapes.append(n)
+    return pl.pallas_call(
+        functools.partial(exchange_kernel, plans, sizes),
+        out_shape=tuple(out_shapes),
+        in_specs=[pl.BlockSpec(memory_space=pl.ANY)] * len(sends),
+        out_specs=tuple(pl.BlockSpec(memory_space=pl.ANY) for _ in sends),
+        scratch_shapes=[pltpu.SemaphoreType.DMA((n,)) for n in sem_shapes]
+        + [pltpu.SemaphoreType.DMA((n,)) for n in sem_shapes]
+        + [pltpu.SemaphoreType.DMA((len(sends),))],
+        compiler_params=pltpu.CompilerParams(
+            collective_id=collective_id, has_side_effects=True
+        ),
+    )(*sends)
 
 
 def gated_mlp(inputs, gate_matrix, up_matrix, down_matrix):
@@ -69,40 +196,40 @@
     inner_count = lax.axis_size("inner")
     outer_count = lax.axis_size("outer")
     capacity = TOPK // TOP_GROUPS * row_count // inner_count
-    gate_matrix = expert_gate[0]
-    up_matrix = expert_up[0]
-    down_matrix = expert_down[0]
-    segment = lax.all_gather(tokens, "inner", axis=0, tiled=True)
-    gate_part = jnp.dot(segment, shared_gate, preferred_element_type=jnp.float32)
-    up_part = jnp.dot(segment, shared_up, preferred_element_type=jnp.float32)
-    shared_hidden = (jax.nn.silu(gate_part) * up_part).astype(jnp.bfloat16)
-    shared = lax.psum_scatter(
-        jnp.dot(shared_hidden, shared_down, preferred_element_type=jnp.float32).astype(
-            jnp.bfloat16
-        ),
-        "inner",
-        scatter_dimension=0,
-        tiled=True,
-    ).astype(jnp.float32)
+    total_count = inner_count * outer_count
     weights = gate_weights(gate_score)
     group_ids = experts // inner_count
     slot_rank = group_rank(group_ids)
-    total_count = inner_count * outer_count
     matches = experts[:, :, None] == jnp.arange(total_count, dtype=jnp.int32)[None, None, :]
     named_mask, earlier, slot_ranks = rank_slots(matches)
     slot_ids = jnp.arange(capacity, dtype=jnp.int32)[None, :, None]
     selector = jnp.logical_and(
         named_mask.T[:, None, :] == 1, earlier.T[:, None, :] == slot_ids
+    ).astype(jnp.bfloat16).reshape(total_count * capacity, row_count)
+    outbound = jnp.dot(selector, tokens, preferred_element_type=jnp.float32).astype(
+        jnp.bfloat16
+    )
+    segment, received = exchange(
+        [tokens, outbound],
+        [(("inner",), row_count, True), (ALL_AXES, capacity, False)],
+        0,
+    )
+    gate_part = jnp.dot(segment, shared_gate, preferred_element_type=jnp.float32)
+    up_part = jnp.dot(segment, shared_up, preferred_element_type=jnp.float32)
+    shared_hidden = (jax.nn.silu(gate_part) * up_part).astype(jnp.bfloat16)
+    shared_partial = jnp.dot(
+        shared_hidden, shared_down, preferred_element_type=jnp.float32
     ).astype(jnp.bfloat16)
-    outbound = jnp.einsum(
-        "ecr,rd->ecd", selector, tokens, preferred_element_type=jnp.float32
-    ).astype(jnp.bfloat16)
-    received = lax.all_to_all(outbound, ("outer", "inner"), split_axis=0, concat_axis=0, tiled=True)
-    answer = gated_mlp(received.reshape(-1, model_width), gate_matrix, up_matrix, down_matrix)
-    returned = lax.all_to_all(
-        answer.reshape(received.shape), ("outer", "inner"), split_axis=0, concat_axis=0, tiled=True
-    )
-    flat_rows = returned.reshape(-1, model_width)
+    answer = gated_mlp(received, expert_gate[0], expert_up[0], expert_down[0])
+    shared_parts, flat_rows = exchange(
+        [shared_partial, answer],
+        [(("inner",), row_count, False), (ALL_AXES, capacity, False)],
+        1,
+    )
+    shared = jnp.sum(
+        shared_parts.reshape(inner_count, row_count, model_width).astype(jnp.float32),
+        axis=0,
+    )
     slot_index = experts * capacity + slot_ranks
     chosen, present, pair_weights = pair_tables(
         group_ids, slot_rank, slot_index, weights, outer_count

time: 173 us -> 174 us (level)
  Pallas kernels: 0 us -> 126 us
  waiting for transfers between devices: 84.5 us -> 0 us
  starting transfers between devices: 17.7 us -> 0 us
  between operations: 13.6 us -> 0.22 us
  local copies, waits for them, and re-layouts: 25.9 us -> 14.3 us
  other arithmetic: 4.73 us -> 7.3 us
    pallas_call x0 -> x2, Pallas kernels: none -> 126 us  [exchange(): pl.pallas_call(functools.partial(exchange_kernel, plans, sizes), out_shap...]
    all_to_all x2 -> x0, waiting for transfers between devices: 44.5 us -> none  [the longest x1 25.3 us: per_device(): lax.all_to_all(outbound, ('outer', 'inner'), split_axis=0, concat_axis=0,...]
    reduce_scatter x1 -> x0, waiting for transfers between devices: 39.3 us -> none  [per_device(): lax.psum_scatter(jnp.dot(shared_hidden, shared_down, preferred_element_ty...]
    all_to_all x2 -> x0, starting transfers between devices: 17.4 us -> none  [the longest x1 11.5 us: per_device(): lax.all_to_all(outbound, ('outer', 'inner'), split_axis=0, concat_axis=0,...]
    reshape x3 -> x0, local copies, waits for them, and re-layouts: 10.4 us -> none  [the longest x1 4.75 us: per_device(): answer.reshape(received.shape)]
    convert_element_type x1 -> x0, local copies, waits for them, and re-layouts: 3.12 us -> none  [per_device(): outbound = jnp.einsum('ecr,rd->ecd', selector, tokens, preferred_element_...]
    reduce_sum x0 -> x1, other arithmetic: none -> 1.9 us  [per_device(): jnp.sum(shared_parts.reshape(inner_count, row_count, model_width).astype(...]
  transfers between devices with their start and end apart: 4 -> 0, of which waited for: 3 -> 0; matrix products, arithmetic and copies ran while one was open for 28% -> 0% of each run, Pallas kernels for 0% -> 0%
where the time goes in v2:
time: 174 us
  Pallas kernels  126 us (72%)
  matrix products  26.5 us (15%)
  local copies, waits for them, and re-layouts  14.3 us (8%)
  other arithmetic  7.3 us (4%)
    pallas_call x2, Pallas kernels, exchange(): pl.pallas_call(functools.partial(exchange_kernel, plans, sizes), out_shap...  126 us
    dot_general x1, matrix products, gated_mlp(): jnp.dot(hidden, down_matrix, preferred_element_type=jnp.float32)  10.8 us
    gather x2, local copies, waits for them, and re-layouts, per_device(): flat_rows[chosen]  7.03 us
    dot_general x1, matrix products, gated_mlp(): gate_part = jnp.dot(inputs, gate_matrix, preferred_element_type=jnp.float32)  6.79 us
    slice x1, local copies, waits for them, and re-layouts, combine_pairs(): values[..., 0, :]  5.16 us
    dot_general x1, matrix products, per_device(): jnp.dot(shared_hidden, shared_down, preferred_element_type=jnp.float32)  3.62 us

profile of v2, /device:TPU:1, one launch (start us, length us, event | category | flops | bytes accessed | tf_op | source)
XLA Modules:
  0.0 174.2 jit_solution(17776436316855060611)
XLA Ops:
  0.0 0.0 copy-start
  0.0 0.8 copy.40
  0.8 0.1 fusion.34
  1.0 0.1 copy.41
  1.1 0.1 and.37
  1.2 0.1 and.38
  1.3 0.1 copy.42
  1.5 0.1 eq.99
  1.6 2.8 %convolution_convert_fusion.1.refs_1_ = bf16[256,3584]{1,0:T(8,128)(2,1)} fusion(bf16[16,3584]{1,0:T(8,128)(2,1)} %refs_0_.1, pred[256,16]{1,0:T(32,128)(4,1)S(1)} %and.38, s32[256,16]{1,0:T(8,128)S(1)} %bitcast.56, s32[256]{0:T(256)S(1)} %eq.99), kind=kOutput, calls=%fused_computation.9 | convolution fusion | flops 30285824 | bytes 1971200 | tf_op jit(solution)/shard_map/dot_general | solution.py:209
  4.4 65.0 %shard_map.91 = (bf16[256,3584]{1,0:T(8,128)(2,1)}, bf16[256,3584]{1,0:T(8,128)(2,1)}) custom-call(bf16[16,3584]{1,0:T(8,128)(2,1)} %refs_0_.1, bf16[256,3584]{1,0:T(8,128)(2,1)} %convolution_convert_fusion.1.refs_1_), custom_call_target="tpu_custom_call" | custom-call | tf_op jit(solution)/shard_map/pallas_call | solution.py:123
  69.5 0.0 copy-start.2
  69.5 2.5 %fusion.42 = f32[256,128]{1,0:T(8,128)S(1)} fusion(bf16[256,3584]{1,0:T(8,128)(2,1)} %get-tuple-element.9, bf16[3584,128]{1,0:T(8,128)(2,1)} %param.15), kind=kOutput, calls=%fused_computation.65 | convolution fusion | flops 234881024 | bytes 2883584 | tf_op jit(solution)/shard_map/dot_general | solution.py:217
  72.0 0.0 copy-done
  72.0 0.0 copy-done.2
  72.0 3.6 %convolution_convert_fusion.refs_0_ = bf16[256,3584]{1,0:T(8,128)(2,1)} fusion(bf16[128,3584]{1,0:T(8,128)(2,1)S(1)} %copy-done, bf16[256,3584]{1,0:T(8,128)(2,1)S(1)} %copy-done.2, bf16[3584,128]{1,0:T(8,128)(2,1)} %param.16, f32[256,128]{1,0:T(8,128)S(1)} %fusion.42), kind=kOutput, calls=%fused_computation.8 | convolution fusion | flops 470876160 | bytes 5636096 | tf_op jit(solution)/shard_map/dot_general | solution.py:220
  75.6 0.0 copy-start.5
  75.6 6.8 %fusion.4 = f32[256,1024]{1,0:T(8,128)} fusion(bf16[256,3584]{1,0:T(8,128)(2,1)} %get-tuple-element.10, bf16[1,3584,1024]{2,1,0:T(8,128)(2,1)} %param.12), kind=kOutput, calls=%fused_computation.5 | convolution fusion | flops 1879048192 | bytes 10223616 | tf_op jit(solution)/shard_map/dot_general | solution.py:138
  82.4 0.0 copy-done.5
  82.4 10.8 %fusion.6.refs_1_ = bf16[256,3584]{1,0:T(8,128)(2,1)} fusion(bf16[1,1024,3584]{2,1,0:T(8,128)(2,1)} %param.14, bf16[256,3584]{1,0:T(8,128)(2,1)S(1)} %copy-done.5, bf16[1,3584,1024]{2,1,0:T(8,128)(2,1)} %param.13, f32[256,1024]{1,0:T(8,128)} %fusion.4), kind=kOutput, calls=%fused_computation.7 | convolution fusion | flops 3760586752 | bytes 19398656 | tf_op jit(solution)/shard_map/dot_general | solution.py:141
  93.2 60.9 %shard_map.92 = (bf16[256,3584]{1,0:T(8,128)(2,1)}, bf16[256,3584]{1,0:T(8,128)(2,1)}) custom-call(bf16[256,3584]{1,0:T(8,128)(2,1)} %convolution_convert_fusion.refs_0_, bf16[256,3584]{1,0:T(8,128)(2,1)} %fusion.6.refs_1_), custom_call_target="tpu_custom_call" | custom-call | tf_op jit(solution)/shard_map/pallas_call | solution.py:123
  154.1 0.0 copy-start.3
  154.1 0.0 copy-start.1
  154.1 1.9 %convert_reduce_fusion = f32[16,3584]{1,0:T(8,128)S(1)} fusion(bf16[16,16,3584]{2,1,0:T(8,128)(2,1)} %bitcast.55), kind=kLoop, calls=%fused_computation.10 | loop fusion | flops 1777664 | bytes 2064384 | tf_op jit(solution)/shard_map/reduce_sum | solution.py:229
  156.0 0.4 select_reduce_fusion
  156.4 0.1 copy.45
  156.5 0.0 copy-done.3
  156.5 0.1 convert_reduce_fusion.2
  156.7 0.1 copy.46
  156.8 0.1 reshape.67
  157.0 0.0 copy-done.1
  157.0 3.0 %gather_fusion = bf16[256,3584]{1,0:T(8,128)(2,1)} fusion(bf16[256,3584]{1,0:T(8,128)(2,1)S(1)} %copy-done.1, s32[1024]{0:T(1024)S(1)} %pad_clamp_fusion), kind=kCustom, calls=%fused_computation | custom fusion | bytes 3671040 | tf_op jit(solution)/shard_map/gather | solution.py:237
  160.0 4.1 %reshape.66 = bf16[16,8,2,3584]{3,2,1,0:T(2,128)(2,1)S(1)} reshape(bf16[256,3584]{1,0:T(8,128)(2,1)} %gather_fusion) | data formatting | bytes 3670016 | tf_op jit(solution)/shard_map/gather | solution.py:237
  164.1 0.1 copy.44
  164.2 1.5 fusion.9
  165.8 0.0 copy-start.4
  165.8 5.2 %fusion.39 = (f32[16,8,1,3584]{3,2,1,0:T(1,128)S(1)}, f32[16,8,1,3584]{3,2,1,0:T(1,128)}) fusion(f32[16,8,2,3584]{3,2,1,0:T(2,128)S(1)} %fusion.9), kind=kLoop, calls=%fused_computation.62 | loop fusion | bytes 7340032 | tf_op jit(solution)/shard_map/slice | solution.py:159
  171.0 0.0 copy-done.4
  171.1 0.1 copy.48
  171.1 0.1 copy.43
  171.2 2.3 %convert_reduce_fusion.1 = f32[16,3584]{1,0:T(8,128)S(1)} fusion(f32[16,8,1,3584]{3,2,1,0:T(1,128)} %get-tuple-element.14, f32[16,8,1,3584]{3,2,1,0:T(1,128)S(1)} %get-tuple-element.13, f32[16,8]{1,0:T(8,128)S(1)} %copy.48, f32[16,8]{1,0:T(8,128)S(1)} %copy.43), kind=kLoop, calls=%fused_computation.18 | loop fusion | flops 2695168 | bytes 3900416 | tf_op jit(solution)/shard_map/reduce_sum | solution.py:239
  173.6 0.7 add_convert_fusion
  (17 shorter events, 0.3 us)
Async XLA Ops:
  0.0 72.0 %copy-start = (bf16[128,3584]{1,0:T(8,128)(2,1)S(1)}, bf16[128,3584]{1,0:T(8,128)(2,1)}, u32[]{:S(2)}) copy-start(bf16[128,3584]{1,0:T(8,128)(2,1)} %param.17) | copy-start | bytes 2752516
  69.5 2.5 %copy-start.2 = (bf16[256,3584]{1,0:T(8,128)(2,1)S(1)}, bf16[256,3584]{1,0:T(8,128)(2,1)}, u32[]{:S(2)}) copy-start(bf16[256,3584]{1,0:T(8,128)(2,1)} %get-tuple-element.9) | copy-start | bytes 5505028
  75.6 6.8 %copy-start.5 = (bf16[256,3584]{1,0:T(8,128)(2,1)S(1)}, bf16[256,3584]{1,0:T(8,128)(2,1)}, u32[]{:S(2)}) copy-start(bf16[256,3584]{1,0:T(8,128)(2,1)} %get-tuple-element.10) | copy-start | bytes 5505028
  154.1 2.4 %copy-start.3 = (s32[16,8]{0,1:T(8,128)S(1)}, s32[16,8]{0,1:T(8,128)}, u32[]{:S(2)}) copy-start(s32[16,8]{0,1:T(8,128)} %param.10) | copy-start | bytes 1540
  154.1 2.9 %copy-start.1 = (bf16[256,3584]{1,0:T(8,128)(2,1)S(1)}, bf16[256,3584]{1,0:T(8,128)(2,1)}, u32[]{:S(2)}) copy-start(bf16[256,3584]{1,0:T(8,128)(2,1)} %get-tuple-element.12) | copy-start | bytes 5505028
  165.8 5.2 %copy-start.4 = (s32[16,8]{0,1:T(8,128)S(1)}, s32[16,8]{0,1:T(8,128)}, u32[]{:S(2)}) copy-start(s32[16,8]{0,1:T(8,128)} %param.11) | copy-start | bytes 1540

commit v3 on v2

--- a/solution.py
+++ b/solution.py
@@ -36,8 +36,12 @@
     recv_sems = refs[3 * count:4 * count]
     local_sems = refs[4 * count]
     axis_size = dict(zip(ALL_AXES, sizes))
-    world = sizes[0] * sizes[1]
-    world_me = flat_index(ALL_AXES, sizes)
+    greet_axes = max((axes for axes, _, _ in plans), key=len)
+    greet_sizes = tuple(axis_size[a] for a in greet_axes)
+    world = 1
+    for size in greet_sizes:
+        world *= size
+    world_me = flat_index(greet_axes, greet_sizes)
 
     barrier = pltpu.get_barrier_semaphore()
 
@@ -45,7 +49,7 @@
     def _(step):
         peer = lax.rem(world_me + step, world)
         pl.semaphore_signal(
-            barrier, inc=1, device_id=mesh_coords(peer, ALL_AXES, sizes),
+            barrier, inc=1, device_id=mesh_coords(peer, greet_axes, greet_sizes),
             device_id_type=MESH_ID,
         )
 
@@ -209,11 +213,11 @@
     outbound = jnp.dot(selector, tokens, preferred_element_type=jnp.float32).astype(
         jnp.bfloat16
     )
-    segment, received = exchange(
-        [tokens, outbound],
-        [(("inner",), row_count, True), (ALL_AXES, capacity, False)],
-        0,
-    )
+    received = lax.all_to_all(
+        outbound.reshape(total_count, capacity, model_width),
+        ALL_AXES, split_axis=0, concat_axis=0, tiled=True,
+    ).reshape(total_count * capacity, model_width)
+    (segment,) = exchange([tokens], [(("inner",), row_count, True)], 0)
     gate_part = jnp.dot(segment, shared_gate, preferred_element_type=jnp.float32)
     up_part = jnp.dot(segment, shared_up, preferred_element_type=jnp.float32)
     shared_hidden = (jax.nn.silu(gate_part) * up_part).astype(jnp.bfloat16)
@@ -221,11 +225,11 @@
         shared_hidden, shared_down, preferred_element_type=jnp.float32
     ).astype(jnp.bfloat16)
     answer = gated_mlp(received, expert_gate[0], expert_up[0], expert_down[0])
-    shared_parts, flat_rows = exchange(
-        [shared_partial, answer],
-        [(("inner",), row_count, False), (ALL_AXES, capacity, False)],
-        1,
-    )
+    flat_rows = lax.all_to_all(
+        answer.reshape(total_count, capacity, model_width),
+        ALL_AXES, split_axis=0, concat_axis=0, tiled=True,
+    ).reshape(total_count * capacity, model_width)
+    (shared_parts,) = exchange([shared_partial], [(("inner",), row_count, False)], 1)
     shared = jnp.sum(
         shared_parts.reshape(inner_count, row_count, model_width).astype(jnp.float32),
         axis=0,

time: 174 us -> 182 us (1.046); the launches traced: 174 us -> 179 us
  Pallas kernels: 126 us -> 79.1 us
  waiting for transfers between devices: 0 us -> 26 us
  starting transfers between devices: 0 us -> 17.4 us
  local copies, waits for them, and re-layouts: 14.3 us -> 25 us
    pallas_call x2, Pallas kernels: 126 us -> 79.1 us  [exchange(): pl.pallas_call(functools.partial(exchange_kernel, plans, sizes), out_shap...]
    all_to_all x0 -> x2, waiting for transfers between devices: none -> 26 us  [the longest x1 26 us: per_device(): lax.all_to_all(outbound.reshape(total_count, capacity, model_width), ALL_...]
    all_to_all x0 -> x2, starting transfers between devices: none -> 17.4 us  [the longest x1 11.5 us: per_device(): lax.all_to_all(outbound.reshape(total_count, capacity, model_width), ALL_...]
    reshape x0 -> x4, local copies, waits for them, and re-layouts: none -> 12.2 us  [the longest x1 4.79 us: per_device(): answer.reshape(total_count, capacity, model_width)]
  transfers between devices with their start and end apart: 0 -> 2, of which waited for: 0 -> 1; matrix products, arithmetic and copies ran while one was open for 0% -> 5% of each run, Pallas kernels for 0% -> 44%
where the time goes in v3:
time: 182 us; the launch traced here: 179 us
  Pallas kernels  79.1 us (43%)
  waiting for transfers between devices  26 us (14%)
  matrix products  25.1 us (14%)
  local copies, waits for them, and re-layouts  25 us (14%)
  starting transfers between devices  17.4 us (10%)
  other arithmetic  5.66 us (3%)
    pallas_call x2, Pallas kernels, exchange(): pl.pallas_call(functools.partial(exchange_kernel, plans, sizes), out_shap...  79.1 us
    all_to_all x1, waiting for transfers between devices, per_device(): lax.all_to_all(outbound.reshape(total_count, capacity, model_width), ALL_...  26 us
    all_to_all x1, starting transfers between devices, per_device(): lax.all_to_all(outbound.reshape(total_count, capacity, model_width), ALL_...  11.5 us
    dot_general x1, matrix products, gated_mlp(): jnp.dot(hidden, down_matrix, preferred_element_type=jnp.float32)  10.8 us
    gather x2, local copies, waits for them, and re-layouts, per_device(): flat_rows[chosen]  6.85 us
    dot_general x1, matrix products, gated_mlp(): gate_part = jnp.dot(inputs, gate_matrix, preferred_element_type=jnp.float32)  6.79 us
    all_to_all x1, starting transfers between devices, per_device(): lax.all_to_all(answer.reshape(total_count, capacity, model_width), ALL_AX...  5.9 us
    reshape x1, local copies, waits for them, and re-layouts, per_device(): answer.reshape(total_count, capacity, model_width)  4.79 us
  transfers between devices with their start and end apart: 2, of which 1 were waited for; matrix products, arithmetic and copies ran while one was open for 5% of the time, Pallas kernels for 44%

profile of v3, /device:TPU:1, one launch (start us, length us, event | category | flops | bytes accessed | tf_op | source)
XLA Modules:
  0.0 178.5 jit_solution(14328733234867027783)
XLA Ops:
  0.0 0.0 copy-start
  0.0 0.8 copy.42
  0.8 0.1 fusion.33
  1.0 0.1 copy.44
  1.1 0.1 copy.43
  1.2 0.1 and.43
  1.3 0.1 and.44
  1.4 0.1 eq.107
  1.6 1.6 convolution_convert_fusion.1
  3.2 1.7 reshape.76
  4.9 0.0 copy-start.3
  4.9 11.5 %all-to-all-start = ((bf16[128,2,3584]{2,1,0:T(2,128)(2,1)}), bf16[128,2,3584]{2,1,0:T(2,128)(2,1)S(1)}, u32[]{:S(2)}, u32[]{:S(2)}) async-start(bf16[128,2,3584]{2,1,0:T(2,128)(2,1)} %reshape.76), calls=%async_computation | async-start | bytes 3670016 | tf_op jit(solution)/shard_map/all_to_all | solution.py:216
  16.4 0.4 select_reduce_fusion
  16.8 0.1 copy.45
  16.9 0.0 copy-done.3
  16.9 0.1 convert_reduce_fusion.2
  17.0 26.0 %all-to-all-done = bf16[128,2,3584]{2,1,0:T(2,128)(2,1)S(1)} async-done(((bf16[128,2,3584]{2,1,0:T(2,128)(2,1)}), bf16[128,2,3584]{2,1,0:T(2,128)(2,1)S(1)}, u32[]{:S(2)}, u32[]{:S(2)}) %all-to-all-start) | async-done | bytes 1835040 | tf_op jit(solution)/shard_map/all_to_all | solution.py:216
  43.1 1.7 reshape.77
  44.7 0.0 copy-start.2
  44.7 6.8 %fusion.4 = f32[256,1024]{1,0:T(8,128)} fusion(bf16[256,3584]{1,0:T(8,128)(2,1)} %reshape.77, bf16[1,3584,1024]{2,1,0:T(8,128)(2,1)} %param.12), kind=kOutput, calls=%fused_computation.5 | convolution fusion | flops 1879048192 | bytes 10223616 | tf_op jit(solution)/shard_map/dot_general | solution.py:142
  51.5 0.0 copy-done.2
  51.5 10.8 %fusion.6 = bf16[256,3584]{1,0:T(8,128)(2,1)} fusion(bf16[1,1024,3584]{2,1,0:T(8,128)(2,1)} %param.14, bf16[256,3584]{1,0:T(8,128)(2,1)S(1)} %copy-done.2, bf16[1,3584,1024]{2,1,0:T(8,128)(2,1)} %param.13, f32[256,1024]{1,0:T(8,128)} %fusion.4), kind=kOutput, calls=%fused_computation.7 | convolution fusion | flops 3760586752 | bytes 19398656 | tf_op jit(solution)/shard_map/dot_general | solution.py:145
  62.3 4.8 %reshape.78 = bf16[128,2,3584]{2,1,0:T(2,128)(2,1)} reshape(bf16[256,3584]{1,0:T(8,128)(2,1)} %fusion.6) | data formatting | bytes 3670016 | tf_op jit(solution)/shard_map/reshape | solution.py:229
  67.1 5.9 %all-to-all-start.1 = ((bf16[128,2,3584]{2,1,0:T(2,128)(2,1)}), bf16[128,2,3584]{2,1,0:T(2,128)(2,1)}, u32[]{:S(2)}, u32[]{:S(2)}) async-start(bf16[128,2,3584]{2,1,0:T(2,128)(2,1)} %reshape.78), calls=%async_computation.1 | async-start | bytes 3670016 | tf_op jit(solution)/shard_map/all_to_all | solution.py:228
  73.0 0.0 copy-start.4
  73.0 48.4 %shard_map.91 = bf16[256,3584]{1,0:T(8,128)(2,1)} custom-call(bf16[16,3584]{1,0:T(8,128)(2,1)} %refs_0_.1), custom_call_target="tpu_custom_call" | custom-call | tf_op jit(solution)/shard_map/pallas_call | solution.py:127
  121.5 0.0 copy-start.1
  121.5 0.1 copy.46
  121.6 0.1 reshape.83
  121.8 0.1 copy.41
  121.9 0.0 copy-done.4
  122.0 0.1 copy.40
  122.1 0.1 copy.48
  122.2 2.4 %fusion.42 = f32[256,128]{1,0:T(8,128)S(1)} fusion(bf16[256,3584]{1,0:T(8,128)(2,1)} %shard_map.91, bf16[3584,128]{1,0:T(8,128)(2,1)} %param.15), kind=kOutput, calls=%fused_computation.65 | convolution fusion | flops 234881024 | bytes 2883584 | tf_op jit(solution)/shard_map/dot_general | solution.py:221
  124.5 0.0 copy-done
  124.6 0.0 copy-done.1
  124.6 3.6 %convolution_convert_fusion.refs_0_ = bf16[256,3584]{1,0:T(8,128)(2,1)} fusion(bf16[128,3584]{1,0:T(8,128)(2,1)S(1)} %copy-done, bf16[256,3584]{1,0:T(8,128)(2,1)S(1)} %copy-done.1, bf16[3584,128]{1,0:T(8,128)(2,1)} %param.16, f32[256,128]{1,0:T(8,128)S(1)} %fusion.42), kind=kOutput, calls=%fused_computation.8 | convolution fusion | flops 470876160 | bytes 5636096 | tf_op jit(solution)/shard_map/dot_general | solution.py:224
  128.2 30.7 %shard_map.92 = bf16[256,3584]{1,0:T(8,128)(2,1)} custom-call(bf16[256,3584]{1,0:T(8,128)(2,1)} %convolution_convert_fusion.refs_0_), custom_call_target="tpu_custom_call" | custom-call | tf_op jit(solution)/shard_map/pallas_call | solution.py:127
  158.9 1.8 convert_reduce_fusion
  160.6 0.0 all-to-all-done.1
  160.6 4.1 %reshape.79 = bf16[256,3584]{1,0:T(8,128)(2,1)S(1)} reshape(bf16[128,2,3584]{2,1,0:T(2,128)(2,1)} %all-to-all-done.1) | data formatting | bytes 3670016 | tf_op jit(solution)/shard_map/reshape | solution.py:231
  164.7 3.0 %gather_fusion = bf16[256,3584]{1,0:T(8,128)(2,1)} fusion(bf16[256,3584]{1,0:T(8,128)(2,1)S(1)} %reshape.79, s32[1024]{0:T(1024)S(1)} %pad_clamp_fusion), kind=kCustom, calls=%fused_computation | custom fusion | bytes 3671040 | tf_op jit(solution)/shard_map/gather | solution.py:241
  167.7 3.9 %reshape.82 = bf16[16,8,2,3584]{3,2,1,0:T(2,128)(2,1)S(1)} reshape(bf16[256,3584]{1,0:T(8,128)(2,1)} %gather_fusion) | data formatting | bytes 3670016 | tf_op jit(solution)/shard_map/gather | solution.py:241
  171.6 1.5 fusion.9
  173.1 3.9 %fusion.39 = (f32[16,8,1,3584]{3,2,1,0:T(1,128)S(1)}, f32[16,8,1,3584]{3,2,1,0:T(1,128)S(1)}) fusion(f32[16,8,2,3584]{3,2,1,0:T(2,128)S(1)} %fusion.9), kind=kLoop, calls=%fused_computation.62 | loop fusion | bytes 7340032 | tf_op jit(solution)/shard_map/slice | solution.py:163
  177.0 0.8 convert_reduce_fusion.1
  177.9 0.7 add_convert_fusion
  (17 shorter events, 0.3 us)
Async XLA Ops:
  0.0 124.5 %copy-start = (bf16[128,3584]{1,0:T(8,128)(2,1)S(1)}, bf16[128,3584]{1,0:T(8,128)(2,1)}, u32[]{:S(2)}) copy-start(bf16[128,3584]{1,0:T(8,128)(2,1)} %param.17) | copy-start | bytes 2752516
  4.9 12.0 %copy-start.3 = (s32[16,8]{0,1:T(8,128)S(1)}, s32[16,8]{0,1:T(8,128)}, u32[]{:S(2)}) copy-start(s32[16,8]{0,1:T(8,128)} %param.10) | copy-start | bytes 1540
  4.9 38.2 %all-to-all-start = ((bf16[128,2,3584]{2,1,0:T(2,128)(2,1)}), bf16[128,2,3584]{2,1,0:T(2,128)(2,1)S(1)}, u32[]{:S(2)}, u32[]{:S(2)}) async-start(bf16[128,2,3584]{2,1,0:T(2,128)(2,1)} %reshape.76), calls=%async_computation | async-start | bytes 3670016 | tf_op jit(solution)/shard_map/all_to_all | solution.py:216
  44.7 6.8 %copy-start.2 = (bf16[256,3584]{1,0:T(8,128)(2,1)S(1)}, bf16[256,3584]{1,0:T(8,128)(2,1)}, u32[]{:S(2)}) copy-start(bf16[256,3584]{1,0:T(8,128)(2,1)} %reshape.77) | copy-start | bytes 5505028
  67.1 93.6 %all-to-all-start.1 = ((bf16[128,2,3584]{2,1,0:T(2,128)(2,1)}), bf16[128,2,3584]{2,1,0:T(2,128)(2,1)}, u32[]{:S(2)}, u32[]{:S(2)}) async-start(bf16[128,2,3584]{2,1,0:T(2,128)(2,1)} %reshape.78), calls=%async_computation.1 | async-start | bytes 3670016 | tf_op jit(solution)/shard_map/all_to_all | solution.py:228
  73.0 49.0 %copy-start.4 = (s32[16,8]{0,1:T(8,128)S(1)}, s32[16,8]{0,1:T(8,128)}, u32[]{:S(2)}) copy-start(s32[16,8]{0,1:T(8,128)} %param.11) | copy-start | bytes 1540
  121.5 3.1 %copy-start.1 = (bf16[256,3584]{1,0:T(8,128)(2,1)S(1)}, bf16[256,3584]{1,0:T(8,128)(2,1)}, u32[]{:S(2)}) copy-start(bf16[256,3584]{1,0:T(8,128)(2,1)} %shard_map.91) | copy-start | bytes 5505028

commit v4 on v1

--- a/solution.py
+++ b/solution.py
@@ -1,10 +1,136 @@
+import functools
+import math
+
 import jax
 import jax.numpy as jnp
 from jax import lax
+from jax.experimental import pallas as pl
+from jax.experimental.pallas import tpu as pltpu
 from jax.sharding import PartitionSpec as P
 
 TOPK = 8
 TOP_GROUPS = 4
+MESH_ID = pl.DeviceIdType.MESH
+
+
+def torus_gather_kernel(side, tokens_ref, out_ref, send_sems, recv_sems, local_sems):
+    me = lax.axis_index("inner")
+    z, y = me // side, me % side
+    half = tokens_ref.shape[0] // 2
+
+    def node(zz, yy):
+        return lax.rem(zz + side, side) * side + lax.rem(yy + side, side)
+
+    steps = [
+        (lambda zz, yy, k: node(zz, yy + k), lambda zz, yy, k: node(zz + k, yy)),
+        (lambda zz, yy, k: node(zz + k, yy), lambda zz, yy, k: node(zz, yy + k)),
+    ]
+    neighbours = [node(z, y + 1), node(z, y - 1), node(z + 1, y), node(z - 1, y)]
+    barrier = pltpu.get_barrier_semaphore()
+    for peer in neighbours:
+        pl.semaphore_signal(barrier, inc=1, device_id={"inner": peer}, device_id_type=MESH_ID)
+    pl.semaphore_wait(barrier, len(neighbours))
+
+    rows = [pl.ds(0, half), pl.ds(half, half)]
+    for h in range(2):
+        pltpu.make_async_copy(
+            tokens_ref.at[rows[h]], out_ref.at[me, rows[h]], local_sems.at[h]
+        ).start()
+
+    counter = [0]
+
+    def run_round(moves):
+        started = []
+        for block, h, dest, from_tokens in moves:
+            index = counter[0]
+            counter[0] += 1
+            src = tokens_ref.at[rows[h]] if from_tokens else out_ref.at[block, rows[h]]
+            copy = pltpu.make_async_remote_copy(
+                src_ref=src,
+                dst_ref=out_ref.at[block, rows[h]],
+                send_sem=send_sems.at[index],
+                recv_sem=recv_sems.at[index],
+                device_id={"inner": dest},
+                device_id_type=MESH_ID,
+            )
+            copy.start()
+            started.append(copy)
+        return started
+
+    def finish(started, incoming):
+        for copy in started:
+            copy.wait_send()
+        for index, block, h, sender in incoming:
+            pltpu.make_async_remote_copy(
+                src_ref=out_ref.at[block, rows[h]],
+                dst_ref=out_ref.at[block, rows[h]],
+                send_sem=send_sems.at[index],
+                recv_sem=recv_sems.at[index],
+                device_id={"inner": sender},
+                device_id_type=MESH_ID,
+            ).wait_recv()
+
+    base = counter[0]
+    moves, incoming = [], []
+    for h in range(2):
+        first = steps[h][0]
+        for k in (1, -1):
+            moves.append((me, h, first(z, y, k), True))
+            incoming.append((base + len(incoming), first(z, y, -k), h, first(z, y, -k)))
+    finish(run_round(moves), incoming)
+    base = counter[0]
+    moves, incoming = [], []
+    for h in range(2):
+        first = steps[h][0]
+        moves.append((first(z, y, -1), h, first(z, y, 1), False))
+        incoming.append((base + len(incoming), first(z, y, -2), h, first(z, y, -1)))
+    finish(run_round(moves), incoming)
+    for h in range(2):
+        pltpu.make_async_copy(
+            tokens_ref.at[rows[h]], out_ref.at[me, rows[h]], local_sems.at[h]
+        ).wait()
+    base = counter[0]
+    moves, incoming = [], []
+    for h in range(2):
+        first, second = steps[h]
+        for k in (1, -1):
+            for j in range(side):
+                moves.append((first(z, y, j), h, second(z, y, k), False))
+                origin = second(z, y, -k)
+                oz, oy = origin // side, origin % side
+                incoming.append((base + len(incoming), first(oz, oy, j), h, origin))
+    finish(run_round(moves), incoming)
+    base = counter[0]
+    moves, incoming = [], []
+    for h in range(2):
+        first, second = steps[h]
+        src_node = second(z, y, -1)
+        sz, sy = src_node // side, src_node % side
+        far = second(z, y, -2)
+        fz, fy = far // side, far % side
+        for j in range(side):
+            moves.append((first(sz, sy, j), h, second(z, y, 1), False))
+            incoming.append((base + len(incoming), first(fz, fy, j), h, src_node))
+    finish(run_round(moves), incoming)
+
+
+def torus_gather(tokens, side, collective_id):
+    count = lax.axis_size("inner")
+    copies = 4 + 2 + 4 * side + 2 * side
+    return pl.pallas_call(
+        functools.partial(torus_gather_kernel, side),
+        out_shape=jax.ShapeDtypeStruct((count,) + tokens.shape, tokens.dtype),
+        in_specs=[pl.BlockSpec(memory_space=pl.ANY)],
+        out_specs=pl.BlockSpec(memory_space=pl.ANY),
+        scratch_shapes=[
+            pltpu.SemaphoreType.DMA((copies,)),
+            pltpu.SemaphoreType.DMA((copies,)),
+            pltpu.SemaphoreType.DMA((2,)),
+        ],
+        compiler_params=pltpu.CompilerParams(
+            collective_id=collective_id, has_side_effects=True
+        ),
+    )(tokens)
 
 
 def gated_mlp(inputs, gate_matrix, up_matrix, down_matrix):
@@ -72,10 +198,8 @@
     gate_matrix = expert_gate[0]
     up_matrix = expert_up[0]
     down_matrix = expert_down[0]
-    tiled_tokens = jnp.broadcast_to(tokens[None], (inner_count,) + tokens.shape)
-    segment = lax.all_to_all(
-        tiled_tokens, "inner", split_axis=0, concat_axis=0, tiled=True
-    ).reshape(inner_count * row_count, model_width)
+    side = math.isqrt(inner_count)
+    segment = torus_gather(tokens, side, 0).reshape(inner_count * row_count, model_width)
     gate_part = jnp.dot(segment, shared_gate, preferred_element_type=jnp.float32)
     up_part = jnp.dot(segment, shared_up, preferred_element_type=jnp.float32)
     shared_hidden = (jax.nn.silu(gate_part) * up_part).astype(jnp.bfloat16)

time: 158 us -> 154 us (0.975)
  waiting for transfers between devices: 68.4 us -> 25.3 us
  Pallas kernels: 0 us -> 40.2 us
  local copies, waits for them, and re-layouts: 30.8 us -> 29.1 us
    pallas_call x0 -> x1, Pallas kernels: none -> 40.2 us  [torus_gather(): pl.pallas_call(functools.partial(torus_gather_kernel, side), out_shape=ja...]
    all_to_all x1 -> x0, waiting for transfers between devices: 22.7 us -> none  [per_device(): lax.all_to_all(tiled_tokens, 'inner', split_axis=0, concat_axis=0, tiled=...]
    all_to_all x1, waiting for transfers between devices: 20.3 us -> 0.01 us  [per_device(): lax.all_to_all(outbound, ('outer', 'inner'), split_axis=0, concat_axis=0,...]
    all_to_all x1 -> x0, starting transfers between devices: 8.73 us -> none  [per_device(): lax.all_to_all(tiled_tokens, 'inner', split_axis=0, concat_axis=0, tiled=...]
    all_to_all x1, starting transfers between devices: 7.56 us -> 11.9 us  [per_device(): lax.all_to_all(outbound, ('outer', 'inner'), split_axis=0, concat_axis=0,...]
    all_to_all x1, starting transfers between devices: 9.35 us -> 13.2 us  [per_device(): lax.all_to_all(answer.reshape(received.shape), ('outer', 'inner'), split_...]
    broadcast_in_dim x1 -> x0, local copies, waits for them, and re-layouts: 2.41 us -> none  [per_device(): tiled_tokens = jnp.broadcast_to(tokens[None], (inner_count,) + tokens.shape)]
  transfers between devices with their start and end apart: 4 -> 3, of which waited for: 3 -> 1; matrix products, arithmetic and copies ran while one was open for 25% -> 23% of each run, Pallas kernels for 0% -> 26%
where the time goes in v4:
time: 154 us
  Pallas kernels  40.2 us (26%)
  starting transfers between devices  29.4 us (19%)
  local copies, waits for them, and re-layouts  29.1 us (19%)
  matrix products  25.5 us (17%)
  waiting for transfers between devices  25.3 us (16%)
  other arithmetic  4.14 us (3%)
    pallas_call x1, Pallas kernels, torus_gather(): pl.pallas_call(functools.partial(torus_gather_kernel, side), out_shape=ja...  40.2 us
    all_to_all x1, waiting for transfers between devices, per_device(): lax.all_to_all(answer.reshape(received.shape), ('outer', 'inner'), split_...  25.3 us
    all_to_all x1, starting transfers between devices, per_device(): lax.all_to_all(answer.reshape(received.shape), ('outer', 'inner'), split_...  13.2 us
    all_to_all x1, starting transfers between devices, per_device(): lax.all_to_all(outbound, ('outer', 'inner'), split_axis=0, concat_axis=0,...  11.9 us
    dot_general x1, matrix products, gated_mlp(): jnp.dot(hidden, down_matrix, preferred_element_type=jnp.float32)  11.2 us
    gather x2, local copies, waits for them, and re-layouts, per_device(): flat_rows[chosen]  6.85 us
    dot_general x1, matrix products, gated_mlp(): gate_part = jnp.dot(inputs, gate_matrix, preferred_element_type=jnp.float32)  6.71 us
    reshape x1, local copies, waits for them, and re-layouts, per_device(): received.reshape(-1, model_width)  4.93 us
  transfers between devices with their start and end apart: 3, of which 1 were waited for; matrix products, arithmetic and copies ran while one was open for 23% of the time, Pallas kernels for 26%

profile of v4, /device:TPU:1, one launch (start us, length us, event | category | flops | bytes accessed | tf_op | source)
XLA Modules:
  0.0 153.8 jit_solution(15101519700518879763)
XLA Ops:
  0.0 0.0 copy-start
  0.0 0.8 copy.47
  0.8 0.1 fusion.31
  1.0 1.6 %convolution_convert_fusion.1 = bf16[128,2,3584]{2,0,1:T(8,128)(2,1)S(1)} fusion(bf16[16,3584]{1,0:T(8,128)(2,1)} %tokens_ref.1, s32[128,16]{0,1:T(8,128)S(1)} %bitcast.59, pred[128,16]{0,1:T(8,128)(4,1)S(1)} %get-tuple-element.11), kind=kOutput, calls=%fused_computation.9 | convolution fusion | flops 30285824 | bytes 1959936 | tf_op jit(solution)/shard_map/ecr,rd->ecd/dot_general | solution.py:227
  2.6 3.1 %copy.48 = bf16[128,2,3584]{2,1,0:T(2,128)(2,1)} copy(bf16[128,2,3584]{2,0,1:T(8,128)(2,1)S(1)} %convolution_convert_fusion.1) | data formatting | bytes 3670016 | tf_op jit(solution)/shard_map/convert_element_type | solution.py:229
  5.7 11.9 %all-to-all-start.1 = ((bf16[128,2,3584]{2,1,0:T(2,128)(2,1)}), bf16[128,2,3584]{2,1,0:T(2,128)(2,1)}, u32[]{:S(2)}, u32[]{:S(2)}) async-start(bf16[128,2,3584]{2,1,0:T(2,128)(2,1)} %copy.48), calls=%async_computation.1 | async-start | bytes 3670016 | tf_op jit(solution)/shard_map/all_to_all | solution.py:230
  17.6 0.0 copy-start.2
  17.6 40.2 %shard_map.91 = bf16[16,16,3584]{2,1,0:T(8,128)(2,1)} custom-call(bf16[16,3584]{1,0:T(8,128)(2,1)} %tokens_ref.1), custom_call_target="tpu_custom_call" | custom-call | tf_op jit(solution)/shard_map/pallas_call | solution.py:120
  57.8 0.0 copy-start.1
  57.8 0.4 select_reduce_fusion
  58.2 0.1 copy.49
  58.3 0.0 copy-done.2
  58.3 0.1 convert_reduce_fusion.2
  58.4 2.4 %fusion.43 = f32[256,128]{1,0:T(8,128)S(1)} fusion(bf16[256,3584]{1,0:T(8,128)(2,1)} %bitcast.56, bf16[3584,128]{1,0:T(8,128)(2,1)} %param.15), kind=kOutput, calls=%fused_computation.66 | convolution fusion | flops 234881024 | bytes 2883584 | tf_op jit(solution)/shard_map/dot_general | solution.py:203
  60.8 0.0 copy-done
  60.8 0.0 copy-done.1
  60.8 3.6 %convolution_convert_fusion = bf16[256,3584]{1,0:T(8,128)(2,1)} fusion(bf16[128,3584]{1,0:T(8,128)(2,1)S(1)} %copy-done, bf16[256,3584]{1,0:T(8,128)(2,1)S(1)} %bitcast.57, bf16[3584,128]{1,0:T(8,128)(2,1)} %param.16, f32[256,128]{1,0:T(8,128)S(1)} %fusion.43), kind=kOutput, calls=%fused_computation.8 | convolution fusion | flops 470876160 | bytes 5636096 | tf_op jit(solution)/shard_map/dot_general | solution.py:206
  64.4 0.0 all-to-all-done.1
  64.4 4.3 %all-to-all-start = ((bf16[16,16,3584]{2,1,0:T(8,128)(2,1)}), bf16[16,16,3584]{2,1,0:T(8,128)(2,1)S(1)}, u32[]{:S(2)}, u32[]{:S(2)}) async-start(bf16[16,16,3584]{2,1,0:T(8,128)(2,1)} %bitcast.58), calls=%async_computation | async-start | bytes 3670016 | tf_op jit(solution)/shard_map/all_to_all | solution.py:209
  68.7 4.9 %reshape.74 = bf16[256,3584]{1,0:T(8,128)(2,1)} reshape(bf16[128,2,3584]{2,1,0:T(2,128)(2,1)} %all-to-all-done.1) | data formatting | bytes 3670016 | tf_op jit(solution)/shard_map/reshape | solution.py:231
  73.6 6.7 %fusion.4 = f32[256,1024]{1,0:T(8,128)} fusion(bf16[256,3584]{1,0:T(8,128)(2,1)} %reshape.74, bf16[1,3584,1024]{2,1,0:T(8,128)(2,1)} %param.12), kind=kOutput, calls=%fused_computation.5 | convolution fusion | flops 1879048192 | bytes 10223616 | tf_op jit(solution)/shard_map/dot_general | solution.py:137
  80.4 11.2 %fusion.6 = bf16[256,3584]{1,0:T(8,128)(2,1)} fusion(bf16[1,1024,3584]{2,1,0:T(8,128)(2,1)} %param.14, bf16[256,3584]{1,0:T(8,128)(2,1)} %reshape.74, bf16[1,3584,1024]{2,1,0:T(8,128)(2,1)} %param.13, f32[256,1024]{1,0:T(8,128)} %fusion.4), kind=kOutput, calls=%fused_computation.7 | convolution fusion | flops 3760586752 | bytes 19398656 | tf_op jit(solution)/shard_map/dot_general | solution.py:140
  91.6 4.8 %reshape.75 = bf16[128,2,3584]{2,1,0:T(2,128)(2,1)} reshape(bf16[256,3584]{1,0:T(8,128)(2,1)} %fusion.6) | data formatting | bytes 3670016 | tf_op jit(solution)/shard_map/reshape | solution.py:233
  96.4 0.0 copy-start.3
  96.4 0.0 all-to-all-done
  96.4 13.2 %all-to-all-start.2 = ((bf16[128,2,3584]{2,1,0:T(2,128)(2,1)}), bf16[128,2,3584]{2,1,0:T(2,128)(2,1)}, u32[]{:S(2)}, u32[]{:S(2)}) async-start(bf16[128,2,3584]{2,1,0:T(2,128)(2,1)} %reshape.75), calls=%async_computation.2 | async-start | bytes 3670016 | tf_op jit(solution)/shard_map/all_to_all | solution.py:232
  109.7 0.1 copy.50
  109.8 0.1 reshape.79
  110.0 0.1 copy.46
  110.1 0.0 copy-done.3
  110.2 0.1 copy.45
  110.3 0.1 copy.52
  110.4 0.2 convert_reduce_fusion
  110.6 25.3 %all-to-all-done.2 = bf16[128,2,3584]{2,1,0:T(2,128)(2,1)} async-done(((bf16[128,2,3584]{2,1,0:T(2,128)(2,1)}), bf16[128,2,3584]{2,1,0:T(2,128)(2,1)}, u32[]{:S(2)}, u32[]{:S(2)}) %all-to-all-start.2) | async-done | bytes 1835040 | tf_op jit(solution)/shard_map/all_to_all | solution.py:232
  135.9 4.1 %reshape.76 = bf16[256,3584]{1,0:T(8,128)(2,1)S(1)} reshape(bf16[128,2,3584]{2,1,0:T(2,128)(2,1)} %all-to-all-done.2) | data formatting | bytes 3670016 | tf_op jit(solution)/shard_map/reshape | solution.py:235
  140.0 3.0 %gather_fusion = bf16[256,3584]{1,0:T(8,128)(2,1)} fusion(bf16[256,3584]{1,0:T(8,128)(2,1)S(1)} %reshape.76, s32[1024]{0:T(1024)S(1)} %pad_clamp_fusion), kind=kCustom, calls=%fused_computation | custom fusion | bytes 3671040 | tf_op jit(solution)/shard_map/gather | solution.py:240
  143.0 3.9 %reshape.78 = bf16[16,8,2,3584]{3,2,1,0:T(2,128)(2,1)S(1)} reshape(bf16[256,3584]{1,0:T(8,128)(2,1)} %gather_fusion) | data formatting | bytes 3670016 | tf_op jit(solution)/shard_map/gather | solution.py:240
  146.9 1.5 %fusion.9 = f32[16,8,2,3584]{3,2,1,0:T(2,128)S(1)} fusion(bf16[16,8,2,3584]{3,2,1,0:T(2,128)(2,1)S(1)} %reshape.78, pred[16,8,2]{2,1,0:T(8,128)(4,1)S(1)} %copy.46), kind=kLoop, calls=%fused_computation.12 | loop fusion | flops 1835008 | bytes 5505280 | tf_op jit(solution)/shard_map/convert_element_type | solution.py:156
  148.4 3.9 %fusion.41 = (f32[16,8,1,3584]{3,2,1,0:T(1,128)S(1)}, f32[16,8,1,3584]{3,2,1,0:T(1,128)S(1)}) fusion(f32[16,8,2,3584]{3,2,1,0:T(2,128)S(1)} %fusion.9), kind=kLoop, calls=%fused_computation.64 | loop fusion | bytes 7340032 | tf_op jit(solution)/shard_map/slice | solution.py:158
  152.3 0.8 convert_reduce_fusion.1
  153.2 0.7 add_convert_fusion
  (15 shorter events, 0.2 us)
Async XLA Ops:
  0.0 60.8 %copy-start = (bf16[128,3584]{1,0:T(8,128)(2,1)S(1)}, bf16[128,3584]{1,0:T(8,128)(2,1)}, u32[]{:S(2)}) copy-start(bf16[128,3584]{1,0:T(8,128)(2,1)} %param.17) | copy-start | bytes 2752516
  5.7 58.7 %all-to-all-start.1 = ((bf16[128,2,3584]{2,1,0:T(2,128)(2,1)}), bf16[128,2,3584]{2,1,0:T(2,128)(2,1)}, u32[]{:S(2)}, u32[]{:S(2)}) async-start(bf16[128,2,3584]{2,1,0:T(2,128)(2,1)} %copy.48), calls=%async_computation.1 | async-start | bytes 3670016 | tf_op jit(solution)/shard_map/all_to_all | solution.py:230
  17.6 40.7 %copy-start.2 = (s32[16,8]{0,1:T(8,128)S(1)}, s32[16,8]{0,1:T(8,128)}, u32[]{:S(2)}) copy-start(s32[16,8]{0,1:T(8,128)} %param.10) | copy-start | bytes 1540
  57.8 3.0 %copy-start.1 = (bf16[16,16,3584]{2,1,0:T(8,128)(2,1)S(1)}, bf16[16,16,3584]{2,1,0:T(8,128)(2,1)}, u32[]{:S(2)}) copy-start(bf16[16,16,3584]{2,1,0:T(8,128)(2,1)} %shard_map.91) | copy-start | bytes 5505028
  64.4 31.9 %all-to-all-start = ((bf16[16,16,3584]{2,1,0:T(8,128)(2,1)}), bf16[16,16,3584]{2,1,0:T(8,128)(2,1)S(1)}, u32[]{:S(2)}, u32[]{:S(2)}) async-start(bf16[16,16,3584]{2,1,0:T(8,128)(2,1)} %bitcast.58), calls=%async_computation | async-start | bytes 3670016 | tf_op jit(solution)/shard_map/all_to_all | solution.py:209
  96.4 13.8 %copy-start.3 = (s32[16,8]{0,1:T(8,128)S(1)}, s32[16,8]{0,1:T(8,128)}, u32[]{:S(2)}) copy-start(s32[16,8]{0,1:T(8,128)} %param.11) | copy-start | bytes 1540
  96.4 39.6 %all-to-all-start.2 = ((bf16[128,2,3584]{2,1,0:T(2,128)(2,1)}), bf16[128,2,3584]{2,1,0:T(2,128)(2,1)}, u32[]{:S(2)}, u32[]{:S(2)}) async-start(bf16[128,2,3584]{2,1,0:T(2,128)(2,1)} %reshape.75), calls=%async_computation.2 | async-start | bytes 3670016 | tf_op jit(solution)/shard_map/all_to_all | solution.py:232

commit v5 on v4

--- a/solution.py
+++ b/solution.py
@@ -11,6 +11,129 @@
 TOPK = 8
 TOP_GROUPS = 4
 MESH_ID = pl.DeviceIdType.MESH
+
+ALL_AXES = ("outer", "inner")
+
+
+def flat_index(axes, sizes):
+    index = 0
+    for axis, size in zip(axes, sizes):
+        index = index * size + lax.axis_index(axis)
+    return index
+
+
+def mesh_coords(flat, axes, sizes):
+    coords = []
+    for size in reversed(sizes):
+        coords.append(flat % size)
+        flat = flat // size
+    return dict(zip(axes, reversed(coords)))
+
+
+def exchange_kernel(plans, sizes, *refs):
+    count = len(plans)
+    sends = refs[:count]
+    recvs = refs[count:2 * count]
+    send_sems = refs[2 * count:3 * count]
+    recv_sems = refs[3 * count:4 * count]
+    local_sems = refs[4 * count]
+    axis_size = dict(zip(ALL_AXES, sizes))
+    world = sizes[0] * sizes[1]
+    world_me = flat_index(ALL_AXES, sizes)
+
+    barrier = pltpu.get_barrier_semaphore()
+
+    @pl.loop(1, world)
+    def _(step):
+        peer = lax.rem(world_me + step, world)
+        pl.semaphore_signal(
+            barrier, inc=1, device_id=mesh_coords(peer, ALL_AXES, sizes),
+            device_id_type=MESH_ID,
+        )
+
+    pl.semaphore_wait(barrier, world - 1)
+
+    def block(ref, index, rows, same):
+        if same:
+            return ref
+        return ref.at[pl.ds(index * rows, rows)]
+
+    locals_ = []
+    for k, (axes, rows, same) in enumerate(plans):
+        axis_sizes = tuple(axis_size[a] for a in axes)
+        me = flat_index(axes, axis_sizes)
+        local = pltpu.make_async_copy(
+            block(sends[k], me, rows, same), recvs[k].at[pl.ds(me * rows, rows)],
+            local_sems.at[k],
+        )
+        local.start()
+        locals_.append(local)
+
+    for k, (axes, rows, same) in enumerate(plans):
+        axis_sizes = tuple(axis_size[a] for a in axes)
+        n = 1
+        for size in axis_sizes:
+            n *= size
+        me = flat_index(axes, axis_sizes)
+
+        @pl.loop(1, n)
+        def _(step):
+            peer = lax.rem(me + step, n)
+            pltpu.make_async_remote_copy(
+                src_ref=block(sends[k], peer, rows, same),
+                dst_ref=recvs[k].at[pl.ds(me * rows, rows)],
+                send_sem=send_sems[k].at[peer],
+                recv_sem=recv_sems[k].at[me],
+                device_id=mesh_coords(peer, axes, axis_sizes),
+                device_id_type=MESH_ID,
+            ).start()
+
+    for k, (axes, rows, same) in enumerate(plans):
+        axis_sizes = tuple(axis_size[a] for a in axes)
+        n = 1
+        for size in axis_sizes:
+            n *= size
+        me = flat_index(axes, axis_sizes)
+
+        @pl.loop(1, n)
+        def _(step):
+            peer = lax.rem(me + step, n)
+            pltpu.make_async_remote_copy(
+                src_ref=block(sends[k], peer, rows, same),
+                dst_ref=recvs[k].at[pl.ds(peer * rows, rows)],
+                send_sem=send_sems[k].at[peer],
+                recv_sem=recv_sems[k].at[peer],
+                device_id=mesh_coords(peer, axes, axis_sizes),
+                device_id_type=MESH_ID,
+            ).wait()
+
+    for local in locals_:
+        local.wait()
+
+
+def exchange(sends, plans, collective_id):
+    sizes = (lax.axis_size("outer"), lax.axis_size("inner"))
+    axis_size = dict(zip(ALL_AXES, sizes))
+    out_shapes = []
+    sem_shapes = []
+    for send, (axes, rows, same) in zip(sends, plans):
+        n = 1
+        for a in axes:
+            n *= axis_size[a]
+        out_shapes.append(jax.ShapeDtypeStruct((n * rows,) + send.shape[1:], send.dtype))
+        sem_shapes.append(n)
+    return pl.pallas_call(
+        functools.partial(exchange_kernel, plans, sizes),
+        out_shape=tuple(out_shapes),
+        in_specs=[pl.BlockSpec(memory_space=pl.ANY)] * len(sends),
+        out_specs=tuple(pl.BlockSpec(memory_space=pl.ANY) for _ in sends),
+        scratch_shapes=[pltpu.SemaphoreType.DMA((n,)) for n in sem_shapes]
+        + [pltpu.SemaphoreType.DMA((n,)) for n in sem_shapes]
+        + [pltpu.SemaphoreType.DMA((len(sends),))],
+        compiler_params=pltpu.CompilerParams(
+            collective_id=collective_id, has_side_effects=True
+        ),
+    )(*sends)
 
 
 def torus_gather_kernel(side, tokens_ref, out_ref, send_sems, recv_sems, local_sems):
@@ -224,15 +347,14 @@
     selector = jnp.logical_and(
         named_mask.T[:, None, :] == 1, earlier.T[:, None, :] == slot_ids
     ).astype(jnp.bfloat16)
-    outbound = jnp.einsum(
-        "ecr,rd->ecd", selector, tokens, preferred_element_type=jnp.float32
+    outbound = jnp.dot(
+        selector.reshape(total_count * capacity, row_count),
+        tokens,
+        preferred_element_type=jnp.float32,
     ).astype(jnp.bfloat16)
-    received = lax.all_to_all(outbound, ("outer", "inner"), split_axis=0, concat_axis=0, tiled=True)
-    answer = gated_mlp(received.reshape(-1, model_width), gate_matrix, up_matrix, down_matrix)
-    returned = lax.all_to_all(
-        answer.reshape(received.shape), ("outer", "inner"), split_axis=0, concat_axis=0, tiled=True
-    )
-    flat_rows = returned.reshape(-1, model_width)
+    (received,) = exchange([outbound], [(ALL_AXES, capacity, False)], 1)
+    answer = gated_mlp(received, gate_matrix, up_matrix, down_matrix)
+    (flat_rows,) = exchange([answer], [(ALL_AXES, capacity, False)], 2)
     slot_index = experts * capacity + slot_ranks
     chosen, present, pair_weights = pair_tables(
         group_ids, slot_rank, slot_index, weights, outer_count

time: 154 us -> 162 us (1.052)
  Pallas kernels: 40.2 us -> 104 us
  starting transfers between devices: 29.4 us -> 4.02 us
  waiting for transfers between devices: 25.3 us -> 0.01 us
  local copies, waits for them, and re-layouts: 29.1 us -> 19.5 us
  other arithmetic: 4.14 us -> 7.44 us
    pallas_call x0 -> x2, Pallas kernels: none -> 80.3 us  [exchange(): pl.pallas_call(functools.partial(exchange_kernel, plans, sizes), out_shap...]
    all_to_all x2 -> x0, waiting for transfers between devices: 25.3 us -> none  [the longest x1 25.3 us: per_device(): lax.all_to_all(answer.reshape(received.shape), ('outer', 'inner'), split_...]
    all_to_all x2 -> x0, starting transfers between devices: 25.1 us -> none  [the longest x1 13.2 us: per_device(): lax.all_to_all(answer.reshape(received.shape), ('outer', 'inner'), split_...]
    pallas_call x1, Pallas kernels: 40.2 us -> 23.7 us  [torus_gather(): pl.pallas_call(functools.partial(torus_gather_kernel, side), out_shape=ja...]
    reshape x3 -> x0, local copies, waits for them, and re-layouts: 13.7 us -> none  [the longest x1 4.93 us: per_device(): received.reshape(-1, model_width)]
    gather x2, local copies, waits for them, and re-layouts: 6.85 us -> 11.3 us  [per_device(): flat_rows[chosen]]
    convert_element_type x1, other arithmetic: 1.55 us -> 4.89 us  [combine_pairs(): values = pair_rows.astype(jnp.float32)]
    convert_element_type x1 -> x0, local copies, waits for them, and re-layouts: 3.14 us -> none  [per_device(): outbound = jnp.einsum('ecr,rd->ecd', selector, tokens, preferred_element_...]
  transfers between devices with their start and end apart: 3 -> 1, of which waited for: 1 -> 0; matrix products, arithmetic and copies ran while one was open for 23% -> 28% of each run, Pallas kernels for 26% -> 50%
where the time goes in v5:
time: 162 us; the launch traced here: 161 us
  Pallas kernels  104 us (64%)
  matrix products  26 us (16%)
  local copies, waits for them, and re-layouts  19.5 us (12%)
  other arithmetic  7.44 us (5%)
  starting transfers between devices  4.02 us (2%)
    pallas_call x2, Pallas kernels, exchange(): pl.pallas_call(functools.partial(exchange_kernel, plans, sizes), out_shap...  80.3 us
    pallas_call x1, Pallas kernels, torus_gather(): pl.pallas_call(functools.partial(torus_gather_kernel, side), out_shape=ja...  23.7 us
    gather x2, local copies, waits for them, and re-layouts, per_device(): flat_rows[chosen]  11.3 us
    dot_general x1, matrix products, gated_mlp(): jnp.dot(hidden, down_matrix, preferred_element_type=jnp.float32)  11.2 us
    slice x1, local copies, waits for them, and re-layouts, combine_pairs(): values[..., 0, :]  6.89 us
    dot_general x1, matrix products, gated_mlp(): gate_part = jnp.dot(inputs, gate_matrix, preferred_element_type=jnp.float32)  6.71 us
    convert_element_type x1, other arithmetic, combine_pairs(): values = pair_rows.astype(jnp.float32)  4.89 us
    all_to_all x1, starting transfers between devices, per_device(): lax.all_to_all(shared_partial.reshape(inner_count, row_count, model_width...  4.02 us
  transfers between devices with their start and end apart: 1, of which 0 were waited for; matrix products, arithmetic and copies ran while one was open for 28% of the time, Pallas kernels for 50%

profile of v5, /device:TPU:1, one launch (start us, length us, event | category | flops | bytes accessed | tf_op | source)
XLA Modules:
  0.0 161.1 jit_solution(17594252918336908831)
XLA Ops:
  0.0 0.0 copy-start
  0.0 23.7 %shard_map.91 = bf16[16,16,3584]{2,1,0:T(8,128)(2,1)} custom-call(bf16[16,3584]{1,0:T(8,128)(2,1)} %tokens_ref.1), custom_call_target="tpu_custom_call" | custom-call | tf_op jit(solution)/shard_map/pallas_call | solution.py:243
  23.7 0.0 copy-start.1
  23.7 2.5 %fusion.42 = f32[256,128]{1,0:T(8,128)S(1)} fusion(bf16[256,3584]{1,0:T(8,128)(2,1)} %bitcast.55, bf16[3584,128]{1,0:T(8,128)(2,1)} %param.15), kind=kOutput, calls=%fused_computation.65 | convolution fusion | flops 234881024 | bytes 2883584 | tf_op jit(solution)/shard_map/dot_general | solution.py:326
  26.2 0.0 copy-done
  26.2 0.0 copy-done.1
  26.2 3.6 %convolution_convert_fusion = bf16[256,3584]{1,0:T(8,128)(2,1)} fusion(bf16[128,3584]{1,0:T(8,128)(2,1)S(1)} %copy-done, bf16[256,3584]{1,0:T(8,128)(2,1)S(1)} %bitcast.56, bf16[3584,128]{1,0:T(8,128)(2,1)} %param.16, f32[256,128]{1,0:T(8,128)S(1)} %fusion.42), kind=kOutput, calls=%fused_computation.8 | convolution fusion | flops 470876160 | bytes 5636096 | tf_op jit(solution)/shard_map/dot_general | solution.py:329
  29.8 0.0 copy-start.3
  29.8 0.0 copy-start.2
  29.8 4.0 %all-to-all-start = ((bf16[16,16,3584]{2,1,0:T(8,128)(2,1)}), bf16[16,16,3584]{2,1,0:T(8,128)(2,1)S(1)}, u32[]{:S(2)}, u32[]{:S(2)}) async-start(bf16[16,16,3584]{2,1,0:T(8,128)(2,1)} %bitcast.57), calls=%async_computation | async-start | bytes 3670016 | tf_op jit(solution)/shard_map/all_to_all | solution.py:332
  33.9 0.0 copy-done.3
  33.9 0.1 copy.42
  34.0 0.1 fusion.33
  34.1 0.4 select_reduce_fusion
  34.5 0.1 copy.45
  34.6 0.1 convert_reduce_fusion.2
  34.8 0.1 copy.46
  35.0 0.1 reshape.71
  35.1 0.1 copy.44
  35.2 0.1 copy.43
  35.4 0.1 and.43
  35.4 0.1 and.44
  35.5 0.1 eq.107
  35.7 0.0 copy-done.2
  35.7 1.9 %convolution_convert_fusion.1.refs_0_ = bf16[256,3584]{1,0:T(8,128)(2,1)} fusion(bf16[16,3584]{1,0:T(8,128)(2,1)S(1)} %copy-done.2, pred[256,16]{1,0:T(32,128)(4,1)S(1)} %and.44, s32[256,16]{1,0:T(8,128)S(1)} %bitcast.58, s32[256]{0:T(256)S(1)} %eq.107), kind=kOutput, calls=%fused_computation.9 | convolution fusion | flops 30285824 | bytes 1971200 | tf_op jit(solution)/shard_map/dot_general | solution.py:350
  37.6 43.3 %shard_map.92 = bf16[256,3584]{1,0:T(8,128)(2,1)} custom-call(bf16[256,3584]{1,0:T(8,128)(2,1)} %convolution_convert_fusion.1.refs_0_), custom_call_target="tpu_custom_call" | custom-call | tf_op jit(solution)/shard_map/pallas_call | solution.py:125
  81.0 6.7 %fusion.4 = f32[256,1024]{1,0:T(8,128)} fusion(bf16[256,3584]{1,0:T(8,128)(2,1)} %shard_map.92, bf16[1,3584,1024]{2,1,0:T(8,128)(2,1)} %param.12), kind=kOutput, calls=%fused_computation.5 | convolution fusion | flops 1879048192 | bytes 10223616 | tf_op jit(solution)/shard_map/dot_general | solution.py:260
  87.7 11.2 %fusion.6.refs_0_ = bf16[256,3584]{1,0:T(8,128)(2,1)} fusion(bf16[1,1024,3584]{2,1,0:T(8,128)(2,1)} %param.14, bf16[256,3584]{1,0:T(8,128)(2,1)} %shard_map.92, bf16[1,3584,1024]{2,1,0:T(8,128)(2,1)} %param.13, f32[256,1024]{1,0:T(8,128)} %fusion.4), kind=kOutput, calls=%fused_computation.7 | convolution fusion | flops 3760586752 | bytes 19398656 | tf_op jit(solution)/shard_map/dot_general | solution.py:263
  98.9 37.0 %shard_map.93 = bf16[256,3584]{1,0:T(8,128)(2,1)} custom-call(bf16[256,3584]{1,0:T(8,128)(2,1)} %fusion.6.refs_0_), custom_call_target="tpu_custom_call" | custom-call | tf_op jit(solution)/shard_map/pallas_call | solution.py:125
  135.9 6.5 %gather_fusion = bf16[256,3584]{1,0:T(8,128)(2,1)} fusion(bf16[256,3584]{1,0:T(8,128)(2,1)} %shard_map.93, s32[1024]{0:T(1024)S(1)} %pad_clamp_fusion), kind=kCustom, calls=%fused_computation | custom fusion | bytes 3671040 | tf_op jit(solution)/shard_map/gather | solution.py:362
  142.4 0.0 copy-start.4
  142.4 4.8 %reshape.70 = bf16[16,8,2,3584]{3,2,1,0:T(2,128)(2,1)} reshape(bf16[256,3584]{1,0:T(8,128)(2,1)} %gather_fusion) | data formatting | bytes 3670016 | tf_op jit(solution)/shard_map/gather | solution.py:362
  147.2 0.1 copy.41
  147.4 0.0 copy-done.4
  147.4 4.9 %fusion.9 = f32[16,8,2,3584]{3,2,1,0:T(2,128)} fusion(bf16[16,8,2,3584]{3,2,1,0:T(2,128)(2,1)} %reshape.70, pred[16,8,2]{2,1,0:T(8,128)(4,1)S(1)} %copy.41), kind=kLoop, calls=%fused_computation.12 | loop fusion | flops 1835008 | bytes 5505280 | tf_op jit(solution)/shard_map/convert_element_type | solution.py:279
  152.4 0.1 copy.40
  152.4 0.1 copy.48
  152.5 6.9 %fusion.39 = (f32[16,8,1,3584]{3,2,1,0:T(1,128)S(1)}, f32[16,8,1,3584]{3,2,1,0:T(1,128)S(1)}) fusion(f32[16,8,2,3584]{3,2,1,0:T(2,128)} %fusion.9), kind=kLoop, calls=%fused_computation.62 | loop fusion | bytes 7340032 | tf_op jit(solution)/shard_map/slice | solution.py:281
  159.4 0.8 convert_reduce_fusion.1
  160.2 0.0 all-to-all-done
  160.2 0.2 convert_reduce_fusion
  160.4 0.7 add_convert_fusion
  (17 shorter events, 0.3 us)
Async XLA Ops:
  0.0 26.2 %copy-start = (bf16[128,3584]{1,0:T(8,128)(2,1)S(1)}, bf16[128,3584]{1,0:T(8,128)(2,1)}, u32[]{:S(2)}) copy-start(bf16[128,3584]{1,0:T(8,128)(2,1)} %param.17) | copy-start | bytes 2752516
  23.7 2.5 %copy-start.1 = (bf16[16,16,3584]{2,1,0:T(8,128)(2,1)S(1)}, bf16[16,16,3584]{2,1,0:T(8,128)(2,1)}, u32[]{:S(2)}) copy-start(bf16[16,16,3584]{2,1,0:T(8,128)(2,1)} %shard_map.91) | copy-start | bytes 5505028
  29.8 4.1 %copy-start.3 = (s32[16,8]{0,1:T(8,128)S(1)}, s32[16,8]{0,1:T(8,128)}, u32[]{:S(2)}) copy-start(s32[16,8]{0,1:T(8,128)} %param.10) | copy-start | bytes 1540
  29.8 5.9 %copy-start.2 = (bf16[16,3584]{1,0:T(8,128)(2,1)S(1)}, bf16[16,3584]{1,0:T(8,128)(2,1)}, u32[]{:S(2)}) copy-start(bf16[16,3584]{1,0:T(8,128)(2,1)} %tokens_ref.1) | copy-start | bytes 344068
  29.8 130.3 %all-to-all-start = ((bf16[16,16,3584]{2,1,0:T(8,128)(2,1)}), bf16[16,16,3584]{2,1,0:T(8,128)(2,1)S(1)}, u32[]{:S(2)}, u32[]{:S(2)}) async-start(bf16[16,16,3584]{2,1,0:T(8,128)(2,1)} %bitcast.57), calls=%async_computation | async-start | bytes 3670016 | tf_op jit(solution)/shard_map/all_to_all | solution.py:332
  142.4 4.9 %copy-start.4 = (s32[16,8]{0,1:T(8,128)S(1)}, s32[16,8]{0,1:T(8,128)}, u32[]{:S(2)}) copy-start(s32[16,8]{0,1:T(8,128)} %param.11) | copy-start | bytes 1540

commit v6 on v4

--- a/solution.py
+++ b/solution.py
@@ -133,6 +133,68 @@
     )(tokens)
 
 
+def exchange_kernel(axis, rows, send_ref, recv_ref, send_sems, recv_sems, local_sem):
+    count = lax.axis_size(axis)
+    me = lax.axis_index(axis)
+    barrier = pltpu.get_barrier_semaphore()
+
+    @pl.loop(1, count)
+    def _(step):
+        peer = lax.rem(me + step, count)
+        pl.semaphore_signal(barrier, inc=1, device_id={axis: peer}, device_id_type=MESH_ID)
+
+    pl.semaphore_wait(barrier, count - 1)
+    local = pltpu.make_async_copy(
+        send_ref.at[pl.ds(me * rows, rows)], recv_ref.at[pl.ds(me * rows, rows)], local_sem
+    )
+    local.start()
+
+    @pl.loop(1, count)
+    def _(step):
+        peer = lax.rem(me + step, count)
+        pltpu.make_async_remote_copy(
+            src_ref=send_ref.at[pl.ds(peer * rows, rows)],
+            dst_ref=recv_ref.at[pl.ds(me * rows, rows)],
+            send_sem=send_sems.at[peer],
+            recv_sem=recv_sems.at[me],
+            device_id={axis: peer},
+            device_id_type=MESH_ID,
+        ).start()
+
+    @pl.loop(1, count)
+    def _(step):
+        peer = lax.rem(me + step, count)
+        pltpu.make_async_remote_copy(
+            src_ref=send_ref.at[pl.ds(peer * rows, rows)],
+            dst_ref=recv_ref.at[pl.ds(peer * rows, rows)],
+            send_sem=send_sems.at[peer],
+            recv_sem=recv_sems.at[peer],
+            device_id={axis: peer},
+            device_id_type=MESH_ID,
+        ).wait()
+
+    local.wait()
+
+
+def exchange(send, axis, collective_id):
+    count = lax.axis_size(axis)
+    rows = send.shape[0] // count
+    return pl.pallas_call(
+        functools.partial(exchange_kernel, axis, rows),
+        out_shape=jax.ShapeDtypeStruct(send.shape, send.dtype),
+        in_specs=[pl.BlockSpec(memory_space=pl.ANY)],
+        out_specs=pl.BlockSpec(memory_space=pl.ANY),
+        scratch_shapes=[
+            pltpu.SemaphoreType.DMA((count,)),
+            pltpu.SemaphoreType.DMA((count,)),
+            pltpu.SemaphoreType.DMA(()),
+        ],
+        compiler_params=pltpu.CompilerParams(
+            collective_id=collective_id, has_side_effects=True
+        ),
+    )(send)
+
+
 def gated_mlp(inputs, gate_matrix, up_matrix, down_matrix):
     gate_part = jnp.dot(inputs, gate_matrix, preferred_element_type=jnp.float32)
     up_part = jnp.dot(inputs, up_matrix, preferred_element_type=jnp.float32)
@@ -145,38 +207,12 @@
     return 2.5 * values / jnp.sum(values, axis=-1, keepdims=True)
 
 
-def group_rank(group_ids):
-    slot_width = group_ids.shape[-1]
-    same_group = group_ids[..., :, None] == group_ids[..., None, :]
-    earlier = jnp.arange(slot_width)[None, :] < jnp.arange(slot_width)[:, None]
-    return jnp.sum(jnp.logical_and(same_group, earlier), axis=-1)
-
-
-def combine_pairs(pair_rows, pair_weights):
-    values = pair_rows.astype(jnp.float32)
-    mixed = (
-        pair_weights[..., 0, None] * values[..., 0, :]
-        + pair_weights[..., 1, None] * values[..., 1, :]
-    )
-    return mixed.astype(jnp.bfloat16)
-
-
-def rank_slots(matches):
-    named_mask = jnp.any(matches, axis=-2).astype(jnp.int32)
-    earlier = jnp.cumsum(named_mask, axis=-2) - named_mask
-    slot_ranks = jnp.sum(jnp.where(matches, earlier[..., None, :], 0), axis=-1)
-    return (named_mask, earlier, slot_ranks)
-
-
-def pair_tables(group_ids, slot_rank, slot_index, weights, group_count):
-    wanted = jnp.arange(group_count, dtype=jnp.int32)
-    in_group = group_ids[..., None, None, :] == wanted[:, None, None]
-    in_place = slot_rank[..., None, None, :] == jnp.arange(2, dtype=jnp.int32)[None, :, None]
-    picked = jnp.logical_and(in_group, in_place)
-    chosen = jnp.sum(jnp.where(picked, slot_index[..., None, None, :], 0), axis=-1)
-    present = jnp.any(picked, axis=-1)
-    pair_weights = jnp.sum(jnp.where(picked, weights[..., None, None, :], 0.0), axis=-1)
-    return (chosen, present, pair_weights)
+def weighted_rows(weights, rows):
+    high = weights.astype(jnp.bfloat16)
+    low = (weights - high.astype(jnp.float32)).astype(jnp.bfloat16)
+    return jnp.dot(high, rows, preferred_element_type=jnp.float32) + jnp.dot(
+        low, rows, preferred_element_type=jnp.float32
+    )
 
 
 def per_device(
@@ -194,53 +230,52 @@
     model_width = tokens.shape[1]
     inner_count = lax.axis_size("inner")
     outer_count = lax.axis_size("outer")
-    capacity = TOPK // TOP_GROUPS * row_count // inner_count
-    gate_matrix = expert_gate[0]
-    up_matrix = expert_up[0]
-    down_matrix = expert_down[0]
+    capacity = TOPK // TOP_GROUPS
+    me = lax.axis_index("inner")
     side = math.isqrt(inner_count)
     segment = torus_gather(tokens, side, 0).reshape(inner_count * row_count, model_width)
+    all_experts = lax.all_gather(experts, "inner", axis=0, tiled=False)
+    all_scores = lax.all_gather(gate_score, "inner", axis=0, tiled=False)
+    weights = gate_weights(all_scores)
+    local_experts = jnp.arange(outer_count, dtype=jnp.int32) * inner_count + me
+    matches = all_experts[..., None] == local_experts
+    named = jnp.any(matches, axis=2)
+    named_int = named.astype(jnp.int32)
+    earlier = jnp.cumsum(named_int, axis=1) - named_int
+    slot_ids = jnp.arange(capacity, dtype=jnp.int32)
+    placed = jnp.logical_and(named[..., None], earlier[..., None] == slot_ids)
+    same_block = jnp.eye(inner_count, dtype=jnp.bool_)
+    selector = jnp.logical_and(
+        jnp.transpose(placed, (2, 0, 3, 1))[:, :, :, None, :],
+        same_block[None, :, None, :, None],
+    ).reshape(outer_count * inner_count * capacity, inner_count * row_count)
+    outbound = jnp.dot(
+        selector.astype(jnp.bfloat16), segment, preferred_element_type=jnp.float32
+    ).astype(jnp.bfloat16)
+    received = exchange(outbound, "outer", 1)
+    answer = gated_mlp(received, expert_gate[0], expert_up[0], expert_down[0])
+    returned = exchange(answer, "outer", 2)
+    slot_weight = jnp.sum(jnp.where(matches, weights[..., None], 0.0), axis=2)
+    placed_weight = jnp.where(placed, slot_weight[..., None], 0.0)
+    combine = jnp.where(
+        same_block[:, None, None, :, None],
+        jnp.transpose(placed_weight, (0, 1, 2, 3))[:, :, :, None, :],
+        0.0,
+    ).reshape(inner_count * row_count, outer_count * inner_count * capacity)
+    routed = weighted_rows(combine, returned)
     gate_part = jnp.dot(segment, shared_gate, preferred_element_type=jnp.float32)
     up_part = jnp.dot(segment, shared_up, preferred_element_type=jnp.float32)
     shared_hidden = (jax.nn.silu(gate_part) * up_part).astype(jnp.bfloat16)
-    shared_partial = jnp.dot(
-        shared_hidden, shared_down, preferred_element_type=jnp.float32
-    ).astype(jnp.bfloat16)
-    shared_parts = lax.all_to_all(
-        shared_partial.reshape(inner_count, row_count, model_width),
+    shared = jnp.dot(shared_hidden, shared_down, preferred_element_type=jnp.float32)
+    total = (shared + routed).astype(jnp.bfloat16)
+    parts = lax.all_to_all(
+        total.reshape(inner_count, row_count, model_width),
         "inner",
         split_axis=0,
         concat_axis=0,
         tiled=True,
     )
-    shared = jnp.sum(shared_parts.astype(jnp.float32), axis=0)
-    weights = gate_weights(gate_score)
-    group_ids = experts // inner_count
-    slot_rank = group_rank(group_ids)
-    total_count = inner_count * outer_count
-    matches = experts[:, :, None] == jnp.arange(total_count, dtype=jnp.int32)[None, None, :]
-    named_mask, earlier, slot_ranks = rank_slots(matches)
-    slot_ids = jnp.arange(capacity, dtype=jnp.int32)[None, :, None]
-    selector = jnp.logical_and(
-        named_mask.T[:, None, :] == 1, earlier.T[:, None, :] == slot_ids
-    ).astype(jnp.bfloat16)
-    outbound = jnp.einsum(
-        "ecr,rd->ecd", selector, tokens, preferred_element_type=jnp.float32
-    ).astype(jnp.bfloat16)
-    received = lax.all_to_all(outbound, ("outer", "inner"), split_axis=0, concat_axis=0, tiled=True)
-    answer = gated_mlp(received.reshape(-1, model_width), gate_matrix, up_matrix, down_matrix)
-    returned = lax.all_to_all(
-        answer.reshape(received.shape), ("outer", "inner"), split_axis=0, concat_axis=0, tiled=True
-    )
-    flat_rows = returned.reshape(-1, model_width)
-    slot_index = experts * capacity + slot_ranks
-    chosen, present, pair_weights = pair_tables(
-        group_ids, slot_rank, slot_index, weights, outer_count
-    )
-    pair_rows = jnp.where(present[..., None], flat_rows[chosen], jnp.zeros((), jnp.bfloat16))
-    partial_value = combine_pairs(pair_rows, pair_weights)
-    routed = jnp.sum(partial_value.astype(jnp.float32), axis=1)
-    return (shared + routed).astype(jnp.bfloat16)
+    return jnp.sum(parts.astype(jnp.float32), axis=0).astype(jnp.bfloat16)
 
 
 def solution(mesh):

time: 154 us -> 194 us (1.26)
  blocking collectives: 0 us -> 68.6 us
  Pallas kernels: 40.2 us -> 82 us
  starting transfers between devices: 29.4 us -> 0 us
  local copies, waits for them, and re-layouts: 29.1 us -> 3.79 us
  waiting for transfers between devices: 25.3 us -> 0 us
  matrix products: 25.5 us -> 34.8 us
    pallas_call x0 -> x2, Pallas kernels: none -> 63 us  [exchange(): pl.pallas_call(functools.partial(exchange_kernel, axis, rows), out_shape=...]
    all_gather x0 -> x2, blocking collectives: none -> 38.2 us  [the longest x1 20.8 us: per_device(): all_experts = lax.all_gather(experts, 'inner', axis=0, tiled=False)]
    all_to_all x0 -> x1, blocking collectives: none -> 30.5 us  [per_device(): lax.all_to_all(total.reshape(inner_count, row_count, model_width), 'inner...]
    all_to_all x3 -> x0, starting transfers between devices: 29.4 us -> none  [the longest x1 13.2 us: per_device(): lax.all_to_all(answer.reshape(received.shape), ('outer', 'inner'), split_...]
    all_to_all x3 -> x0, waiting for transfers between devices: 25.3 us -> none  [the longest x1 25.3 us: per_device(): lax.all_to_all(answer.reshape(received.shape), ('outer', 'inner'), split_...]
    pallas_call x1, Pallas kernels: 40.2 us -> 19 us  [torus_gather(): pl.pallas_call(functools.partial(torus_gather_kernel, side), out_shape=ja...]
    reshape x3 -> x0, local copies, waits for them, and re-layouts: 13.7 us -> none  [the longest x1 4.93 us: per_device(): received.reshape(-1, model_width)]
    dot_general x1 -> x3, matrix products: 1.57 us -> 10.2 us  [the longest x1 4.36 us: weighted_rows(): jnp.dot(low, rows, preferred_element_type=jnp.float32)]
  transfers between devices with their start and end apart: 3 -> 0, of which waited for: 1 -> 0; matrix products, arithmetic and copies ran while one was open for 23% -> 0% of each run, Pallas kernels for 26% -> 0%
where the time goes in v6:
time: 194 us; the launch traced here: 193 us
  Pallas kernels  82 us (42%)
  blocking collectives  68.6 us (35%)
  matrix products  34.8 us (18%)
  local copies, waits for them, and re-layouts  3.79 us (2%)
  other arithmetic  3.76 us (2%)
    pallas_call x2, Pallas kernels, exchange(): pl.pallas_call(functools.partial(exchange_kernel, axis, rows), out_shape=...  63 us
    all_to_all x1, blocking collectives, per_device(): lax.all_to_all(total.reshape(inner_count, row_count, model_width), 'inner...  30.5 us
    all_gather x1, blocking collectives, per_device(): all_experts = lax.all_gather(experts, 'inner', axis=0, tiled=False)  20.8 us
    pallas_call x1, Pallas kernels, torus_gather(): pl.pallas_call(functools.partial(torus_gather_kernel, side), out_shape=ja...  19 us
    all_gather x1, blocking collectives, per_device(): all_scores = lax.all_gather(gate_score, 'inner', axis=0, tiled=False)  17.3 us
    dot_general x1, matrix products, gated_mlp(): jnp.dot(hidden, down_matrix, preferred_element_type=jnp.float32)  11.2 us
    dot_general x1, matrix products, gated_mlp(): gate_part = jnp.dot(inputs, gate_matrix, preferred_element_type=jnp.float32)  6.67 us
    dot_general x1, matrix products, weighted_rows(): jnp.dot(low, rows, preferred_element_type=jnp.float32)  4.36 us

profile of v6, /device:TPU:1, one launch (start us, length us, event | category | flops | bytes accessed | tf_op | source)
XLA Modules:
  0.0 193.2 jit_solution(2728923221888697166)
XLA Ops:
  0.0 0.0 copy-start
  0.0 20.8 %all-gather.2 = s32[16,16,8]{1,2,0:T(8,128)S(1)} all-gather(s32[1,16,8]{1,2,0:T(8,128)} %bitcast.48), channel_id=2, replica_groups=mesh['outer'=8,'inner'=16] {'inner'}, dimensions={0}, use_global_device_ids=true | all-gather | bytes 8704 | tf_op jit(solution)/shard_map/all_gather | solution.py:237
  20.9 0.1 compare_reduce_fusion
  21.0 0.1 copy.31
  21.2 0.1 copy.37
  21.3 17.3 %all-gather.3 = s32[16,16,8]{1,2,0:T(8,128)S(1)} all-gather(s32[1,16,8]{1,2,0:T(8,128)} %bitcast.49), channel_id=3, replica_groups=mesh['outer'=8,'inner'=16] {'inner'}, dimensions={0}, use_global_device_ids=true | all-gather | bytes 8704 | tf_op jit(solution)/shard_map/all_gather | solution.py:238
  38.6 0.4 multiply_divide_fusion
  39.0 0.2 fusion.21
  39.2 0.1 copy.36
  39.4 0.1 copy.32
  39.5 0.1 compare_and_fusion
  39.6 0.3 broadcast_and_fusion
  40.0 0.8 and.55
  40.8 19.0 %shard_map.91 = bf16[16,16,3584]{2,1,0:T(8,128)(2,1)} custom-call(bf16[16,3584]{1,0:T(8,128)(2,1)} %tokens_ref.1), custom_call_target="tpu_custom_call" | custom-call | tf_op jit(solution)/shard_map/pallas_call | solution.py:120
  59.9 0.0 copy-start.1
  59.9 2.5 %fusion.43 = f32[256,128]{1,0:T(8,128)S(1)} fusion(bf16[256,3584]{1,0:T(8,128)(2,1)} %bitcast.43, bf16[3584,128]{1,0:T(8,128)(2,1)} %param.15), kind=kOutput, calls=%fused_computation.50 | convolution fusion | flops 234881024 | bytes 2883584 | tf_op jit(solution)/shard_map/dot_general | solution.py:266
  62.4 0.0 copy-done.1
  62.4 1.9 convolution_convert_fusion.send_ref
  64.3 38.9 %shard_map.92 = bf16[256,3584]{1,0:T(8,128)(2,1)} custom-call(bf16[256,3584]{1,0:T(8,128)(2,1)} %convolution_convert_fusion.send_ref), custom_call_target="tpu_custom_call" | custom-call | tf_op jit(solution)/shard_map/pallas_call | solution.py:182
  103.2 6.7 %fusion.4 = f32[256,1024]{1,0:T(8,128)} fusion(bf16[256,3584]{1,0:T(8,128)(2,1)} %shard_map.92, bf16[1,3584,1024]{2,1,0:T(8,128)(2,1)} %param.12), kind=kOutput, calls=%fused_computation.4 | convolution fusion | flops 1879048192 | bytes 10223616 | tf_op jit(solution)/shard_map/dot_general | solution.py:199
  109.8 11.2 %fusion.7.send_ref = bf16[256,3584]{1,0:T(8,128)(2,1)} fusion(bf16[1,1024,3584]{2,1,0:T(8,128)(2,1)} %param.14, bf16[256,3584]{1,0:T(8,128)(2,1)} %shard_map.92, bf16[1,3584,1024]{2,1,0:T(8,128)(2,1)} %param.13, f32[256,1024]{1,0:T(8,128)} %fusion.4), kind=kOutput, calls=%fused_computation.8 | convolution fusion | flops 3760586752 | bytes 19398656 | tf_op jit(solution)/shard_map/dot_general | solution.py:202
  121.1 24.1 %shard_map.93 = bf16[256,3584]{1,0:T(8,128)(2,1)} custom-call(bf16[256,3584]{1,0:T(8,128)(2,1)} %fusion.7.send_ref), custom_call_target="tpu_custom_call" | custom-call | tf_op jit(solution)/shard_map/pallas_call | solution.py:182
  145.2 1.6 broadcast_select_fusion
  146.8 2.4 %select_n.23 = f32[256,256]{0,1:T(8,128)S(1)} reshape(f32[16,16,8,16,2]{1,0,4,3,2:T(8,128)} %broadcast_select_fusion) | data formatting | bytes 524288 | tf_op jit(solution)/shard_map/jit(_where)/select_n | solution.py:260
  149.3 4.0 %fusion.34 = f32[256,3584]{1,0:T(8,128)} fusion(bf16[256,3584]{1,0:T(8,128)(2,1)} %shard_map.93, f32[256,256]{0,1:T(8,128)S(1)} %select_n.23), kind=kOutput, calls=%fused_computation.39 | convolution fusion | flops 469827584 | bytes 5767168 | tf_op jit(solution)/shard_map/dot_general | solution.py:213
  153.3 0.0 copy-done
  153.3 4.2 %fusion.18 = f32[256,3584]{1,0:T(8,128)} fusion(bf16[128,3584]{1,0:T(8,128)(2,1)S(1)} %copy-done, bf16[256,3584]{1,0:T(8,128)(2,1)S(1)} %bitcast.45, bf16[3584,128]{1,0:T(8,128)(2,1)} %param.16, f32[256,128]{1,0:T(8,128)S(1)} %fusion.43), kind=kOutput, calls=%fused_computation.15 | convolution fusion | flops 469958656 | bytes 7471104 | tf_op jit(solution)/shard_map/dot_general | solution.py:269
  157.4 4.4 %fusion.10 = bf16[256,3584]{1,0:T(8,128)(2,1)S(1)} fusion(f32[256,3584]{1,0:T(8,128)} %fusion.18, f32[256,3584]{1,0:T(8,128)} %fusion.34, bf16[256,3584]{1,0:T(8,128)(2,1)} %shard_map.93, f32[256,256]{0,1:T(8,128)S(1)} %select_n.23), kind=kOutput, calls=%fused_computation.9 | convolution fusion | flops 472776704 | bytes 11272192 | tf_op jit(solution)/shard_map/dot_general | solution.py:213
  161.8 30.5 %all_to_all.5 = bf16[16,16,3584]{2,1,0:T(8,128)(2,1)S(1)} all-to-all(bf16[16,16,3584]{2,1,0:T(8,128)(2,1)S(1)} %bitcast.46), channel_id=1, replica_groups=mesh['outer'=8,'inner'=16] {'inner'}, dimensions={0} | all-to-all | bytes 3670016 | tf_op jit(solution)/shard_map/all_to_all | solution.py:271
  192.3 0.9 reduce_sum.32
  (8 shorter events, 0.1 us)
Async XLA Ops:
  0.0 153.3 %copy-start = (bf16[128,3584]{1,0:T(8,128)(2,1)S(1)}, bf16[128,3584]{1,0:T(8,128)(2,1)}, u32[]{:S(2)}) copy-start(bf16[128,3584]{1,0:T(8,128)(2,1)} %param.17) | copy-start | bytes 2752516
  59.9 2.5 %copy-start.1 = (bf16[16,16,3584]{2,1,0:T(8,128)(2,1)S(1)}, bf16[16,16,3584]{2,1,0:T(8,128)(2,1)}, u32[]{:S(2)}) copy-start(bf16[16,16,3584]{2,1,0:T(8,128)(2,1)} %shard_map.91) | copy-start | bytes 5505028

commit v7 on v6

--- a/solution.py
+++ b/solution.py
@@ -13,10 +13,13 @@
 MESH_ID = pl.DeviceIdType.MESH
 
 
-def torus_gather_kernel(side, tokens_ref, out_ref, send_sems, recv_sems, local_sems):
+def torus_gather_kernel(side, count, *refs):
+    sources = refs[:count]
+    outs = refs[count:2 * count]
+    send_sems, recv_sems, local_sems = refs[2 * count:]
     me = lax.axis_index("inner")
     z, y = me // side, me % side
-    half = tokens_ref.shape[0] // 2
+    half = sources[0].shape[0] // 2
 
     def node(zz, yy):
         return lax.rem(zz + side, side) * side + lax.rem(yy + side, side)
@@ -32,43 +35,49 @@
     pl.semaphore_wait(barrier, len(neighbours))
 
     rows = [pl.ds(0, half), pl.ds(half, half)]
-    for h in range(2):
-        pltpu.make_async_copy(
-            tokens_ref.at[rows[h]], out_ref.at[me, rows[h]], local_sems.at[h]
-        ).start()
+    local_copies = []
+    for a in range(count):
+        for h in range(2):
+            copy = pltpu.make_async_copy(
+                sources[a].at[rows[h]], outs[a].at[me, rows[h]], local_sems.at[a, h]
+            )
+            copy.start()
+            local_copies.append(copy)
 
     counter = [0]
 
     def run_round(moves):
         started = []
-        for block, h, dest, from_tokens in moves:
+        for block, h, dest, from_input in moves:
             index = counter[0]
             counter[0] += 1
-            src = tokens_ref.at[rows[h]] if from_tokens else out_ref.at[block, rows[h]]
-            copy = pltpu.make_async_remote_copy(
-                src_ref=src,
-                dst_ref=out_ref.at[block, rows[h]],
-                send_sem=send_sems.at[index],
-                recv_sem=recv_sems.at[index],
-                device_id={"inner": dest},
-                device_id_type=MESH_ID,
-            )
-            copy.start()
-            started.append(copy)
+            for a in range(count):
+                src = sources[a].at[rows[h]] if from_input else outs[a].at[block, rows[h]]
+                copy = pltpu.make_async_remote_copy(
+                    src_ref=src,
+                    dst_ref=outs[a].at[block, rows[h]],
+                    send_sem=send_sems.at[a, index],
+                    recv_sem=recv_sems.at[a, index],
+                    device_id={"inner": dest},
+                    device_id_type=MESH_ID,
+                )
+                copy.start()
+                started.append(copy)
         return started
 
     def finish(started, incoming):
         for copy in started:
             copy.wait_send()
         for index, block, h, sender in incoming:
-            pltpu.make_async_remote_copy(
-                src_ref=out_ref.at[block, rows[h]],
-                dst_ref=out_ref.at[block, rows[h]],
-                send_sem=send_sems.at[index],
-                recv_sem=recv_sems.at[index],
-                device_id={"inner": sender},
-                device_id_type=MESH_ID,
-            ).wait_recv()
+            for a in range(count):
+                pltpu.make_async_remote_copy(
+                    src_ref=outs[a].at[block, rows[h]],
+                    dst_ref=outs[a].at[block, rows[h]],
+                    send_sem=send_sems.at[a, index],
+                    recv_sem=recv_sems.at[a, index],
+                    device_id={"inner": sender},
+                    device_id_type=MESH_ID,
+                ).wait_recv()
 
     base = counter[0]
     moves, incoming = [], []
@@ -85,10 +94,8 @@
         moves.append((first(z, y, -1), h, first(z, y, 1), False))
         incoming.append((base + len(incoming), first(z, y, -2), h, first(z, y, -1)))
     finish(run_round(moves), incoming)
-    for h in range(2):
-        pltpu.make_async_copy(
-            tokens_ref.at[rows[h]], out_ref.at[me, rows[h]], local_sems.at[h]
-        ).wait()
+    for copy in local_copies:
+        copy.wait()
     base = counter[0]
     moves, incoming = [], []
     for h in range(2):
@@ -114,23 +121,26 @@
     finish(run_round(moves), incoming)
 
 
-def torus_gather(tokens, side, collective_id):
-    count = lax.axis_size("inner")
+def torus_gather(arrays, side, collective_id):
+    members = lax.axis_size("inner")
+    count = len(arrays)
     copies = 4 + 2 + 4 * side + 2 * side
     return pl.pallas_call(
-        functools.partial(torus_gather_kernel, side),
-        out_shape=jax.ShapeDtypeStruct((count,) + tokens.shape, tokens.dtype),
-        in_specs=[pl.BlockSpec(memory_space=pl.ANY)],
-        out_specs=pl.BlockSpec(memory_space=pl.ANY),
+        functools.partial(torus_gather_kernel, side, count),
+        out_shape=tuple(
+            jax.ShapeDtypeStruct((members,) + x.shape, x.dtype) for x in arrays
+        ),
+        in_specs=[pl.BlockSpec(memory_space=pl.ANY)] * count,
+        out_specs=tuple(pl.BlockSpec(memory_space=pl.ANY) for _ in arrays),
         scratch_shapes=[
-            pltpu.SemaphoreType.DMA((copies,)),
-            pltpu.SemaphoreType.DMA((copies,)),
-            pltpu.SemaphoreType.DMA((2,)),
+            pltpu.SemaphoreType.DMA((count, copies)),
+            pltpu.SemaphoreType.DMA((count, copies)),
+            pltpu.SemaphoreType.DMA((count, 2)),
         ],
         compiler_params=pltpu.CompilerParams(
             collective_id=collective_id, has_side_effects=True
         ),
-    )(tokens)
+    )(*arrays)
 
 
 def exchange_kernel(axis, rows, send_ref, recv_ref, send_sems, recv_sems, local_sem):
@@ -233,9 +243,12 @@
     capacity = TOPK // TOP_GROUPS
     me = lax.axis_index("inner")
     side = math.isqrt(inner_count)
-    segment = torus_gather(tokens, side, 0).reshape(inner_count * row_count, model_width)
-    all_experts = lax.all_gather(experts, "inner", axis=0, tiled=False)
-    all_scores = lax.all_gather(gate_score, "inner", axis=0, tiled=False)
+    routing = jnp.concatenate([experts, gate_score], axis=1).astype(jnp.bfloat16)
+    routing = jnp.pad(routing, ((0, 0), (0, 128 - routing.shape[1])))
+    gathered, gathered_routing = torus_gather([tokens, routing], side, 0)
+    segment = gathered.reshape(inner_count * row_count, model_width)
+    all_experts = gathered_routing[:, :, :TOPK].astype(jnp.int32)
+    all_scores = gathered_routing[:, :, TOPK:2 * TOPK].astype(jnp.int32)
     weights = gate_weights(all_scores)
     local_experts = jnp.arange(outer_count, dtype=jnp.int32) * inner_count + me
     matches = all_experts[..., None] == local_experts

time: 194 us -> 155 us (0.80)
  blocking collectives: 68.6 us -> 30.8 us
  Pallas kernels: 82 us -> 76.8 us
  other arithmetic: 3.76 us -> 8.46 us
    all_gather x2 -> x0, blocking collectives: 38.2 us -> none  [the longest x1 20.8 us: per_device(): all_experts = lax.all_gather(experts, 'inner', axis=0, tiled=False)]
    pallas_call x2, Pallas kernels: 63 us -> 51.9 us  [exchange(): pl.pallas_call(functools.partial(exchange_kernel, axis, rows), out_shape=...]
    pallas_call x1, Pallas kernels: 19 us -> 24.9 us  [torus_gather(): pl.pallas_call(functools.partial(torus_gather_kernel, side, count), out_s...]
where the time goes in v7:
time: 155 us
  Pallas kernels  76.8 us (50%)
  matrix products  34.1 us (22%)
  blocking collectives  30.8 us (20%)
  other arithmetic  8.46 us (5%)
  local copies, waits for them, and re-layouts  4.12 us (3%)
    pallas_call x2, Pallas kernels, exchange(): pl.pallas_call(functools.partial(exchange_kernel, axis, rows), out_shape=...  51.9 us
    all_to_all x1, blocking collectives, per_device(): lax.all_to_all(total.reshape(inner_count, row_count, model_width), 'inner...  30.8 us
    pallas_call x1, Pallas kernels, torus_gather(): pl.pallas_call(functools.partial(torus_gather_kernel, side, count), out_s...  24.9 us
    dot_general x1, matrix products, gated_mlp(): jnp.dot(hidden, down_matrix, preferred_element_type=jnp.float32)  11.2 us
    dot_general x1, matrix products, gated_mlp(): gate_part = jnp.dot(inputs, gate_matrix, preferred_element_type=jnp.float32)  6.67 us
    dot_general x1, matrix products, weighted_rows(): jnp.dot(low, rows, preferred_element_type=jnp.float32)  4.36 us
    dot_general x1, matrix products, per_device(): jnp.dot(shared_hidden, shared_down, preferred_element_type=jnp.float32)  4.16 us
    dot_general x1, matrix products, weighted_rows(): jnp.dot(high, rows, preferred_element_type=jnp.float32)  4 us

profile of v7, /device:TPU:1, one launch (start us, length us, event | category | flops | bytes accessed | tf_op | source)
XLA Modules:
  0.0 154.5 jit_solution(7382266199745036136)
XLA Ops:
  0.0 0.0 copy-start
  0.0 0.8 convert.7
  0.8 0.1 copy.35
  0.9 0.7 convert.8
  1.6 0.1 copy.36
  1.6 0.7 fusion.38.refs_1_
  2.3 24.9 %shard_map.91 = (bf16[16,16,3584]{2,1,0:T(8,128)(2,1)}, bf16[16,16,128]{2,1,0:T(8,128)(2,1)}) custom-call(bf16[16,3584]{1,0:T(8,128)(2,1)} %refs_0_.1, bf16[16,128]{1,0:T(8,128)(2,1)} %fusion.38.refs_1_), custom_call_target="tpu_custom_call" | custom-call | tf_op jit(solution)/shard_map/pallas_call | solution.py:128
  27.2 1.0 convert_reduce_fusion
  28.3 0.0 copy-start.1
  28.3 1.0 slice_convert_fusion
  29.3 0.1 copy.37
  29.4 0.2 compare_reduce_fusion
  29.5 0.1 copy.39
  29.7 0.1 copy.46
  29.8 1.0 multiply_divide_fusion
  30.8 0.1 copy.41
  30.8 0.2 fusion.21
  31.1 0.1 copy.45
  31.2 0.1 copy.40
  31.3 0.1 compare_and_fusion
  31.4 0.3 broadcast_and_fusion
  31.8 0.8 and.55
  32.6 0.0 copy-done.1
  32.7 1.8 %fusion.41 = f32[256,128]{1,0:T(8,128)S(1)} fusion(bf16[256,3584]{1,0:T(8,128)(2,1)S(1)} %bitcast.41, bf16[3584,128]{1,0:T(8,128)(2,1)} %param.15), kind=kOutput, calls=%fused_computation.51 | convolution fusion | flops 234881024 | bytes 2883584 | tf_op jit(solution)/shard_map/dot_general | solution.py:279
  34.5 1.9 %convolution_convert_fusion.send_ref = bf16[256,3584]{1,0:T(8,128)(2,1)} fusion(pred[256,256]{1,0:T(32,128)(4,1)S(1)} %and.55, bf16[256,3584]{1,0:T(8,128)(2,1)S(1)} %bitcast.42), kind=kOutput, calls=%fused_computation.10 | convolution fusion | flops 470679552 | bytes 3735552 | tf_op jit(solution)/shard_map/dot_general | solution.py:265
  36.3 27.8 %shard_map.92 = bf16[256,3584]{1,0:T(8,128)(2,1)} custom-call(bf16[256,3584]{1,0:T(8,128)(2,1)} %convolution_convert_fusion.send_ref), custom_call_target="tpu_custom_call" | custom-call | tf_op jit(solution)/shard_map/pallas_call | solution.py:192
  64.2 6.7 %fusion.4 = f32[256,1024]{1,0:T(8,128)} fusion(bf16[256,3584]{1,0:T(8,128)(2,1)} %shard_map.92, bf16[1,3584,1024]{2,1,0:T(8,128)(2,1)} %param.12), kind=kOutput, calls=%fused_computation.4 | convolution fusion | flops 1879048192 | bytes 10223616 | tf_op jit(solution)/shard_map/dot_general | solution.py:209
  70.8 11.2 %fusion.7.send_ref = bf16[256,3584]{1,0:T(8,128)(2,1)} fusion(bf16[1,1024,3584]{2,1,0:T(8,128)(2,1)} %param.14, bf16[256,3584]{1,0:T(8,128)(2,1)} %shard_map.92, bf16[1,3584,1024]{2,1,0:T(8,128)(2,1)} %param.13, f32[256,1024]{1,0:T(8,128)} %fusion.4), kind=kOutput, calls=%fused_computation.8 | convolution fusion | flops 3760586752 | bytes 19398656 | tf_op jit(solution)/shard_map/dot_general | solution.py:212
  82.1 24.1 %shard_map.93 = bf16[256,3584]{1,0:T(8,128)(2,1)} custom-call(bf16[256,3584]{1,0:T(8,128)(2,1)} %fusion.7.send_ref), custom_call_target="tpu_custom_call" | custom-call | tf_op jit(solution)/shard_map/pallas_call | solution.py:192
  106.2 1.6 %broadcast_select_fusion = f32[16,16,8,16,2]{1,0,4,3,2:T(8,128)} fusion(f32[16,16,8,2]{1,0,3,2:T(8,128)S(1)} %fusion.31, pred[16,16]{0,1:T(8,128)(4,1)S(1)} %iota_compare_fusion.2), kind=kLoop, calls=%fused_computation.16 | loop fusion | flops 65536 | bytes 278784 | tf_op jit(solution)/shard_map/jit(_where)/select_n | solution.py:273
  107.8 2.4 %select_n.23 = f32[256,256]{0,1:T(8,128)S(1)} reshape(f32[16,16,8,16,2]{1,0,4,3,2:T(8,128)} %broadcast_select_fusion) | data formatting | bytes 524288 | tf_op jit(solution)/shard_map/jit(_where)/select_n | solution.py:273
  110.3 4.0 %fusion.33 = f32[256,3584]{1,0:T(8,128)} fusion(bf16[256,3584]{1,0:T(8,128)(2,1)} %shard_map.93, f32[256,256]{0,1:T(8,128)S(1)} %select_n.23), kind=kOutput, calls=%fused_computation.39 | convolution fusion | flops 469827584 | bytes 5767168 | tf_op jit(solution)/shard_map/dot_general | solution.py:223
  114.3 0.0 copy-done
  114.3 4.2 %fusion.18 = f32[256,3584]{1,0:T(8,128)} fusion(bf16[128,3584]{1,0:T(8,128)(2,1)S(1)} %copy-done, bf16[256,3584]{1,0:T(8,128)(2,1)S(1)} %bitcast.43, bf16[3584,128]{1,0:T(8,128)(2,1)} %param.16, f32[256,128]{1,0:T(8,128)S(1)} %fusion.41), kind=kOutput, calls=%fused_computation.15 | convolution fusion | flops 469958656 | bytes 7471104 | tf_op jit(solution)/shard_map/dot_general | solution.py:282
  118.4 4.4 %fusion.10 = bf16[256,3584]{1,0:T(8,128)(2,1)S(1)} fusion(f32[256,3584]{1,0:T(8,128)} %fusion.18, f32[256,3584]{1,0:T(8,128)} %fusion.33, bf16[256,3584]{1,0:T(8,128)(2,1)} %shard_map.93, f32[256,256]{0,1:T(8,128)S(1)} %select_n.23), kind=kOutput, calls=%fused_computation.9 | convolution fusion | flops 472776704 | bytes 11272192 | tf_op jit(solution)/shard_map/dot_general | solution.py:223
  122.8 30.8 %all_to_all.5 = bf16[16,16,3584]{2,1,0:T(8,128)(2,1)S(1)} all-to-all(bf16[16,16,3584]{2,1,0:T(8,128)(2,1)S(1)} %bitcast.44), channel_id=1, replica_groups=mesh['outer'=8,'inner'=16] {'inner'}, dimensions={0} | all-to-all | bytes 3670016 | tf_op jit(solution)/shard_map/all_to_all | solution.py:284
  153.6 0.9 reduce_sum.32
  (8 shorter events, 0.1 us)
Async XLA Ops:
  0.0 114.3 %copy-start = (bf16[128,3584]{1,0:T(8,128)(2,1)S(1)}, bf16[128,3584]{1,0:T(8,128)(2,1)}, u32[]{:S(2)}) copy-start(bf16[128,3584]{1,0:T(8,128)(2,1)} %param.17) | copy-start | bytes 2752516
  28.3 4.4 %copy-start.1 = (bf16[16,16,3584]{2,1,0:T(8,128)(2,1)S(1)}, bf16[16,16,3584]{2,1,0:T(8,128)(2,1)}, u32[]{:S(2)}) copy-start(bf16[16,16,3584]{2,1,0:T(8,128)(2,1)} %get-tuple-element.7) | copy-start | bytes 5505028

commit v8 on v7

--- a/solution.py
+++ b/solution.py
@@ -141,6 +141,135 @@
             collective_id=collective_id, has_side_effects=True
         ),
     )(*arrays)
+
+
+def torus_reduce_kernel(side, x_ref, out_ref, recv_a, recv_bp, recv_bm, send_b, partial,
+                        send_a2, recv_a2, send_b2, send_c2, recv_b2p, recv_b2m,
+                        send_sems, recv_sems):
+    me = lax.axis_index("inner")
+    z, y = me // side, me % side
+    half = x_ref.shape[1] // 2
+    rows = [pl.ds(0, half), pl.ds(half, half)]
+
+    def node(zz, yy):
+        return lax.rem(zz + side, side) * side + lax.rem(yy + side, side)
+
+    def wrap(p):
+        return lax.rem(p + side, side)
+
+    plans = [
+        (lambda k: node(z + k, y), lambda k: node(z, y + k), z, y,
+         lambda pos, j: pos * side + j),
+        (lambda k: node(z, y + k), lambda k: node(z + k, y), y, z,
+         lambda pos, j: j * side + pos),
+    ]
+    neighbours = [node(z, y + 1), node(z, y - 1), node(z + 1, y), node(z - 1, y)]
+    barrier = pltpu.get_barrier_semaphore()
+    for peer in neighbours:
+        pl.semaphore_signal(barrier, inc=1, device_id={"inner": peer}, device_id_type=MESH_ID)
+    pl.semaphore_wait(barrier, len(neighbours))
+
+    counter = [0]
+
+    def send(src, dst, dest):
+        index = counter[0]
+        counter[0] += 1
+        copy = pltpu.make_async_remote_copy(
+            src_ref=src, dst_ref=dst, send_sem=send_sems.at[index],
+            recv_sem=recv_sems.at[index], device_id={"inner": dest},
+            device_id_type=MESH_ID,
+        )
+        copy.start()
+        return copy, (index, dst, src)
+
+    def settle(sent, senders):
+        for copy, _ in sent:
+            copy.wait_send()
+        for (_, (index, dst, src)), sender in zip(sent, senders):
+            pltpu.make_async_remote_copy(
+                src_ref=src, dst_ref=dst, send_sem=send_sems.at[index],
+                recv_sem=recv_sems.at[index], device_id={"inner": sender},
+                device_id_type=MESH_ID,
+            ).wait_recv()
+
+    sent, senders = [], []
+    for h, (ring1, ring2, p1, p2, block) in enumerate(plans):
+        for j in range(side):
+            sent.append(send(x_ref.at[block(wrap(p1 + 2), j), rows[h]], recv_a.at[h, j], ring1(1)))
+            senders.append(ring1(-1))
+    settle(sent, senders)
+    sent, senders = [], []
+    for h, (ring1, ring2, p1, p2, block) in enumerate(plans):
+        for j in range(side):
+            mine = x_ref[block(wrap(p1 + 1), j), rows[h], :].astype(jnp.float32)
+            send_b[h, j] = (mine + recv_a[h, j].astype(jnp.float32)).astype(send_b.dtype)
+        for j in range(side):
+            sent.append(send(send_b.at[h, j], recv_bp.at[h, j], ring1(1)))
+            senders.append(ring1(-1))
+            sent.append(send(x_ref.at[block(wrap(p1 - 1), j), rows[h]], recv_bm.at[h, j], ring1(-1)))
+            senders.append(ring1(1))
+    settle(sent, senders)
+    for h, (ring1, ring2, p1, p2, block) in enumerate(plans):
+        for j in range(side):
+            partial[h, j] = (
+                x_ref[block(p1, j), rows[h], :].astype(jnp.float32)
+                + recv_bp[h, j].astype(jnp.float32)
+                + recv_bm[h, j].astype(jnp.float32)
+            )
+    sent, senders = [], []
+    for h, (ring1, ring2, p1, p2, block) in enumerate(plans):
+        send_a2[h] = partial[h, wrap(p2 + 2)].astype(send_a2.dtype)
+        sent.append(send(send_a2.at[h], recv_a2.at[h], ring2(1)))
+        senders.append(ring2(-1))
+    settle(sent, senders)
+    sent, senders = [], []
+    for h, (ring1, ring2, p1, p2, block) in enumerate(plans):
+        send_b2[h] = (partial[h, wrap(p2 + 1)] + recv_a2[h].astype(jnp.float32)).astype(send_b2.dtype)
+        send_c2[h] = partial[h, wrap(p2 - 1)].astype(send_c2.dtype)
+        sent.append(send(send_b2.at[h], recv_b2p.at[h], ring2(1)))
+        senders.append(ring2(-1))
+        sent.append(send(send_c2.at[h], recv_b2m.at[h], ring2(-1)))
+        senders.append(ring2(1))
+    settle(sent, senders)
+    for h, (ring1, ring2, p1, p2, block) in enumerate(plans):
+        out_ref[rows[h], :] = (
+            partial[h, p2]
+            + recv_b2p[h].astype(jnp.float32)
+            + recv_b2m[h].astype(jnp.float32)
+        ).astype(out_ref.dtype)
+
+
+def torus_reduce(parts, side, collective_id):
+    _, row_count, width = parts.shape
+    half = row_count // 2
+    piece = (2, side, half, width)
+    one = (2, half, width)
+    copies = 2 * side + 4 * side + 2 + 4
+    vmem = pltpu.VMEM
+    return pl.pallas_call(
+        functools.partial(torus_reduce_kernel, side),
+        out_shape=jax.ShapeDtypeStruct((row_count, width), jnp.bfloat16),
+        in_specs=[pl.BlockSpec(memory_space=vmem)],
+        out_specs=pl.BlockSpec(memory_space=vmem),
+        scratch_shapes=[
+            vmem(piece, parts.dtype),
+            vmem(piece, parts.dtype),
+            vmem(piece, parts.dtype),
+            vmem(piece, parts.dtype),
+            vmem(piece, jnp.float32),
+            vmem(one, parts.dtype),
+            vmem(one, parts.dtype),
+            vmem(one, parts.dtype),
+            vmem(one, parts.dtype),
+            vmem(one, parts.dtype),
+            vmem(one, parts.dtype),
+            pltpu.SemaphoreType.DMA((copies,)),
+            pltpu.SemaphoreType.DMA((copies,)),
+        ],
+        compiler_params=pltpu.CompilerParams(
+            collective_id=collective_id, has_side_effects=True
+        ),
+    )(parts)
 
 
 def exchange_kernel(axis, rows, send_ref, recv_ref, send_sems, recv_sems, local_sem):
@@ -281,14 +410,7 @@
     shared_hidden = (jax.nn.silu(gate_part) * up_part).astype(jnp.bfloat16)
     shared = jnp.dot(shared_hidden, shared_down, preferred_element_type=jnp.float32)
     total = (shared + routed).astype(jnp.bfloat16)
-    parts = lax.all_to_all(
-        total.reshape(inner_count, row_count, model_width),
-        "inner",
-        split_axis=0,
-        concat_axis=0,
-        tiled=True,
-    )
-    return jnp.sum(parts.astype(jnp.float32), axis=0).astype(jnp.bfloat16)
+    return torus_reduce(total.reshape(inner_count, row_count, model_width), side, 3)
 
 
 def solution(mesh):

time: 155 us -> 150 us (0.968)
  blocking collectives: 30.8 us -> 0 us
  Pallas kernels: 76.8 us -> 102 us
  matrix products: 34.1 us -> 29.6 us
  local copies, waits for them, and re-layouts: 4.12 us -> 7.68 us
    all_to_all x1 -> x0, blocking collectives: 30.8 us -> none  [per_device(): lax.all_to_all(total.reshape(inner_count, row_count, model_width), 'inner...]
    pallas_call x0 -> x1, Pallas kernels: none -> 24.9 us  [torus_reduce(): pl.pallas_call(functools.partial(torus_reduce_kernel, side), out_shape=ja...]
    dot_general x1, matrix products: 4 us -> 0.66 us  [weighted_rows(): jnp.dot(high, rows, preferred_element_type=jnp.float32)]
    unnamed x4 -> x11, local copies, waits for them, and re-layouts: 0.01 us -> 2.94 us
    dot_general x1, matrix products: 4.36 us -> 2.02 us  [weighted_rows(): jnp.dot(low, rows, preferred_element_type=jnp.float32)]
where the time goes in v8:
time: 150 us; the launch traced here: 148 us
  Pallas kernels  102 us (68%)
  matrix products  29.6 us (20%)
  other arithmetic  8.96 us (6%)
  local copies, waits for them, and re-layouts  7.68 us (5%)
    pallas_call x2, Pallas kernels, exchange(): pl.pallas_call(functools.partial(exchange_kernel, axis, rows), out_shape=...  51.9 us
    pallas_call x1, Pallas kernels, torus_gather(): pl.pallas_call(functools.partial(torus_gather_kernel, side, count), out_s...  24.9 us
    pallas_call x1, Pallas kernels, torus_reduce(): pl.pallas_call(functools.partial(torus_reduce_kernel, side), out_shape=ja...  24.9 us
    dot_general x1, matrix products, gated_mlp(): jnp.dot(hidden, down_matrix, preferred_element_type=jnp.float32)  11.2 us
    dot_general x1, matrix products, gated_mlp(): gate_part = jnp.dot(inputs, gate_matrix, preferred_element_type=jnp.float32)  6.67 us
    dot_general x1, matrix products, per_device(): jnp.dot(shared_hidden, shared_down, preferred_element_type=jnp.float32)  4.16 us

profile of v8, /device:TPU:1, one launch (start us, length us, event | category | flops | bytes accessed | tf_op | source)
XLA Modules:
  0.0 148.1 jit_solution(6936500711977450421)
XLA Ops:
  0.0 0.0 copy-start
  0.0 0.0 copy-start.4
  0.0 0.1 copy.46
  0.1 0.8 convert.6
  0.9 0.1 copy.35
  1.0 0.7 convert.7
  1.7 0.1 copy.36
  1.8 0.7 fusion.38.refs_1_
  2.5 24.9 %shard_map.91 = (bf16[16,16,3584]{2,1,0:T(8,128)(2,1)}, bf16[16,16,128]{2,1,0:T(8,128)(2,1)}) custom-call(bf16[16,3584]{1,0:T(8,128)(2,1)} %refs_0_.1, bf16[16,128]{1,0:T(8,128)(2,1)} %fusion.38.refs_1_), custom_call_target="tpu_custom_call" | custom-call | tf_op jit(solution)/shard_map/pallas_call | solution.py:128
  27.4 1.0 convert_reduce_fusion
  28.4 1.0 multiply_divide_fusion
  29.4 0.1 copy.41
  29.5 0.9 slice_convert_fusion
  30.4 0.1 copy.37
  30.4 0.2 fusion.21
  30.6 0.1 compare_reduce_fusion
  30.8 0.1 copy.39
  31.0 0.0 copy-done.4
  31.0 2.1 %fusion.41 = f32[256,128]{1,0:T(8,128)S(1)} fusion(bf16[256,3584]{1,0:T(8,128)(2,1)} %bitcast.41, bf16[3584,128]{1,0:T(8,128)(2,1)S(1)} %copy-done.4), kind=kOutput, calls=%fused_computation.51 | convolution fusion | flops 234881024 | bytes 2883584 | tf_op jit(solution)/shard_map/dot_general | solution.py:408
  33.1 0.0 copy-start.1
  33.1 0.1 copy.45
  33.3 0.7 compare_and_fusion
  34.0 0.1 copy.40
  34.2 1.2 broadcast_and_fusion
  35.4 1.5 and.55
  36.8 0.0 copy-done.1
  36.8 2.7 %convolution_convert_fusion.send_ref = bf16[256,3584]{1,0:T(8,128)(2,1)} fusion(pred[256,256]{1,0:T(32,128)(4,1)} %and.55, bf16[256,3584]{1,0:T(8,128)(2,1)S(1)} %bitcast.42), kind=kOutput, calls=%fused_computation.10 | convolution fusion | flops 470679552 | bytes 3735552 | tf_op jit(solution)/shard_map/dot_general | solution.py:394
  39.6 27.8 %shard_map.92 = bf16[256,3584]{1,0:T(8,128)(2,1)} custom-call(bf16[256,3584]{1,0:T(8,128)(2,1)} %convolution_convert_fusion.send_ref), custom_call_target="tpu_custom_call" | custom-call | tf_op jit(solution)/shard_map/pallas_call | solution.py:321
  67.4 6.7 %fusion.4 = f32[256,1024]{1,0:T(8,128)} fusion(bf16[256,3584]{1,0:T(8,128)(2,1)} %shard_map.92, bf16[1,3584,1024]{2,1,0:T(8,128)(2,1)} %param.12), kind=kOutput, calls=%fused_computation.4 | convolution fusion | flops 1879048192 | bytes 10223616 | tf_op jit(solution)/shard_map/dot_general | solution.py:338
  74.0 11.2 %fusion.7.send_ref = bf16[256,3584]{1,0:T(8,128)(2,1)} fusion(bf16[1,1024,3584]{2,1,0:T(8,128)(2,1)} %param.14, bf16[256,3584]{1,0:T(8,128)(2,1)} %shard_map.92, bf16[1,3584,1024]{2,1,0:T(8,128)(2,1)} %param.13, f32[256,1024]{1,0:T(8,128)} %fusion.4), kind=kOutput, calls=%fused_computation.8 | convolution fusion | flops 3760586752 | bytes 19398656 | tf_op jit(solution)/shard_map/dot_general | solution.py:341
  85.3 24.1 %shard_map.93 = bf16[256,3584]{1,0:T(8,128)(2,1)} custom-call(bf16[256,3584]{1,0:T(8,128)(2,1)} %fusion.7.send_ref), custom_call_target="tpu_custom_call" | custom-call | tf_op jit(solution)/shard_map/pallas_call | solution.py:321
  109.4 0.0 copy-done
  109.4 4.2 %fusion.18 = f32[256,3584]{1,0:T(8,128)} fusion(bf16[128,3584]{1,0:T(8,128)(2,1)S(1)} %copy-done, bf16[256,3584]{1,0:T(8,128)(2,1)S(1)} %bitcast.43, bf16[3584,128]{1,0:T(8,128)(2,1)} %param.16, f32[256,128]{1,0:T(8,128)S(1)} %fusion.41), kind=kOutput, calls=%fused_computation.15 | convolution fusion | flops 469958656 | bytes 7471104 | tf_op jit(solution)/shard_map/dot_general | solution.py:411
  113.6 0.0 copy-start.2
  113.6 1.6 %broadcast_select_fusion = f32[16,16,8,16,2]{1,0,4,3,2:T(8,128)} fusion(f32[16,16,8,2]{1,0,3,2:T(8,128)S(1)} %fusion.31, pred[16,16]{0,1:T(8,128)(4,1)S(1)} %iota_compare_fusion.2), kind=kLoop, calls=%fused_computation.16 | loop fusion | flops 65536 | bytes 278784 | tf_op jit(solution)/shard_map/jit(_where)/select_n | solution.py:402
  115.2 2.4 %select_n.23 = f32[256,256]{0,1:T(8,128)S(1)} reshape(f32[16,16,8,16,2]{1,0,4,3,2:T(8,128)} %broadcast_select_fusion) | data formatting | bytes 524288 | tf_op jit(solution)/shard_map/jit(_where)/select_n | solution.py:402
  117.6 0.0 copy-done.2
  117.6 0.0 copy-start.3
  117.6 0.7 fusion.33
  118.3 1.4 copy-done.3
  119.7 2.0 %fusion.10 = bf16[256,3584]{1,0:T(8,128)(2,1)} fusion(f32[256,3584]{1,0:T(8,128)S(1)} %copy-done.3, f32[256,3584]{1,0:T(8,128)S(1)} %fusion.33, bf16[256,3584]{1,0:T(8,128)(2,1)S(1)} %copy-done.2, f32[256,256]{0,1:T(8,128)S(1)} %select_n.23), kind=kOutput, calls=%fused_computation.9 | convolution fusion | flops 472776704 | bytes 11272192 | tf_op jit(solution)/shard_map/dot_general | solution.py:352
  121.7 24.9 %shard_map.94 = bf16[16,3584]{1,0:T(8,128)(2,1)} custom-call(bf16[16,16,3584]{2,1,0:T(8,128)(2,1)} %bitcast.44), custom_call_target="tpu_custom_call" | custom-call | tf_op jit(solution)/shard_map/pallas_call | solution.py:249
  146.5 1.6 %copy.50 = bf16[16,3584]{1,0:T(8,128)(2,1)} copy(bf16[16,3584]{1,0:T(8,128)(2,1)} %shard_map.94) | data formatting | bytes 229376
  (8 shorter events, 0.1 us)
Async XLA Ops:
  0.0 109.4 %copy-start = (bf16[128,3584]{1,0:T(8,128)(2,1)S(1)}, bf16[128,3584]{1,0:T(8,128)(2,1)}, u32[]{:S(2)}) copy-start(bf16[128,3584]{1,0:T(8,128)(2,1)} %param.17) | copy-start | bytes 2752516
  0.0 31.0 %copy-start.4 = (bf16[3584,128]{1,0:T(8,128)(2,1)S(1)}, bf16[3584,128]{1,0:T(8,128)(2,1)}, u32[]{:S(2)}) copy-start(bf16[3584,128]{1,0:T(8,128)(2,1)} %param.15) | copy-start | bytes 2752516
  33.1 3.7 %copy-start.1 = (bf16[16,16,3584]{2,1,0:T(8,128)(2,1)S(1)}, bf16[16,16,3584]{2,1,0:T(8,128)(2,1)}, u32[]{:S(2)}) copy-start(bf16[16,16,3584]{2,1,0:T(8,128)(2,1)} %get-tuple-element.7) | copy-start | bytes 5505028
  113.6 4.0 %copy-start.2 = (bf16[256,3584]{1,0:T(8,128)(2,1)S(1)}, bf16[256,3584]{1,0:T(8,128)(2,1)}, u32[]{:S(2)}) copy-start(bf16[256,3584]{1,0:T(8,128)(2,1)} %shard_map.93) | copy-start | bytes 5505028
  117.6 2.0 %copy-start.3 = (f32[256,3584]{1,0:T(8,128)S(1)}, f32[256,3584]{1,0:T(8,128)}, u32[]{:S(2)}) copy-start(f32[256,3584]{1,0:T(8,128)} %fusion.18) | copy-start | bytes 11010052

commit v9 on v8

--- a/solution.py
+++ b/solution.py
@@ -334,6 +334,104 @@
     )(send)
 
 
+def dispatch_expert_kernel(axis, rows, tile, send_ref, gate_hbm, up_hbm, down_hbm, out_ref,
+                           recv, gate_w, up_w, down_w, hidden, send_sems, recv_sems,
+                           local_sems):
+    count = lax.axis_size(axis)
+    me = lax.axis_index(axis)
+    weights = [
+        pltpu.make_async_copy(gate_hbm.at[0], gate_w, local_sems.at[0]),
+        pltpu.make_async_copy(up_hbm.at[0], up_w, local_sems.at[1]),
+        pltpu.make_async_copy(down_hbm.at[0], down_w, local_sems.at[2]),
+    ]
+    for copy in weights:
+        copy.start()
+    barrier = pltpu.get_barrier_semaphore()
+
+    @pl.loop(1, count)
+    def _(step):
+        peer = lax.rem(me + step, count)
+        pl.semaphore_signal(barrier, inc=1, device_id={axis: peer}, device_id_type=MESH_ID)
+
+    pl.semaphore_wait(barrier, count - 1)
+    local = pltpu.make_async_copy(
+        send_ref.at[pl.ds(me * rows, rows)], recv.at[pl.ds(me * rows, rows)], local_sems.at[3]
+    )
+    local.start()
+
+    @pl.loop(1, count)
+    def _(step):
+        peer = lax.rem(me + step, count)
+        pltpu.make_async_remote_copy(
+            src_ref=send_ref.at[pl.ds(peer * rows, rows)],
+            dst_ref=recv.at[pl.ds(me * rows, rows)],
+            send_sem=send_sems.at[peer],
+            recv_sem=recv_sems.at[me],
+            device_id={axis: peer},
+            device_id_type=MESH_ID,
+        ).start()
+
+    @pl.loop(1, count)
+    def _(step):
+        peer = lax.rem(me + step, count)
+        pltpu.make_async_remote_copy(
+            src_ref=send_ref.at[pl.ds(peer * rows, rows)],
+            dst_ref=recv.at[pl.ds(peer * rows, rows)],
+            send_sem=send_sems.at[peer],
+            recv_sem=recv_sems.at[peer],
+            device_id={axis: peer},
+            device_id_type=MESH_ID,
+        ).wait()
+
+    local.wait()
+    weights[0].wait()
+    weights[1].wait()
+
+    @pl.loop(0, gate_w.shape[1] // tile)
+    def _(t):
+        cols = pl.ds(pl.multiple_of(t * tile, tile), tile)
+        tokens = recv[...]
+        gate_part = jnp.dot(tokens, gate_w[:, cols], preferred_element_type=jnp.float32)
+        up_part = jnp.dot(tokens, up_w[:, cols], preferred_element_type=jnp.float32)
+        hidden[:, cols] = (gate_part / (1.0 + jnp.exp(-gate_part)) * up_part).astype(hidden.dtype)
+
+    weights[2].wait()
+
+    @pl.loop(0, down_w.shape[1] // (2 * tile))
+    def _(t):
+        cols = pl.ds(pl.multiple_of(t * 2 * tile, 2 * tile), 2 * tile)
+        out_ref[:, cols] = jnp.dot(
+            hidden[...], down_w[:, cols], preferred_element_type=jnp.float32
+        ).astype(out_ref.dtype)
+
+
+def dispatch_expert(send, gate, up, down, axis, collective_id):
+    count = lax.axis_size(axis)
+    rows = send.shape[0] // count
+    width = gate.shape[2]
+    any_space = pl.BlockSpec(memory_space=pl.ANY)
+    return pl.pallas_call(
+        functools.partial(dispatch_expert_kernel, axis, rows, 256),
+        out_shape=jax.ShapeDtypeStruct(send.shape, send.dtype),
+        in_specs=[any_space] * 4,
+        out_specs=pl.BlockSpec(memory_space=pltpu.VMEM),
+        scratch_shapes=[
+            pltpu.VMEM(send.shape, send.dtype),
+            pltpu.VMEM(gate.shape[1:], gate.dtype),
+            pltpu.VMEM(up.shape[1:], up.dtype),
+            pltpu.VMEM(down.shape[1:], down.dtype),
+            pltpu.VMEM((send.shape[0], width), jnp.bfloat16),
+            pltpu.SemaphoreType.DMA((count,)),
+            pltpu.SemaphoreType.DMA((count,)),
+            pltpu.SemaphoreType.DMA((4,)),
+        ],
+        compiler_params=pltpu.CompilerParams(
+            collective_id=collective_id, has_side_effects=True,
+            vmem_limit_bytes=56 * 1024 * 1024,
+        ),
+    )(send, gate, up, down)
+
+
 def gated_mlp(inputs, gate_matrix, up_matrix, down_matrix):
     gate_part = jnp.dot(inputs, gate_matrix, preferred_element_type=jnp.float32)
     up_part = jnp.dot(inputs, up_matrix, preferred_element_type=jnp.float32)
@@ -394,8 +492,7 @@
     outbound = jnp.dot(
         selector.astype(jnp.bfloat16), segment, preferred_element_type=jnp.float32
     ).astype(jnp.bfloat16)
-    received = exchange(outbound, "outer", 1)
-    answer = gated_mlp(received, expert_gate[0], expert_up[0], expert_down[0])
+    answer = dispatch_expert(outbound, expert_gate, expert_up, expert_down, "outer", 1)
     returned = exchange(answer, "outer", 2)
     slot_weight = jnp.sum(jnp.where(matches, weights[..., None], 0.0), axis=2)
     placed_weight = jnp.where(placed, slot_weight[..., None], 0.0)

time: 150 us -> 141 us (0.940)
  matrix products: 29.6 us -> 11.7 us
  Pallas kernels: 102 us -> 111 us
    pallas_call x0 -> x1, Pallas kernels: none -> 36.7 us  [dispatch_expert(): pl.pallas_call(functools.partial(dispatch_expert_kernel, axis, rows, 256)...]
    pallas_call x2 -> x1, Pallas kernels: 51.9 us -> 24.2 us  [exchange(): pl.pallas_call(functools.partial(exchange_kernel, axis, rows), out_shape=...]
    dot_general x2 -> x0, matrix products: 17.9 us -> none  [the longest x1 11.2 us: gated_mlp(): jnp.dot(hidden, down_matrix, preferred_element_type=jnp.float32)]
where the time goes in v9:
time: 141 us; the launch traced here: 139 us
  Pallas kernels  111 us (79%)
  matrix products  11.7 us (8%)
  other arithmetic  8.96 us (6%)
  local copies, waits for them, and re-layouts  7.68 us (5%)
    pallas_call x1, Pallas kernels, dispatch_expert(): pl.pallas_call(functools.partial(dispatch_expert_kernel, axis, rows, 256)...  36.7 us
    pallas_call x1, Pallas kernels, torus_gather(): pl.pallas_call(functools.partial(torus_gather_kernel, side, count), out_s...  24.9 us
    pallas_call x1, Pallas kernels, torus_reduce(): pl.pallas_call(functools.partial(torus_reduce_kernel, side), out_shape=ja...  24.9 us
    pallas_call x1, Pallas kernels, exchange(): pl.pallas_call(functools.partial(exchange_kernel, axis, rows), out_shape=...  24.2 us
    dot_general x1, matrix products, per_device(): jnp.dot(shared_hidden, shared_down, preferred_element_type=jnp.float32)  4.16 us
    unnamed x11, local copies, waits for them, and re-layouts  2.94 us

profile of v9, /device:TPU:1, one launch (start us, length us, event | category | flops | bytes accessed | tf_op | source)
XLA Modules:
  0.0 139.2 jit_solution(10035873033125995794)
XLA Ops:
  0.0 0.0 copy-start
  0.0 0.0 copy-start.4
  0.0 0.1 copy.46
  0.1 0.8 convert.6
  0.9 0.1 copy.35
  1.0 0.7 convert.7
  1.7 0.1 copy.36
  1.8 0.7 fusion.20.refs_1_
  2.5 24.9 %shard_map.91 = (bf16[16,16,3584]{2,1,0:T(8,128)(2,1)}, bf16[16,16,128]{2,1,0:T(8,128)(2,1)}) custom-call(bf16[16,3584]{1,0:T(8,128)(2,1)} %refs_0_.1, bf16[16,128]{1,0:T(8,128)(2,1)} %fusion.20.refs_1_), custom_call_target="tpu_custom_call" | custom-call | tf_op jit(solution)/shard_map/pallas_call | solution.py:128
  27.4 1.0 convert_reduce_fusion
  28.4 1.0 multiply_divide_fusion
  29.4 0.1 copy.41
  29.5 0.9 slice_convert_fusion
  30.4 0.1 copy.37
  30.4 0.2 fusion.4
  30.6 0.1 compare_reduce_fusion
  30.8 0.1 copy.39
  31.0 0.0 copy-done.4
  31.0 2.1 %fusion.22 = f32[256,128]{1,0:T(8,128)S(1)} fusion(bf16[256,3584]{1,0:T(8,128)(2,1)} %bitcast.22, bf16[3584,128]{1,0:T(8,128)(2,1)S(1)} %copy-done.4), kind=kOutput, calls=%fused_computation.40 | convolution fusion | flops 234881024 | bytes 2883584 | tf_op jit(solution)/shard_map/dot_general | solution.py:505
  33.1 0.0 copy-start.1
  33.1 0.1 copy.45
  33.3 0.7 compare_and_fusion
  34.0 0.1 copy.40
  34.2 1.2 broadcast_and_fusion
  35.4 1.5 %and.55 = pred[256,256]{1,0:T(32,128)(4,1)} reshape(pred[8,16,2,16,16]{4,3,2,1,0:T(8,128)(4,1)S(1)} %broadcast_and_fusion) | data formatting | bytes 131072 | tf_op jit(solution)/shard_map/and | solution.py:488
  36.8 0.0 copy-done.1
  36.8 2.7 %convolution_convert_fusion.send_ref = bf16[256,3584]{1,0:T(8,128)(2,1)} fusion(pred[256,256]{1,0:T(32,128)(4,1)} %and.55, bf16[256,3584]{1,0:T(8,128)(2,1)S(1)} %bitcast.23), kind=kOutput, calls=%fused_computation.3 | convolution fusion | flops 470679552 | bytes 3735552 | tf_op jit(solution)/shard_map/dot_general | solution.py:492
  39.6 36.7 %shard_map.92.send_ref = bf16[256,3584]{1,0:T(8,128)(2,1)} custom-call(bf16[256,3584]{1,0:T(8,128)(2,1)} %convolution_convert_fusion.send_ref, bf16[1,3584,1024]{2,1,0:T(8,128)(2,1)} %gate_hbm.1, bf16[1,3584,1024]{2,1,0:T(8,128)(2,1)} %up_hbm.1, bf16[1,1024,3584]{2,1,0:T(8,128)(2,1)} %down_hbm.1), custom_call_target="tpu_custom_call" | custom-call | tf_op jit(solution)/shard_map/pallas_call | solution.py:413
  76.3 24.2 %shard_map.93 = bf16[256,3584]{1,0:T(8,128)(2,1)} custom-call(bf16[256,3584]{1,0:T(8,128)(2,1)} %shard_map.92.send_ref), custom_call_target="tpu_custom_call" | custom-call | tf_op jit(solution)/shard_map/pallas_call | solution.py:321
  100.5 0.0 copy-done
  100.5 4.2 %fusion.3 = f32[256,3584]{1,0:T(8,128)} fusion(bf16[128,3584]{1,0:T(8,128)(2,1)S(1)} %copy-done, bf16[256,3584]{1,0:T(8,128)(2,1)S(1)} %bitcast.24, bf16[3584,128]{1,0:T(8,128)(2,1)} %param.16, f32[256,128]{1,0:T(8,128)S(1)} %fusion.22), kind=kOutput, calls=%fused_computation.6 | convolution fusion | flops 469958656 | bytes 7471104 | tf_op jit(solution)/shard_map/dot_general | solution.py:508
  104.7 0.0 copy-start.2
  104.7 1.6 %broadcast_select_fusion = f32[16,16,8,16,2]{1,0,4,3,2:T(8,128)} fusion(f32[16,16,8,2]{1,0,3,2:T(8,128)S(1)} %fusion.13, pred[16,16]{0,1:T(8,128)(4,1)S(1)} %iota_compare_fusion.2), kind=kLoop, calls=%fused_computation.7 | loop fusion | flops 65536 | bytes 278784 | tf_op jit(solution)/shard_map/jit(_where)/select_n | solution.py:499
  106.3 2.4 %select_n.23 = f32[256,256]{0,1:T(8,128)S(1)} reshape(f32[16,16,8,16,2]{1,0,4,3,2:T(8,128)} %broadcast_select_fusion) | data formatting | bytes 524288 | tf_op jit(solution)/shard_map/jit(_where)/select_n | solution.py:499
  108.7 0.0 copy-done.2
  108.8 0.0 copy-start.3
  108.8 0.7 fusion.15
  109.4 1.4 copy-done.3
  110.8 2.0 %fusion.1 = bf16[256,3584]{1,0:T(8,128)(2,1)} fusion(f32[256,3584]{1,0:T(8,128)S(1)} %copy-done.3, f32[256,3584]{1,0:T(8,128)S(1)} %fusion.15, bf16[256,3584]{1,0:T(8,128)(2,1)S(1)} %copy-done.2, f32[256,256]{0,1:T(8,128)S(1)} %select_n.23), kind=kOutput, calls=%fused_computation.2 | convolution fusion | flops 472776704 | bytes 11272192 | tf_op jit(solution)/shard_map/dot_general | solution.py:450
  112.8 24.9 %shard_map.94 = bf16[16,3584]{1,0:T(8,128)(2,1)} custom-call(bf16[16,16,3584]{2,1,0:T(8,128)(2,1)} %bitcast.25), custom_call_target="tpu_custom_call" | custom-call | tf_op jit(solution)/shard_map/pallas_call | solution.py:249
  137.7 1.6 %copy.50 = bf16[16,3584]{1,0:T(8,128)(2,1)} copy(bf16[16,3584]{1,0:T(8,128)(2,1)} %shard_map.94) | data formatting | bytes 229376
  (8 shorter events, 0.1 us)
Async XLA Ops:
  0.0 100.5 %copy-start = (bf16[128,3584]{1,0:T(8,128)(2,1)S(1)}, bf16[128,3584]{1,0:T(8,128)(2,1)}, u32[]{:S(2)}) copy-start(bf16[128,3584]{1,0:T(8,128)(2,1)} %param.17) | copy-start | bytes 2752516
  0.0 31.0 %copy-start.4 = (bf16[3584,128]{1,0:T(8,128)(2,1)S(1)}, bf16[3584,128]{1,0:T(8,128)(2,1)}, u32[]{:S(2)}) copy-start(bf16[3584,128]{1,0:T(8,128)(2,1)} %param.15) | copy-start | bytes 2752516
  33.1 3.7 %copy-start.1 = (bf16[16,16,3584]{2,1,0:T(8,128)(2,1)S(1)}, bf16[16,16,3584]{2,1,0:T(8,128)(2,1)}, u32[]{:S(2)}) copy-start(bf16[16,16,3584]{2,1,0:T(8,128)(2,1)} %get-tuple-element.7) | copy-start | bytes 5505028
  104.7 4.0 %copy-start.2 = (bf16[256,3584]{1,0:T(8,128)(2,1)S(1)}, bf16[256,3584]{1,0:T(8,128)(2,1)}, u32[]{:S(2)}) copy-start(bf16[256,3584]{1,0:T(8,128)(2,1)} %shard_map.93) | copy-start | bytes 5505028
  108.8 2.0 %copy-start.3 = (f32[256,3584]{1,0:T(8,128)S(1)}, f32[256,3584]{1,0:T(8,128)}, u32[]{:S(2)}) copy-start(f32[256,3584]{1,0:T(8,128)} %fusion.3) | copy-start | bytes 11010052

commit v10 on v9

--- a/solution.py
+++ b/solution.py
@@ -334,9 +334,10 @@
     )(send)
 
 
-def dispatch_expert_kernel(axis, rows, tile, send_ref, gate_hbm, up_hbm, down_hbm, out_ref,
-                           recv, gate_w, up_w, down_w, hidden, send_sems, recv_sems,
-                           local_sems):
+def dispatch_expert_kernel(axis, rows, tile, send_ref, gate_hbm, up_hbm, down_hbm,
+                           segment_hbm, sgate_hbm, sup_hbm, sdown_hbm, out_ref, shared_ref,
+                           recv, gate_w, up_w, down_w, hidden, segment, sgate, sup, sdown,
+                           send_sems, recv_sems, local_sems):
     count = lax.axis_size(axis)
     me = lax.axis_index(axis)
     weights = [
@@ -344,7 +345,13 @@
         pltpu.make_async_copy(up_hbm.at[0], up_w, local_sems.at[1]),
         pltpu.make_async_copy(down_hbm.at[0], down_w, local_sems.at[2]),
     ]
-    for copy in weights:
+    shared_inputs = [
+        pltpu.make_async_copy(segment_hbm, segment, local_sems.at[4]),
+        pltpu.make_async_copy(sgate_hbm, sgate, local_sems.at[5]),
+        pltpu.make_async_copy(sup_hbm, sup, local_sems.at[6]),
+        pltpu.make_async_copy(sdown_hbm, sdown, local_sems.at[7]),
+    ]
+    for copy in shared_inputs + weights:
         copy.start()
     barrier = pltpu.get_barrier_semaphore()
 
@@ -371,6 +378,20 @@
             device_id_type=MESH_ID,
         ).start()
 
+    for copy in shared_inputs:
+        copy.wait()
+    tokens = segment[...]
+    gate_part = jnp.dot(tokens, sgate[...], preferred_element_type=jnp.float32)
+    up_part = jnp.dot(tokens, sup[...], preferred_element_type=jnp.float32)
+    shared_hidden = (gate_part / (1.0 + jnp.exp(-gate_part)) * up_part).astype(sdown.dtype)
+
+    @pl.loop(0, sdown.shape[1] // (2 * tile))
+    def _(t):
+        cols = pl.ds(pl.multiple_of(t * 2 * tile, 2 * tile), 2 * tile)
+        shared_ref[:, cols] = jnp.dot(
+            shared_hidden, sdown[:, cols], preferred_element_type=jnp.float32
+        )
+
     @pl.loop(1, count)
     def _(step):
         peer = lax.rem(me + step, count)
@@ -405,31 +426,39 @@
         ).astype(out_ref.dtype)
 
 
-def dispatch_expert(send, gate, up, down, axis, collective_id):
+def dispatch_expert(send, gate, up, down, segment, sgate, sup, sdown, axis, collective_id):
     count = lax.axis_size(axis)
     rows = send.shape[0] // count
     width = gate.shape[2]
     any_space = pl.BlockSpec(memory_space=pl.ANY)
+    vmem_space = pl.BlockSpec(memory_space=pltpu.VMEM)
     return pl.pallas_call(
         functools.partial(dispatch_expert_kernel, axis, rows, 256),
-        out_shape=jax.ShapeDtypeStruct(send.shape, send.dtype),
-        in_specs=[any_space] * 4,
-        out_specs=pl.BlockSpec(memory_space=pltpu.VMEM),
+        out_shape=(
+            jax.ShapeDtypeStruct(send.shape, send.dtype),
+            jax.ShapeDtypeStruct((segment.shape[0], sdown.shape[1]), jnp.float32),
+        ),
+        in_specs=[any_space] * 8,
+        out_specs=(vmem_space, vmem_space),
         scratch_shapes=[
             pltpu.VMEM(send.shape, send.dtype),
             pltpu.VMEM(gate.shape[1:], gate.dtype),
             pltpu.VMEM(up.shape[1:], up.dtype),
             pltpu.VMEM(down.shape[1:], down.dtype),
             pltpu.VMEM((send.shape[0], width), jnp.bfloat16),
+            pltpu.VMEM(segment.shape, segment.dtype),
+            pltpu.VMEM(sgate.shape, sgate.dtype),
+            pltpu.VMEM(sup.shape, sup.dtype),
+            pltpu.VMEM(sdown.shape, sdown.dtype),
             pltpu.SemaphoreType.DMA((count,)),
             pltpu.SemaphoreType.DMA((count,)),
-            pltpu.SemaphoreType.DMA((4,)),
+            pltpu.SemaphoreType.DMA((8,)),
         ],
         compiler_params=pltpu.CompilerParams(
             collective_id=collective_id, has_side_effects=True,
             vmem_limit_bytes=56 * 1024 * 1024,
         ),
-    )(send, gate, up, down)
+    )(send, gate, up, down, segment, sgate, sup, sdown)
 
 
 def gated_mlp(inputs, gate_matrix, up_matrix, down_matrix):
@@ -492,7 +521,10 @@
     outbound = jnp.dot(
         selector.astype(jnp.bfloat16), segment, preferred_element_type=jnp.float32
     ).astype(jnp.bfloat16)
-    answer = dispatch_expert(outbound, expert_gate, expert_up, expert_down, "outer", 1)
+    answer, shared = dispatch_expert(
+        outbound, expert_gate, expert_up, expert_down,
+        segment, shared_gate, shared_up, shared_down, "outer", 1,
+    )
     returned = exchange(answer, "outer", 2)
     slot_weight = jnp.sum(jnp.where(matches, weights[..., None], 0.0), axis=2)
     placed_weight = jnp.where(placed, slot_weight[..., None], 0.0)
@@ -502,10 +534,6 @@
         0.0,
     ).reshape(inner_count * row_count, outer_count * inner_count * capacity)
     routed = weighted_rows(combine, returned)
-    gate_part = jnp.dot(segment, shared_gate, preferred_element_type=jnp.float32)
-    up_part = jnp.dot(segment, shared_up, preferred_element_type=jnp.float32)
-    shared_hidden = (jax.nn.silu(gate_part) * up_part).astype(jnp.bfloat16)
-    shared = jnp.dot(shared_hidden, shared_down, preferred_element_type=jnp.float32)
     total = (shared + routed).astype(jnp.bfloat16)
     return torus_reduce(total.reshape(inner_count, row_count, model_width), side, 3)
 

time: 141 us -> 132 us (0.936)
  matrix products: 11.7 us -> 4.66 us
  other arithmetic: 8.96 us -> 7.48 us
    dot_general x2 -> x0, matrix products: 6.29 us -> none  [the longest x1 4.16 us: per_device(): jnp.dot(shared_hidden, shared_down, preferred_element_type=jnp.float32)]
    unnamed x11 -> x7, local copies, waits for them, and re-layouts: 2.94 us -> 2.93 us
where the time goes in v10:
time: 132 us; the launch traced here: 131 us
  Pallas kernels  111 us (84%)
  other arithmetic  7.48 us (6%)
  local copies, waits for them, and re-layouts  7.05 us (5%)
  matrix products  4.66 us (4%)
    pallas_call x1, Pallas kernels, dispatch_expert(): pl.pallas_call(functools.partial(dispatch_expert_kernel, axis, rows, 256)...  37.5 us
    pallas_call x1, Pallas kernels, torus_gather(): pl.pallas_call(functools.partial(torus_gather_kernel, side, count), out_s...  24.9 us
    pallas_call x1, Pallas kernels, torus_reduce(): pl.pallas_call(functools.partial(torus_reduce_kernel, side), out_shape=ja...  24.9 us
    pallas_call x1, Pallas kernels, exchange(): pl.pallas_call(functools.partial(exchange_kernel, axis, rows), out_shape=...  24.2 us
    unnamed x7, local copies, waits for them, and re-layouts  2.93 us

profile of v10, /device:TPU:1, one launch (start us, length us, event | category | flops | bytes accessed | tf_op | source)
XLA Modules:
  0.0 130.9 jit_solution(1289179033469247841)
XLA Ops:
  0.0 0.1 copy.42
  0.1 0.7 convert.6
  0.8 0.1 copy.35
  0.9 0.7 convert.7
  1.6 0.1 copy.36
  1.7 0.7 fusion.12.refs_1_
  2.3 24.9 %shard_map.91 = (bf16[16,16,3584]{2,1,0:T(8,128)(2,1)}, bf16[16,16,128]{2,1,0:T(8,128)(2,1)}) custom-call(bf16[16,3584]{1,0:T(8,128)(2,1)} %refs_0_.1, bf16[16,128]{1,0:T(8,128)(2,1)} %fusion.12.refs_1_), custom_call_target="tpu_custom_call" | custom-call | tf_op jit(solution)/shard_map/pallas_call | solution.py:128
  27.2 0.0 copy-start.1
  27.3 1.2 convert_reduce_fusion
  28.4 1.0 multiply_divide_fusion
  29.4 0.1 copy.45
  29.5 0.9 slice_convert_fusion
  30.3 0.1 copy.37
  30.4 0.2 fusion.2
  30.6 0.1 compare_reduce_fusion
  30.8 0.1 copy.40
  31.0 0.1 copy.41
  31.1 0.1 compare_and_fusion
  31.2 0.1 copy.44
  31.4 0.3 broadcast_and_fusion
  31.7 0.8 and.53
  32.6 0.0 copy-done.1
  32.6 2.0 %convolution_convert_fusion.send_ref = bf16[256,3584]{1,0:T(8,128)(2,1)} fusion(pred[256,256]{1,0:T(32,128)(4,1)S(1)} %and.53, bf16[256,3584]{1,0:T(8,128)(2,1)S(1)} %bitcast.18), kind=kOutput, calls=%fused_computation.3 | convolution fusion | flops 470679552 | bytes 3735552 | tf_op jit(solution)/shard_map/dot_general | solution.py:521
  34.6 37.5 %shard_map.92 = (bf16[256,3584]{1,0:T(8,128)(2,1)}, f32[256,3584]{1,0:T(8,128)}) custom-call(bf16[256,3584]{1,0:T(8,128)(2,1)} %convolution_convert_fusion.send_ref, bf16[1,3584,1024]{2,1,0:T(8,128)(2,1)} %gate_hbm.1, bf16[1,3584,1024]{2,1,0:T(8,128)(2,1)} %up_hbm.1, bf16[1,1024,3584]{2,1,0:T(8,128)(2,1)} %down_hbm.1, bf16[256,3584]{1,0:T(8,128)(2,1)} %bitcast.17, ...), custom_call_target="tpu_custom_call" | custom-call | tf_op jit(solution)/shard_map/pallas_call | solution.py:435
  72.1 24.2 %shard_map.93 = bf16[256,3584]{1,0:T(8,128)(2,1)} custom-call(bf16[256,3584]{1,0:T(8,128)(2,1)} %get-tuple-element.12.send_ref), custom_call_target="tpu_custom_call" | custom-call | tf_op jit(solution)/shard_map/pallas_call | solution.py:321
  96.3 0.0 copy-start
  96.3 1.6 %broadcast_select_fusion = f32[16,16,8,16,2]{1,0,4,3,2:T(8,128)} fusion(f32[16,16,8,2]{1,0,3,2:T(8,128)S(1)} %fusion.6, pred[16,16]{0,1:T(8,128)(4,1)S(1)} %iota_compare_fusion.2), kind=kLoop, calls=%fused_computation.4 | loop fusion | flops 65536 | bytes 278784 | tf_op jit(solution)/shard_map/jit(_where)/select_n | solution.py:531
  97.9 2.4 %select_n.23 = f32[256,256]{0,1:T(8,128)S(1)} reshape(f32[16,16,8,16,2]{1,0,4,3,2:T(8,128)} %broadcast_select_fusion) | data formatting | bytes 524288 | tf_op jit(solution)/shard_map/jit(_where)/select_n | solution.py:531
  100.4 0.0 copy-done
  100.4 0.0 copy-start.2
  100.4 0.7 fusion.8
  101.1 1.4 %copy-done.2 = f32[256,3584]{1,0:T(8,128)S(1)} copy-done((f32[256,3584]{1,0:T(8,128)S(1)}, f32[256,3584]{1,0:T(8,128)}, u32[]{:S(2)}) %copy-start.2) | copy-done | bytes 3670040
  102.4 2.0 %fusion.1 = bf16[256,3584]{1,0:T(8,128)(2,1)} fusion(f32[256,3584]{1,0:T(8,128)S(1)} %copy-done.2, f32[256,3584]{1,0:T(8,128)S(1)} %fusion.8, bf16[256,3584]{1,0:T(8,128)(2,1)S(1)} %copy-done, f32[256,256]{0,1:T(8,128)S(1)} %select_n.23), kind=kOutput, calls=%fused_computation.2 | convolution fusion | flops 472776704 | bytes 11272192 | tf_op jit(solution)/shard_map/dot_general | solution.py:479
  104.4 24.9 %shard_map.94 = bf16[16,3584]{1,0:T(8,128)(2,1)} custom-call(bf16[16,16,3584]{2,1,0:T(8,128)(2,1)} %bitcast.19), custom_call_target="tpu_custom_call" | custom-call | tf_op jit(solution)/shard_map/pallas_call | solution.py:249
  129.3 1.6 %copy.50 = bf16[16,3584]{1,0:T(8,128)(2,1)} copy(bf16[16,3584]{1,0:T(8,128)(2,1)} %shard_map.94) | data formatting | bytes 229376
  (8 shorter events, 0.1 us)
Async XLA Ops:
  27.2 5.3 %copy-start.1 = (bf16[16,16,3584]{2,1,0:T(8,128)(2,1)S(1)}, bf16[16,16,3584]{2,1,0:T(8,128)(2,1)}, u32[]{:S(2)}) copy-start(bf16[16,16,3584]{2,1,0:T(8,128)(2,1)} %get-tuple-element.10) | copy-start | bytes 5505028
  96.3 4.1 %copy-start = (bf16[256,3584]{1,0:T(8,128)(2,1)S(1)}, bf16[256,3584]{1,0:T(8,128)(2,1)}, u32[]{:S(2)}) copy-start(bf16[256,3584]{1,0:T(8,128)(2,1)} %shard_map.93) | copy-start | bytes 5505028
  100.4 2.0 %copy-start.2 = (f32[256,3584]{1,0:T(8,128)S(1)}, f32[256,3584]{1,0:T(8,128)}, u32[]{:S(2)}) copy-start(f32[256,3584]{1,0:T(8,128)} %get-tuple-element.11) | copy-start | bytes 11010052

commit v11 on v10

--- a/solution.py
+++ b/solution.py
@@ -335,9 +335,9 @@
 
 
 def dispatch_expert_kernel(axis, rows, tile, send_ref, gate_hbm, up_hbm, down_hbm,
-                           segment_hbm, sgate_hbm, sup_hbm, sdown_hbm, out_ref, shared_ref,
+                           segment_hbm, sgate_hbm, sup_hbm, sdown_hbm, back_ref, shared_ref,
                            recv, gate_w, up_w, down_w, hidden, segment, sgate, sup, sdown,
-                           send_sems, recv_sems, local_sems):
+                           out_ref, send_sems, recv_sems, local_sems, back_send, back_recv):
     count = lax.axis_size(axis)
     me = lax.axis_index(axis)
     weights = [
@@ -417,13 +417,60 @@
         hidden[:, cols] = (gate_part / (1.0 + jnp.exp(-gate_part)) * up_part).astype(hidden.dtype)
 
     weights[2].wait()
-
-    @pl.loop(0, down_w.shape[1] // (2 * tile))
-    def _(t):
-        cols = pl.ds(pl.multiple_of(t * 2 * tile, 2 * tile), 2 * tile)
-        out_ref[:, cols] = jnp.dot(
-            hidden[...], down_w[:, cols], preferred_element_type=jnp.float32
-        ).astype(out_ref.dtype)
+    chunks = 2
+    per_chunk = count // chunks
+    chunk_rows = per_chunk * rows
+    for part in range(chunks):
+        lines = pl.ds(part * chunk_rows, chunk_rows)
+
+        @pl.loop(0, down_w.shape[1] // (2 * tile))
+        def _(t):
+            cols = pl.ds(pl.multiple_of(t * 2 * tile, 2 * tile), 2 * tile)
+            out_ref[lines, cols] = jnp.dot(
+                hidden[lines, :], down_w[:, cols], preferred_element_type=jnp.float32
+            ).astype(out_ref.dtype)
+
+        @pl.loop(part * per_chunk, (part + 1) * per_chunk)
+        def _(peer):
+            @pl.when(peer != me)
+            def _():
+                pltpu.make_async_remote_copy(
+                    src_ref=out_ref.at[pl.ds(peer * rows, rows)],
+                    dst_ref=back_ref.at[pl.ds(me * rows, rows)],
+                    send_sem=back_send.at[peer],
+                    recv_sem=back_recv.at[me],
+                    device_id={axis: peer},
+                    device_id_type=MESH_ID,
+                ).start()
+
+            @pl.when(peer == me)
+            def _():
+                pltpu.make_async_copy(
+                    out_ref.at[pl.ds(peer * rows, rows)],
+                    back_ref.at[pl.ds(me * rows, rows)],
+                    local_sems.at[8],
+                ).start()
+
+    @pl.loop(0, count)
+    def _(peer):
+        @pl.when(peer != me)
+        def _():
+            pltpu.make_async_remote_copy(
+                src_ref=out_ref.at[pl.ds(peer * rows, rows)],
+                dst_ref=back_ref.at[pl.ds(peer * rows, rows)],
+                send_sem=back_send.at[peer],
+                recv_sem=back_recv.at[peer],
+                device_id={axis: peer},
+                device_id_type=MESH_ID,
+            ).wait()
+
+        @pl.when(peer == me)
+        def _():
+            pltpu.make_async_copy(
+                out_ref.at[pl.ds(peer * rows, rows)],
+                back_ref.at[pl.ds(me * rows, rows)],
+                local_sems.at[8],
+            ).wait()
 
 
 def dispatch_expert(send, gate, up, down, segment, sgate, sup, sdown, axis, collective_id):
@@ -450,9 +497,12 @@
             pltpu.VMEM(sgate.shape, sgate.dtype),
             pltpu.VMEM(sup.shape, sup.dtype),
             pltpu.VMEM(sdown.shape, sdown.dtype),
+            pltpu.VMEM(send.shape, send.dtype),
             pltpu.SemaphoreType.DMA((count,)),
             pltpu.SemaphoreType.DMA((count,)),
-            pltpu.SemaphoreType.DMA((8,)),
+            pltpu.SemaphoreType.DMA((9,)),
+            pltpu.SemaphoreType.DMA((count,)),
+            pltpu.SemaphoreType.DMA((count,)),
         ],
         compiler_params=pltpu.CompilerParams(
             collective_id=collective_id, has_side_effects=True,
@@ -521,11 +571,10 @@
     outbound = jnp.dot(
         selector.astype(jnp.bfloat16), segment, preferred_element_type=jnp.float32
     ).astype(jnp.bfloat16)
-    answer, shared = dispatch_expert(
+    returned, shared = dispatch_expert(
         outbound, expert_gate, expert_up, expert_down,
         segment, shared_gate, shared_up, shared_down, "outer", 1,
     )
-    returned = exchange(answer, "outer", 2)
     slot_weight = jnp.sum(jnp.where(matches, weights[..., None], 0.0), axis=2)
     placed_weight = jnp.where(placed, slot_weight[..., None], 0.0)
     combine = jnp.where(

time: 132 us -> 129 us (0.977)
  local copies, waits for them, and re-layouts: 7.05 us -> 4.99 us
  Pallas kernels: 111 us -> 109 us
  matrix products: 4.66 us -> 6.19 us
  other arithmetic: 7.48 us -> 6.13 us
    pallas_call x1 -> x0, Pallas kernels: 24.2 us -> none  [exchange(): pl.pallas_call(functools.partial(exchange_kernel, axis, rows), out_shape=...]
    pallas_call x1, Pallas kernels: 37.5 us -> 59.3 us  [dispatch_expert(): pl.pallas_call(functools.partial(dispatch_expert_kernel, axis, rows, 256)...]
    dot_general x1, matrix products: 0.66 us -> 2.31 us  [weighted_rows(): jnp.dot(high, rows, preferred_element_type=jnp.float32)]
    select_n x1, local copies, waits for them, and re-layouts: 2.44 us -> 0.94 us  [per_device(): jnp.where(same_block[:, None, None, :, None], jnp.transpose(placed_weight...]
    select_n x1, other arithmetic: 1.6 us -> 0.24 us  [per_device(): jnp.where(same_block[:, None, None, :, None], jnp.transpose(placed_weight...]
where the time goes in v11:
time: 129 us; the launch traced here: 127 us
  Pallas kernels  109 us (84%)
  matrix products  6.19 us (5%)
  other arithmetic  6.13 us (5%)
  local copies, waits for them, and re-layouts  4.99 us (4%)
    pallas_call x1, Pallas kernels, dispatch_expert(): pl.pallas_call(functools.partial(dispatch_expert_kernel, axis, rows, 256)...  59.3 us
    pallas_call x1, Pallas kernels, torus_reduce(): pl.pallas_call(functools.partial(torus_reduce_kernel, side), out_shape=ja...  25 us
    pallas_call x1, Pallas kernels, torus_gather(): pl.pallas_call(functools.partial(torus_gather_kernel, side, count), out_s...  24.9 us

profile of v11, /device:TPU:1, one launch (start us, length us, event | category | flops | bytes accessed | tf_op | source)
XLA Modules:
  0.0 126.7 jit_solution(7578795792412188411)
XLA Ops:
  0.0 0.1 copy.42
  0.1 0.7 convert.6
  0.8 0.1 copy.35
  0.9 0.7 convert.7
  1.6 0.1 copy.36
  1.7 0.7 fusion.12.refs_1_
  2.3 24.9 %shard_map.91 = (bf16[16,16,3584]{2,1,0:T(8,128)(2,1)}, bf16[16,16,128]{2,1,0:T(8,128)(2,1)}) custom-call(bf16[16,3584]{1,0:T(8,128)(2,1)} %refs_0_.1, bf16[16,128]{1,0:T(8,128)(2,1)} %fusion.12.refs_1_), custom_call_target="tpu_custom_call" | custom-call | tf_op jit(solution)/shard_map/pallas_call | solution.py:128
  27.2 0.0 copy-start
  27.3 1.2 convert_reduce_fusion
  28.4 1.0 multiply_divide_fusion
  29.4 0.1 copy.45
  29.5 0.9 slice_convert_fusion
  30.3 0.1 copy.37
  30.4 0.2 fusion.2
  30.6 0.1 compare_reduce_fusion
  30.8 0.1 copy.40
  31.0 0.1 copy.41
  31.1 0.1 compare_and_fusion
  31.2 0.1 copy.44
  31.4 0.3 broadcast_and_fusion
  31.7 0.8 and.53
  32.6 0.0 copy-done
  32.6 1.9 %convolution_convert_fusion.send_ref = bf16[256,3584]{1,0:T(8,128)(2,1)} fusion(pred[256,256]{1,0:T(32,128)(4,1)S(1)} %and.53, bf16[256,3584]{1,0:T(8,128)(2,1)S(1)} %bitcast.18), kind=kOutput, calls=%fused_computation.3 | convolution fusion | flops 470679552 | bytes 3735552 | tf_op jit(solution)/shard_map/dot_general | solution.py:571
  34.5 59.3 %shard_map.92 = (bf16[256,3584]{1,0:T(8,128)(2,1)}, f32[256,3584]{1,0:T(8,128)}) custom-call(bf16[256,3584]{1,0:T(8,128)(2,1)} %convolution_convert_fusion.send_ref, bf16[1,3584,1024]{2,1,0:T(8,128)(2,1)} %gate_hbm.1, bf16[1,3584,1024]{2,1,0:T(8,128)(2,1)} %up_hbm.1, bf16[1,1024,3584]{2,1,0:T(8,128)(2,1)} %down_hbm.1, bf16[256,3584]{1,0:T(8,128)(2,1)} %bitcast.17, ...), custom_call_target="tpu_custom_call" | custom-call | tf_op jit(solution)/shard_map/pallas_call | solution.py:482
  93.8 0.2 broadcast_select_fusion
  94.1 0.9 select_n.23
  95.0 0.0 copy-start.1
  95.0 0.0 copy-start.2
  95.0 2.3 %fusion.8 = f32[256,3584]{1,0:T(8,128)S(1)} fusion(bf16[256,3584]{1,0:T(8,128)(2,1)} %get-tuple-element.12, f32[256,256]{0,1:T(8,128)S(1)} %select_n.23), kind=kOutput, calls=%fused_computation.21 | convolution fusion | flops 469827584 | bytes 5767168 | tf_op jit(solution)/shard_map/dot_general | solution.py:529
  97.3 0.0 copy-done.1
  97.4 0.8 copy-done.2
  98.2 1.9 %fusion.1 = bf16[256,3584]{1,0:T(8,128)(2,1)} fusion(f32[256,3584]{1,0:T(8,128)S(1)} %copy-done.2, f32[256,3584]{1,0:T(8,128)S(1)} %fusion.8, bf16[256,3584]{1,0:T(8,128)(2,1)S(1)} %copy-done.1, f32[256,256]{0,1:T(8,128)S(1)} %select_n.23), kind=kOutput, calls=%fused_computation.2 | convolution fusion | flops 472776704 | bytes 11272192 | tf_op jit(solution)/shard_map/dot_general | solution.py:529
  100.1 25.0 %shard_map.93 = bf16[16,3584]{1,0:T(8,128)(2,1)} custom-call(bf16[16,16,3584]{2,1,0:T(8,128)(2,1)} %bitcast.19), custom_call_target="tpu_custom_call" | custom-call | tf_op jit(solution)/shard_map/pallas_call | solution.py:249
  125.1 1.6 %copy.50 = bf16[16,3584]{1,0:T(8,128)(2,1)} copy(bf16[16,3584]{1,0:T(8,128)(2,1)} %shard_map.93) | data formatting | bytes 229376
  (8 shorter events, 0.1 us)
Async XLA Ops:
  27.2 5.3 %copy-start = (bf16[16,16,3584]{2,1,0:T(8,128)(2,1)S(1)}, bf16[16,16,3584]{2,1,0:T(8,128)(2,1)}, u32[]{:S(2)}) copy-start(bf16[16,16,3584]{2,1,0:T(8,128)(2,1)} %get-tuple-element.10) | copy-start | bytes 5505028
  95.0 2.3 %copy-start.1 = (bf16[256,3584]{1,0:T(8,128)(2,1)S(1)}, bf16[256,3584]{1,0:T(8,128)(2,1)}, u32[]{:S(2)}) copy-start(bf16[256,3584]{1,0:T(8,128)(2,1)} %get-tuple-element.12) | copy-start | bytes 5505028
  95.0 3.1 %copy-start.2 = (f32[256,3584]{1,0:T(8,128)S(1)}, f32[256,3584]{1,0:T(8,128)}, u32[]{:S(2)}) copy-start(f32[256,3584]{1,0:T(8,128)} %get-tuple-element.11) | copy-start | bytes 11010052

commit v12 on v11

--- a/solution.py
+++ b/solution.py
@@ -28,7 +28,10 @@
         (lambda zz, yy, k: node(zz, yy + k), lambda zz, yy, k: node(zz + k, yy)),
         (lambda zz, yy, k: node(zz + k, yy), lambda zz, yy, k: node(zz, yy + k)),
     ]
-    neighbours = [node(z, y + 1), node(z, y - 1), node(z + 1, y), node(z - 1, y)]
+    neighbours = [
+        node(z, y + 1), node(z, y - 1), node(z, y + 2),
+        node(z + 1, y), node(z - 1, y), node(z + 2, y),
+    ]
     barrier = pltpu.get_barrier_semaphore()
     for peer in neighbours:
         pl.semaphore_signal(barrier, inc=1, device_id={"inner": peer}, device_id_type=MESH_ID)
@@ -83,16 +86,9 @@
     moves, incoming = [], []
     for h in range(2):
         first = steps[h][0]
-        for k in (1, -1):
+        for k in (1, -1, 2):
             moves.append((me, h, first(z, y, k), True))
             incoming.append((base + len(incoming), first(z, y, -k), h, first(z, y, -k)))
-    finish(run_round(moves), incoming)
-    base = counter[0]
-    moves, incoming = [], []
-    for h in range(2):
-        first = steps[h][0]
-        moves.append((first(z, y, -1), h, first(z, y, 1), False))
-        incoming.append((base + len(incoming), first(z, y, -2), h, first(z, y, -1)))
     finish(run_round(moves), incoming)
     for copy in local_copies:
         copy.wait()
@@ -163,7 +159,10 @@
         (lambda k: node(z, y + k), lambda k: node(z + k, y), y, z,
          lambda pos, j: j * side + pos),
     ]
-    neighbours = [node(z, y + 1), node(z, y - 1), node(z + 1, y), node(z - 1, y)]
+    neighbours = [
+        node(z, y + 1), node(z, y - 1), node(z, y + 2),
+        node(z + 1, y), node(z - 1, y), node(z + 2, y),
+    ]
     barrier = pltpu.get_barrier_semaphore()
     for peer in neighbours:
         pl.semaphore_signal(barrier, inc=1, device_id={"inner": peer}, device_id_type=MESH_ID)
@@ -219,13 +218,10 @@
     sent, senders = [], []
     for h, (ring1, ring2, p1, p2, block) in enumerate(plans):
         send_a2[h] = partial[h, wrap(p2 + 2)].astype(send_a2.dtype)
-        sent.append(send(send_a2.at[h], recv_a2.at[h], ring2(1)))
-        senders.append(ring2(-1))
-    settle(sent, senders)
-    sent, senders = [], []
-    for h, (ring1, ring2, p1, p2, block) in enumerate(plans):
-        send_b2[h] = (partial[h, wrap(p2 + 1)] + recv_a2[h].astype(jnp.float32)).astype(send_b2.dtype)
+        send_b2[h] = partial[h, wrap(p2 + 1)].astype(send_b2.dtype)
         send_c2[h] = partial[h, wrap(p2 - 1)].astype(send_c2.dtype)
+        sent.append(send(send_a2.at[h], recv_a2.at[h], ring2(2)))
+        senders.append(ring2(-2))
         sent.append(send(send_b2.at[h], recv_b2p.at[h], ring2(1)))
         senders.append(ring2(-1))
         sent.append(send(send_c2.at[h], recv_b2m.at[h], ring2(-1)))
@@ -234,6 +230,7 @@
     for h, (ring1, ring2, p1, p2, block) in enumerate(plans):
         out_ref[rows[h], :] = (
             partial[h, p2]
+            + recv_a2[h].astype(jnp.float32)
             + recv_b2p[h].astype(jnp.float32)
             + recv_b2m[h].astype(jnp.float32)
         ).astype(out_ref.dtype)

time: 129 us -> 124 us (0.961)
  Pallas kernels: 109 us -> 105 us
    pallas_call x1, Pallas kernels: 25 us -> 22.6 us  [torus_reduce(): pl.pallas_call(functools.partial(torus_reduce_kernel, side), out_shape=ja...]
where the time goes in v12:
time: 124 us; the launch traced here: 123 us
  Pallas kernels  105 us (85%)
  matrix products  6.19 us (5%)
  other arithmetic  6.13 us (5%)
  local copies, waits for them, and re-layouts  4.99 us (4%)
    pallas_call x1, Pallas kernels, dispatch_expert(): pl.pallas_call(functools.partial(dispatch_expert_kernel, axis, rows, 256)...  58.9 us
    pallas_call x1, Pallas kernels, torus_gather(): pl.pallas_call(functools.partial(torus_gather_kernel, side, count), out_s...  23.6 us
    pallas_call x1, Pallas kernels, torus_reduce(): pl.pallas_call(functools.partial(torus_reduce_kernel, side), out_shape=ja...  22.6 us

profile of v12, /device:TPU:1, one launch (start us, length us, event | category | flops | bytes accessed | tf_op | source)
XLA Modules:
  0.0 122.6 jit_solution(13262954291220063323)
XLA Ops:
  0.0 0.1 copy.42
  0.1 0.7 convert.6
  0.8 0.1 copy.35
  0.9 0.7 convert.7
  1.6 0.1 copy.36
  1.7 0.7 fusion.12.refs_1_
  2.3 23.6 %shard_map.91 = (bf16[16,16,3584]{2,1,0:T(8,128)(2,1)}, bf16[16,16,128]{2,1,0:T(8,128)(2,1)}) custom-call(bf16[16,3584]{1,0:T(8,128)(2,1)} %refs_0_.1, bf16[16,128]{1,0:T(8,128)(2,1)} %fusion.12.refs_1_), custom_call_target="tpu_custom_call" | custom-call | tf_op jit(solution)/shard_map/pallas_call | solution.py:124
  26.0 0.0 copy-start
  26.0 1.2 convert_reduce_fusion
  27.1 1.0 multiply_divide_fusion
  28.1 0.1 copy.45
  28.2 0.9 slice_convert_fusion
  29.1 0.1 copy.37
  29.1 0.2 fusion.2
  29.3 0.1 compare_reduce_fusion
  29.5 0.1 copy.40
  29.7 0.1 copy.41
  29.8 0.1 compare_and_fusion
  30.0 0.1 copy.44
  30.1 0.3 broadcast_and_fusion
  30.5 0.8 and.53
  31.3 0.0 copy-done
  31.3 1.9 %convolution_convert_fusion.send_ref = bf16[256,3584]{1,0:T(8,128)(2,1)} fusion(pred[256,256]{1,0:T(32,128)(4,1)S(1)} %and.53, bf16[256,3584]{1,0:T(8,128)(2,1)S(1)} %bitcast.18), kind=kOutput, calls=%fused_computation.3 | convolution fusion | flops 470679552 | bytes 3735552 | tf_op jit(solution)/shard_map/dot_general | solution.py:568
  33.3 58.9 %shard_map.92 = (bf16[256,3584]{1,0:T(8,128)(2,1)}, f32[256,3584]{1,0:T(8,128)}) custom-call(bf16[256,3584]{1,0:T(8,128)(2,1)} %convolution_convert_fusion.send_ref, bf16[1,3584,1024]{2,1,0:T(8,128)(2,1)} %gate_hbm.1, bf16[1,3584,1024]{2,1,0:T(8,128)(2,1)} %up_hbm.1, bf16[1,1024,3584]{2,1,0:T(8,128)(2,1)} %down_hbm.1, bf16[256,3584]{1,0:T(8,128)(2,1)} %bitcast.17, ...), custom_call_target="tpu_custom_call" | custom-call | tf_op jit(solution)/shard_map/pallas_call | solution.py:479
  92.2 0.2 broadcast_select_fusion
  92.4 0.9 select_n.23
  93.3 0.0 copy-start.1
  93.3 0.0 copy-start.2
  93.4 2.3 %fusion.8 = f32[256,3584]{1,0:T(8,128)S(1)} fusion(bf16[256,3584]{1,0:T(8,128)(2,1)} %get-tuple-element.12, f32[256,256]{0,1:T(8,128)S(1)} %select_n.23), kind=kOutput, calls=%fused_computation.21 | convolution fusion | flops 469827584 | bytes 5767168 | tf_op jit(solution)/shard_map/dot_general | solution.py:526
  95.7 0.0 copy-done.1
  95.7 0.8 copy-done.2
  96.5 1.9 %fusion.1 = bf16[256,3584]{1,0:T(8,128)(2,1)} fusion(f32[256,3584]{1,0:T(8,128)S(1)} %copy-done.2, f32[256,3584]{1,0:T(8,128)S(1)} %fusion.8, bf16[256,3584]{1,0:T(8,128)(2,1)S(1)} %copy-done.1, f32[256,256]{0,1:T(8,128)S(1)} %select_n.23), kind=kOutput, calls=%fused_computation.2 | convolution fusion | flops 472776704 | bytes 11272192 | tf_op jit(solution)/shard_map/dot_general | solution.py:526
  98.4 22.6 %shard_map.93 = bf16[16,3584]{1,0:T(8,128)(2,1)} custom-call(bf16[16,16,3584]{2,1,0:T(8,128)(2,1)} %bitcast.19), custom_call_target="tpu_custom_call" | custom-call | tf_op jit(solution)/shard_map/pallas_call | solution.py:246
  121.1 1.6 %copy.50 = bf16[16,3584]{1,0:T(8,128)(2,1)} copy(bf16[16,3584]{1,0:T(8,128)(2,1)} %shard_map.93) | data formatting | bytes 229376
  (8 shorter events, 0.1 us)
Async XLA Ops:
  26.0 5.3 %copy-start = (bf16[16,16,3584]{2,1,0:T(8,128)(2,1)S(1)}, bf16[16,16,3584]{2,1,0:T(8,128)(2,1)}, u32[]{:S(2)}) copy-start(bf16[16,16,3584]{2,1,0:T(8,128)(2,1)} %get-tuple-element.10) | copy-start | bytes 5505028
  93.3 2.3 %copy-start.1 = (bf16[256,3584]{1,0:T(8,128)(2,1)S(1)}, bf16[256,3584]{1,0:T(8,128)(2,1)}, u32[]{:S(2)}) copy-start(bf16[256,3584]{1,0:T(8,128)(2,1)} %get-tuple-element.12) | copy-start | bytes 5505028
  93.3 3.1 %copy-start.2 = (f32[256,3584]{1,0:T(8,128)S(1)}, f32[256,3584]{1,0:T(8,128)}, u32[]{:S(2)}) copy-start(f32[256,3584]{1,0:T(8,128)} %get-tuple-element.11) | copy-start | bytes 11010052
